TPU v7x, 256 devices: a whole 4x4x8 slice. The times are simulated.
256 devices in a mesh: gx: 4 (over y), gy: 8 (over x, core), gz: 8 (over z).
Axes of the slice: x: 4, y: 4, z: 8, core: 2. Of those that a mesh axis runs over, the one named last changes fastest.
Arguments:
- basis: bfloat16 [8, 3, 64, 1024, 128], P('gx', None, 'gy', 'gz'), may hold values from -4.8 to 4.8
- modal_now: bfloat16 [128, 8], replicated, may hold values from -0.5 to 0.5
- modal_prev: bfloat16 [128, 8], replicated, may hold values from -0.5 to 0.5
- material_ids: int32 [8, 64, 1024], P('gx', 'gy', 'gz'), may hold values from 0 to 3
- moduli: float32 [3, 4], replicated, may hold values from 0.4 to 1.6
- drive_mask: int32 [8, 8, 64, 1024], P(None, 'gx', 'gy', 'gz'), may hold values 0 or 1
- drive: float32 [3, 8], replicated, may hold values from -8 to 8
Outputs:
- displacement: float32 [3, 8, 8, 64, 1024], P(None, None, 'gx', 'gy', 'gz')
- modes: float32 [3, 8, 8, 64, 1024], P(None, None, 'gx', 'gy', 'gz')
- coefficients: float32 [4, 2, 128, 8], replicated
- rfactor: float32 [4, 8, 8], replicated
All inputs are finite; a program needn't handle non-finite values. No bound on the sum of `drive_mask` on one device may be relied on, other than what follows from the above.
Results may differ from a plain program's by a relative error of at most 0.0008.
The roundings to bfloat16 on the way count: a program that leaves them out, or rounds other values in their place, can miss the bound.
Values sent between devices are 32-bit elements; how exact they have to be, the bound alone decides.
No kernel may reach another device: no remote copies, remote signals or barrier semaphores. Data moves between devices by JAX's collectives and lax.ppermute only.
A program may use at most 128 MiB of HBM per device.

v0:
```python
import jax
import jax.numpy as jnp
from jax import lax
from jax.sharding import PartitionSpec as P

STEPS = 4


step_squared = 0.1
ramp_steps = 4.0


def padded_2(block, sides, width):
    for axis, dim in sides:
        count = lax.axis_size(axis)
        forward = [(i, i + 1) for i in range(count - 1)]
        backward = [(target, source) for source, target in forward]
        low = lax.ppermute(
            lax.slice_in_dim(block, block.shape[dim] - width, None, axis=dim), axis, forward
        )
        high = lax.ppermute(lax.slice_in_dim(block, 0, width, axis=dim), axis, backward)
        block = jnp.concatenate([low, block, high], axis=dim)
    return block


def interior(array, direction_axis, offset):
    base_axis = array.ndim - 3
    result = array
    for axis_index in range(3):
        extent = array.shape[base_axis + axis_index]
        begin = offset if axis_index == direction_axis else 1
        result = lax.slice_in_dim(result, begin, extent - 2 + begin, axis=base_axis + axis_index)
    return result


def stiffness(field, material_props):
    component_rows = []
    for component in range(3):
        center = interior(field[component], 0, 1)
        accumulated = jnp.zeros_like(center)
        for direction_axis in range(3):
            modulus = material_props[0] if component == direction_axis else material_props[1]
            center_modulus = interior(modulus, 0, 1)
            for offset in (0, 2):
                coupling = 0.5 * (center_modulus + interior(modulus, direction_axis, offset))
                accumulated = accumulated + coupling * (
                    center - interior(field[component], direction_axis, offset)
                )
        component_rows.append(accumulated)
    return jnp.stack(component_rows)


def lookup(material_ids, moduli):
    levels = jnp.arange(moduli.shape[1], dtype=jnp.int32)
    onehot = (material_ids[None] == levels[:, None, None, None]).astype(jnp.float32)
    return jnp.einsum("mxyz,pm->pxyz", onehot, moduli, precision=lax.Precision.HIGHEST)


def expand(basis, coefficient):
    return jnp.einsum("xcyzk,kj->cjxyz", basis, coefficient, preferred_element_type=jnp.float32)


def project(basis, field):
    return jnp.einsum("xcyzk,cjxyz->kj", basis, field, preferred_element_type=jnp.float32)


def apply_inverse(block, lower_factor):
    identity_block = jnp.eye(lower_factor.shape[0], dtype=jnp.float32)
    lower_inverse = jax.scipy.linalg.solve_triangular(lower_factor, identity_block, lower=True)
    return jnp.einsum("cixyz,ji->cjxyz", block, lower_inverse, precision=lax.Precision.HIGHEST)


def local_gram(block):
    return jnp.einsum("cixyz,cjxyz->ij", block, block, precision=lax.Precision.HIGHEST)


def orthonormalize(following, basis, dof_weight):
    highest = lax.Precision.HIGHEST
    snapshot = following.astype(jnp.bfloat16)
    partial_coef = project(basis, snapshot) * dof_weight
    first_coef = lax.psum(partial_coef, ("gx", "gy", "gz"))
    first_resid = snapshot.astype(jnp.float32) - expand(basis, first_coef.astype(jnp.bfloat16))
    first_gram = lax.psum(local_gram(first_resid) * dof_weight, ("gx", "gy", "gz"))
    first_lower = jnp.linalg.cholesky(first_gram)
    first_q = apply_inverse(first_resid, first_lower)
    second_coef = lax.psum(
        project(basis, first_q.astype(jnp.bfloat16)) * dof_weight, ("gx", "gy", "gz")
    )
    second_resid = first_q - expand(basis, second_coef.astype(jnp.bfloat16))
    second_gram = lax.psum(local_gram(second_resid) * dof_weight, ("gx", "gy", "gz"))
    second_lower = jnp.linalg.cholesky(second_gram)
    modes = apply_inverse(second_resid, second_lower)
    factor = jnp.dot(first_lower, second_lower, precision=highest).T
    return (jnp.stack([first_coef, second_coef]), factor, modes)


def shards(basis, modal_now, modal_prev, material_ids, moduli, drive_mask, drive):
    devices_total = lax.axis_size("gx") * lax.axis_size("gy") * lax.axis_size("gz")
    dof_weight = 1.0 / (3.0 * basis.shape[0] * basis.shape[2] * basis.shape[3] * devices_total)
    current = expand(basis, modal_now)
    earlier = expand(basis, modal_prev)
    material_props = lookup(material_ids, moduli)
    port_mask = drive_mask.astype(jnp.float32)
    static = jnp.concatenate([material_props, port_mask], axis=0)
    wide_static = padded_2(static, (("gx", 1), ("gy", 2), ("gz", 3)), 2)
    props_wide = wide_static[:3]
    props_near = props_wide[:, 1:-1, 1:-1, 1:-1]
    inverse_mass = material_props[2]
    drive_field = drive[:, :, None, None, None]
    coefficient_list = []
    factor_list = []
    modes = current
    for step in range(STEPS):
        padded = padded_2(current, (("gx", 2), ("gy", 3), ("gz", 4)), 1)
        ramp_level = min(1.0, (step + 1) / ramp_steps)
        load_field = drive_field * port_mask[None] * ramp_level
        following = (
            2.0 * current
            - earlier
            + step_squared * inverse_mass * (load_field - stiffness(padded, props_near))
        )
        earlier = current
        current = following
        coefs, factor, modes = orthonormalize(following, basis, dof_weight)
        coefficient_list.append(coefs)
        factor_list.append(factor)
    return (current, modes, jnp.stack(coefficient_list), jnp.stack(factor_list))


def solution(mesh):
    in_specs = (
        P("gx", None, "gy", "gz", None),
        P(),
        P(),
        P("gx", "gy", "gz"),
        P(),
        P(None, "gx", "gy", "gz"),
        P(),
    )
    out_specs = (P(None, None, "gx", "gy", "gz"), P(None, None, "gx", "gy", "gz"), P(), P())
    return jax.shard_map(shards, mesh=mesh, in_specs=in_specs, out_specs=out_specs, check_vma=False)
```

profile of v0, /device:TPU:1, one launch (start us, length us, event | category | flops | bytes accessed | tf_op | source)
XLA Modules:
  0.0 537.8 jit_solution(7000948003984317785)
XLA Ops:
  2.5 4.0 collective-permute-start
  9.1 4.0 collective-permute-start.6
  14.7 3.7 collective-permute-done.7
  18.5 5.7 %collective-permute-start.8 = (f32[3,8,4,1,128]{4,1,3,2,0:T(8,128)S(1)}, f32[3,8,4,1,128]{4,1,3,2,0:T(8,128)S(1)}, u32[]{:S(2)}, u32[]{:S(2)}) collective-permute-start(f32[3,8,4,1,128]{4,1,3,2,0:T(8,128)S(1)} %get-tuple-element.78), channel_id=1, source_target_pairs={{0,8},{8,16},{16,24},{24,32},{32,40},{40,48},{48,56},{1,9},{9,17},... | collective-permute-start | bytes 147464 | tf_op jit(solution)/shard_map/ppermute | solution.py:18
  24.2 1.9 collective-permute-start.9
  26.2 3.4 collective-permute-done.9
  30.7 3.6 collective-permute-start.10
  35.7 3.8 copy.222
  39.5 2.2 collective-permute-start.2
  42.3 2.8 collective-permute-start.3
  45.9 2.0 collective-permute-done.11
  47.9 1.6 pad_maximum_fusion.1
  49.6 4.5 copy.221
  54.1 3.9 copy.223
  58.0 9.0 %pad_maximum_fusion = f32[11,6,12,128]{2,1,3,0:T(8,128)S(1)} fusion(f32[11,6,2,128]{2,1,3,0:T(8,128)} %copy.223, f32[11,6,8,128]{2,1,3,0:T(8,128)} %copy.222, f32[11,6,2,128]{2,1,3,0:T(8,128)} %copy.221), kind=kLoop, calls=%fused_computation | loop fusion | flops 202752 | bytes 811008 | tf_op jit(solution)/shard_map/concatenate | solution.py:22
  67.0 2.5 copy-done.1
  69.5 3.5 collective-permute-start.4
  75.3 4.2 copy.225
  86.2 3.2 collective-permute-start.12
  91.7 3.9 collective-permute-done.13
  95.6 5.9 %collective-permute-start.14 = (f32[3,8,4,1,128]{4,1,3,2,0:T(8,128)S(1)}, f32[3,8,4,1,128]{4,1,3,2,0:T(8,128)S(1)}, u32[]{:S(2)}, u32[]{:S(2)}) collective-permute-start(f32[3,8,4,1,128]{4,1,3,2,0:T(8,128)S(1)} %get-tuple-element.76), channel_id=1, source_target_pairs={{0,8},{8,16},{16,24},{24,32},{32,40},{40,48},{48,56},{1,9},{9,17},... | collective-permute-start | bytes 147464 | tf_op jit(solution)/shard_map/ppermute | solution.py:18
  101.6 1.9 collective-permute-start.15
  103.5 3.5 collective-permute-done.15
  107.2 4.9 collective-permute-start.16
  113.4 7.9 %collective-permute-done.16 = f32[3,8,4,10,1]{4,1,3,2,0:T(8,128)S(1)} collective-permute-done((f32[3,8,4,10,1]{4,1,3,2,0:T(8,128)S(1)}, f32[3,8,4,10,1]{4,1,3,2,0:T(8,128)S(1)}, u32[]{:S(2)}, u32[]{:S(2)}) %collective-permute-start.16) | collective-permute-done | bytes 3872 | tf_op jit(solution)/shard_map/ppermute | solution.py:18
  121.3 5.2 collective-permute-done.17
  127.7 2.9 collective-permute-start.18
  132.5 4.1 collective-permute-done.19
  136.7 5.3 collective-permute-start.20
  142.0 1.9 collective-permute-start.21
  143.9 3.5 collective-permute-done.21
  147.6 3.7 collective-permute-start.22
  152.8 7.7 %collective-permute-done.22 = f32[3,8,4,10,1]{4,1,3,2,0:T(8,128)S(1)} collective-permute-done((f32[3,8,4,10,1]{4,1,3,2,0:T(8,128)S(1)}, f32[3,8,4,10,1]{4,1,3,2,0:T(8,128)S(1)}, u32[]{:S(2)}, u32[]{:S(2)}) %collective-permute-start.22) | collective-permute-done | bytes 3872 | tf_op jit(solution)/shard_map/ppermute | solution.py:18
  160.5 4.1 collective-permute-done.23
  165.8 1.9 collective-permute-start.24
  169.6 4.1 collective-permute-done.25
  173.7 4.8 collective-permute-start.26
  178.5 1.9 collective-permute-start.27
  180.8 3.2 collective-permute-done.27
  184.2 4.6 collective-permute-start.28
  190.4 7.6 %collective-permute-done.28 = f32[3,8,4,10,1]{4,1,3,2,0:T(8,128)S(1)} collective-permute-done((f32[3,8,4,10,1]{4,1,3,2,0:T(8,128)S(1)}, f32[3,8,4,10,1]{4,1,3,2,0:T(8,128)S(1)}, u32[]{:S(2)}, u32[]{:S(2)}) %collective-permute-start.28) | collective-permute-done | bytes 3872 | tf_op jit(solution)/shard_map/ppermute | solution.py:18
  198.0 4.1 collective-permute-done.29
  203.5 73.7 %all-reduce.3 = (f32[128,8]{0,1:T(8,128)S(1)}, f32[128,8]{0,1:T(8,128)S(1)}, f32[128,8]{0,1:T(8,128)S(1)}, f32[128,8]{0,1:T(8,128)S(1)}) all-reduce(f32[128,8]{0,1:T(8,128)S(1)} %fusion.25, f32[128,8]{0,1:T(8,128)S(1)} %fusion.13, f32[128,8]{0,1:T(8,128)S(1)} %fusion.17, ...), channel_id=1, replica_groups=mesh['gx'=4,'gy'=8,'gz'=8] {'gx','gy','gz'}, use_global_device_ids=true, to_apply=%region_0.0 | all-reduce | flops 4096 | bytes 32768 | tf_op jit(solution)/shard_map/psum | solution.py:81
  281.4 73.0 %all-reduce.2 = (f32[8,8]{0,1:T(8,128)S(1)}, f32[8,8]{0,1:T(8,128)S(1)}, f32[8,8]{0,1:T(8,128)S(1)}, f32[8,8]{0,1:T(8,128)S(1)}) all-reduce(f32[8,8]{0,1:T(8,128)S(1)} %fusion.33, f32[8,8]{0,1:T(8,128)S(1)} %fusion.29, f32[8,8]{0,1:T(8,128)S(1)} %fusion.30, f32[8,8]{0,1:T(8,128)S(1)} %fusion.31), channel_id=1, replica_groups=mesh['gx'=4,'gy'=8,'gz'=8] {'gx','gy','gz'}, use_global_device_ids=true, to_apply=%region_1.0 | all-reduce | flops 256 | bytes 2048 | tf_op jit(solution)/shard_map/psum | solution.py:83
  368.8 74.7 %all-reduce.1 = (f32[128,8]{0,1:T(8,128)S(1)}, f32[128,8]{0,1:T(8,128)S(1)}, f32[128,8]{0,1:T(8,128)S(1)}, f32[128,8]{0,1:T(8,128)S(1)}) all-reduce(f32[128,8]{0,1:T(8,128)S(1)} %fusion.23, f32[128,8]{0,1:T(8,128)S(1)} %fusion.11, f32[128,8]{0,1:T(8,128)S(1)} %fusion.15, ...), channel_id=1, replica_groups=mesh['gx'=4,'gy'=8,'gz'=8] {'gx','gy','gz'}, use_global_device_ids=true, to_apply=%region_4.0 | all-reduce | flops 4096 | bytes 32768 | tf_op jit(solution)/shard_map/psum | solution.py:86
  447.7 73.6 %all-reduce = (f32[8,8]{0,1:T(8,128)S(1)}, f32[8,8]{0,1:T(8,128)S(1)}, f32[8,8]{0,1:T(8,128)S(1)}, f32[8,8]{0,1:T(8,128)S(1)}) all-reduce(f32[8,8]{0,1:T(8,128)S(1)} %fusion.32, f32[8,8]{0,1:T(8,128)S(1)} %fusion.26, f32[8,8]{0,1:T(8,128)S(1)} %fusion.27, f32[8,8]{0,1:T(8,128)S(1)} %fusion.28), channel_id=1, replica_groups=mesh['gx'=4,'gy'=8,'gz'=8] {'gx','gy','gz'}, use_global_device_ids=true, to_apply=%region_5.0 | all-reduce | flops 256 | bytes 2048 | tf_op jit(solution)/shard_map/psum | solution.py:90
  522.8 1.5 convolution_bitcast_fusion.16
  526.5 1.5 convolution_bitcast_fusion.19
  (192 shorter events, 70.2 us)
Async XLA Ops:
  0.6 7.2 %copy-start = (bf16[2,3,8,128,128]{4,3,2,1,0:T(8,128)(2,1)S(1)}, bf16[2,3,8,128,128]{4,3,2,1,0:T(8,128)(2,1)}, u32[]{:S(2)}) copy-start(bf16[2,3,8,128,128]{4,3,2,1,0:T(8,128)(2,1)} %param.10) | copy-start | bytes 4718596
  2.5 23.6 %collective-permute-start = (f32[11,2,8,128]{3,2,1,0:T(8,128)S(1)}, f32[11,2,8,128]{3,2,1,0:T(8,128)S(1)}, u32[]{:S(2)}, u32[]{:S(2)}) collective-permute-start(f32[11,2,8,128]{3,2,1,0:T(8,128)S(1)} %pad_maximum_fusion.10), channel_id=1, source_target_pairs={{0,64},{64,128},{128,192},{1,65},{65,129},{129,193},{2,66},{66,130... | collective-permute-start | bytes 270344 | tf_op jit(solution)/shard_map/ppermute | solution.py:18
  6.5 19.6 %collective-permute-start.1 = (f32[11,2,8,128]{3,2,1,0:T(8,128)S(1)}, f32[11,2,8,128]{3,2,1,0:T(8,128)S(1)}, u32[]{:S(2)}, u32[]{:S(2)}) collective-permute-start(f32[11,2,8,128]{3,2,1,0:T(8,128)S(1)} %pad_maximum_fusion.10), channel_id=1, source_target_pairs={{64,0},{128,64},{192,128},{65,1},{129,65},{193,129},{66,2},{130,66... | collective-permute-start | bytes 270344 | tf_op jit(solution)/shard_map/ppermute | solution.py:21
  9.1 5.6 %collective-permute-start.6 = (f32[3,8,1,8,128]{4,1,3,2,0:T(8,128)S(1)}, f32[3,8,1,8,128]{4,1,3,2,0:T(8,128)S(1)}, u32[]{:S(2)}, u32[]{:S(2)}) collective-permute-start(f32[3,8,1,8,128]{4,1,3,2,0:T(8,128)S(1)} %copy.383), channel_id=1, source_target_pairs={{0,64},{64,128},{128,192},{1,65},{65,129},{129,193},{2,66},{66,130... | collective-permute-start | bytes 294920 | tf_op jit(solution)/shard_map/ppermute | solution.py:18
  13.1 5.4 collective-permute-start.7
  18.5 7.7 %collective-permute-start.8 = (f32[3,8,4,1,128]{4,1,3,2,0:T(8,128)S(1)}, f32[3,8,4,1,128]{4,1,3,2,0:T(8,128)S(1)}, u32[]{:S(2)}, u32[]{:S(2)}) collective-permute-start(f32[3,8,4,1,128]{4,1,3,2,0:T(8,128)S(1)} %get-tuple-element.78), channel_id=1, source_target_pairs={{0,8},{8,16},{16,24},{24,32},{32,40},{40,48},{48,56},{1,9},{9,17},... | collective-permute-start | bytes 147464 | tf_op jit(solution)/shard_map/ppermute | solution.py:18
  24.2 5.4 %collective-permute-start.9 = (f32[3,8,4,1,128]{4,1,3,2,0:T(8,128)S(1)}, f32[3,8,4,1,128]{4,1,3,2,0:T(8,128)S(1)}, u32[]{:S(2)}, u32[]{:S(2)}) collective-permute-start(f32[3,8,4,1,128]{4,1,3,2,0:T(8,128)S(1)} %get-tuple-element.79), channel_id=1, source_target_pairs={{8,0},{16,8},{24,16},{32,24},{40,32},{48,40},{56,48},{9,1},{17,9},... | collective-permute-start | bytes 147464 | tf_op jit(solution)/shard_map/ppermute | solution.py:21
  30.7 14.4 %collective-permute-start.10 = (f32[3,8,4,10,1]{4,1,3,2,0:T(8,128)}, f32[3,8,4,10,1]{4,1,3,2,0:T(8,128)S(1)}, u32[]{:S(2)}, u32[]{:S(2)}) collective-permute-start(f32[3,8,4,10,1]{4,1,3,2,0:T(8,128)} %get-tuple-element.70), channel_id=1, source_target_pairs={{0,1},{1,2},{2,3},{3,4},{4,5},{5,6},{6,7},{8,9},{9,10},{10,11},{11... | collective-permute-start | bytes 11528 | tf_op jit(solution)/shard_map/ppermute | solution.py:18
  34.3 13.6 %collective-permute-start.11 = (f32[3,8,4,10,1]{4,1,3,2,0:T(8,128)}, f32[3,8,4,10,1]{4,1,3,2,0:T(8,128)}, u32[]{:S(2)}, u32[]{:S(2)}) collective-permute-start(f32[3,8,4,10,1]{4,1,3,2,0:T(8,128)} %get-tuple-element.71), channel_id=1, source_target_pairs={{1,0},{2,1},{3,2},{4,3},{5,4},{6,5},{7,6},{9,8},{10,9},{11,10},{12... | collective-permute-start | bytes 11528 | tf_op jit(solution)/shard_map/ppermute | solution.py:21
  39.5 10.1 %collective-permute-start.2 = (f32[11,6,2,128]{3,1,2,0:T(8,128)S(1)}, f32[11,6,2,128]{3,1,2,0:T(8,128)}, u32[]{:S(2)}, u32[]{:S(2)}) collective-permute-start(f32[11,6,2,128]{3,1,2,0:T(8,128)S(1)} %copy.326), channel_id=1, source_target_pairs={{0,8},{8,16},{16,24},{24,32},{32,40},{40,48},{48,56},{1,9},{9,17},... | collective-permute-start | bytes 202760 | tf_op jit(solution)/shard_map/ppermute | solution.py:18
  42.3 11.8 %collective-permute-start.3 = (f32[11,6,2,128]{3,1,2,0:T(8,128)}, f32[11,6,2,128]{3,1,2,0:T(8,128)S(1)}, u32[]{:S(2)}, u32[]{:S(2)}) collective-permute-start(f32[11,6,2,128]{3,1,2,0:T(8,128)} %copy.327), channel_id=1, source_target_pairs={{8,0},{16,8},{24,16},{32,24},{40,32},{48,40},{56,48},{9,1},{17,9},... | collective-permute-start | bytes 202760 | tf_op jit(solution)/shard_map/ppermute | solution.py:21
  45.1 0.8 copy-start.2
  67.0 2.5 copy-start.1
  69.5 10.0 %collective-permute-start.4 = (f32[11,6,12,2]{2,1,3,0:T(8,128)S(1)}, f32[11,6,12,2]{2,1,3,0:T(8,128)S(1)}, u32[]{:S(2)}, u32[]{:S(2)}) collective-permute-start(f32[11,6,12,2]{2,1,3,0:T(8,128)S(1)} %get-tuple-element.44), channel_id=1, source_target_pairs={{0,1},{1,2},{2,3},{3,4},{4,5},{5,6},{6,7},{8,9},{9,10},{10,11},{11... | collective-permute-start | bytes 19016 | tf_op jit(solution)/shard_map/ppermute | solution.py:18
  73.1 7.0 %collective-permute-start.5 = (f32[11,6,12,2]{2,1,3,0:T(8,128)S(1)}, f32[11,6,12,2]{2,1,3,0:T(8,128)S(1)}, u32[]{:S(2)}, u32[]{:S(2)}) collective-permute-start(f32[11,6,12,2]{2,1,3,0:T(8,128)S(1)} %get-tuple-element.45), channel_id=1, source_target_pairs={{1,0},{2,1},{3,2},{4,3},{5,4},{6,5},{7,6},{9,8},{10,9},{11,10},{12... | collective-permute-start | bytes 19016 | tf_op jit(solution)/shard_map/ppermute | solution.py:21
  81.4 4.2 copy-start.3
  81.4 4.3 copy-start.4
  86.2 5.6 %collective-permute-start.12 = (f32[3,8,1,8,128]{4,1,3,2,0:T(8,128)S(1)}, f32[3,8,1,8,128]{4,1,3,2,0:T(8,128)S(1)}, u32[]{:S(2)}, u32[]{:S(2)}) collective-permute-start(f32[3,8,1,8,128]{4,1,3,2,0:T(8,128)S(1)} %get-tuple-element.86), channel_id=1, source_target_pairs={{0,64},{64,128},{128,192},{1,65},{65,129},{129,193},{2,66},{66,130... | collective-permute-start | bytes 294920 | tf_op jit(solution)/shard_map/ppermute | solution.py:18
  89.4 6.2 %collective-permute-start.13 = (f32[3,8,1,8,128]{4,1,3,2,0:T(8,128)S(1)}, f32[3,8,1,8,128]{4,1,3,2,0:T(8,128)S(1)}, u32[]{:S(2)}, u32[]{:S(2)}) collective-permute-start(f32[3,8,1,8,128]{4,1,3,2,0:T(8,128)S(1)} %get-tuple-element.87), channel_id=1, source_target_pairs={{64,0},{128,64},{192,128},{65,1},{129,65},{193,129},{66,2},{130,66... | collective-permute-start | bytes 294920 | tf_op jit(solution)/shard_map/ppermute | solution.py:21
  95.6 7.9 %collective-permute-start.14 = (f32[3,8,4,1,128]{4,1,3,2,0:T(8,128)S(1)}, f32[3,8,4,1,128]{4,1,3,2,0:T(8,128)S(1)}, u32[]{:S(2)}, u32[]{:S(2)}) collective-permute-start(f32[3,8,4,1,128]{4,1,3,2,0:T(8,128)S(1)} %get-tuple-element.76), channel_id=1, source_target_pairs={{0,8},{8,16},{16,24},{24,32},{32,40},{40,48},{48,56},{1,9},{9,17},... | collective-permute-start | bytes 147464 | tf_op jit(solution)/shard_map/ppermute | solution.py:18
  101.6 5.4 %collective-permute-start.15 = (f32[3,8,4,1,128]{4,1,3,2,0:T(8,128)S(1)}, f32[3,8,4,1,128]{4,1,3,2,0:T(8,128)S(1)}, u32[]{:S(2)}, u32[]{:S(2)}) collective-permute-start(f32[3,8,4,1,128]{4,1,3,2,0:T(8,128)S(1)} %get-tuple-element.77), channel_id=1, source_target_pairs={{8,0},{16,8},{24,16},{32,24},{40,32},{48,40},{56,48},{9,1},{17,9},... | collective-permute-start | bytes 147464 | tf_op jit(solution)/shard_map/ppermute | solution.py:21
  107.2 14.1 %collective-permute-start.16 = (f32[3,8,4,10,1]{4,1,3,2,0:T(8,128)S(1)}, f32[3,8,4,10,1]{4,1,3,2,0:T(8,128)S(1)}, u32[]{:S(2)}, u32[]{:S(2)}) collective-permute-start(f32[3,8,4,10,1]{4,1,3,2,0:T(8,128)S(1)} %get-tuple-element.68), channel_id=1, source_target_pairs={{0,1},{1,2},{2,3},{3,4},{4,5},{5,6},{6,7},{8,9},{9,10},{10,11},{11... | collective-permute-start | bytes 11528 | tf_op jit(solution)/shard_map/ppermute | solution.py:18
  112.1 14.4 %collective-permute-start.17 = (f32[3,8,4,10,1]{4,1,3,2,0:T(8,128)S(1)}, f32[3,8,4,10,1]{4,1,3,2,0:T(8,128)S(1)}, u32[]{:S(2)}, u32[]{:S(2)}) collective-permute-start(f32[3,8,4,10,1]{4,1,3,2,0:T(8,128)S(1)} %get-tuple-element.69), channel_id=1, source_target_pairs={{1,0},{2,1},{3,2},{4,3},{5,4},{6,5},{7,6},{9,8},{10,9},{11,10},{12... | collective-permute-start | bytes 11528 | tf_op jit(solution)/shard_map/ppermute | solution.py:21
  127.7 4.8 collective-permute-start.18
  130.7 6.0 %collective-permute-start.19 = (f32[3,8,1,8,128]{4,1,3,2,0:T(8,128)S(1)}, f32[3,8,1,8,128]{4,1,3,2,0:T(8,128)S(1)}, u32[]{:S(2)}, u32[]{:S(2)}) collective-permute-start(f32[3,8,1,8,128]{4,1,3,2,0:T(8,128)S(1)} %copy.386), channel_id=1, source_target_pairs={{64,0},{128,64},{192,128},{65,1},{129,65},{193,129},{66,2},{130,66... | collective-permute-start | bytes 294920 | tf_op jit(solution)/shard_map/ppermute | solution.py:21
  136.7 7.2 %collective-permute-start.20 = (f32[3,8,4,1,128]{4,1,3,2,0:T(8,128)S(1)}, f32[3,8,4,1,128]{4,1,3,2,0:T(8,128)S(1)}, u32[]{:S(2)}, u32[]{:S(2)}) collective-permute-start(f32[3,8,4,1,128]{4,1,3,2,0:T(8,128)S(1)} %get-tuple-element.74), channel_id=1, source_target_pairs={{0,8},{8,16},{16,24},{24,32},{32,40},{40,48},{48,56},{1,9},{9,17},... | collective-permute-start | bytes 147464 | tf_op jit(solution)/shard_map/ppermute | solution.py:18
  142.0 5.4 %collective-permute-start.21 = (f32[3,8,4,1,128]{4,1,3,2,0:T(8,128)S(1)}, f32[3,8,4,1,128]{4,1,3,2,0:T(8,128)S(1)}, u32[]{:S(2)}, u32[]{:S(2)}) collective-permute-start(f32[3,8,4,1,128]{4,1,3,2,0:T(8,128)S(1)} %get-tuple-element.75), channel_id=1, source_target_pairs={{8,0},{16,8},{24,16},{32,24},{40,32},{48,40},{56,48},{9,1},{17,9},... | collective-permute-start | bytes 147464 | tf_op jit(solution)/shard_map/ppermute | solution.py:21
  147.6 12.9 %collective-permute-start.22 = (f32[3,8,4,10,1]{4,1,3,2,0:T(8,128)S(1)}, f32[3,8,4,10,1]{4,1,3,2,0:T(8,128)S(1)}, u32[]{:S(2)}, u32[]{:S(2)}) collective-permute-start(f32[3,8,4,10,1]{4,1,3,2,0:T(8,128)S(1)} %get-tuple-element.66), channel_id=1, source_target_pairs={{0,1},{1,2},{2,3},{3,4},{4,5},{5,6},{6,7},{8,9},{9,10},{10,11},{11... | collective-permute-start | bytes 11528 | tf_op jit(solution)/shard_map/ppermute | solution.py:18
  151.3 13.3 %collective-permute-start.23 = (f32[3,8,4,10,1]{4,1,3,2,0:T(8,128)S(1)}, f32[3,8,4,10,1]{4,1,3,2,0:T(8,128)S(1)}, u32[]{:S(2)}, u32[]{:S(2)}) collective-permute-start(f32[3,8,4,10,1]{4,1,3,2,0:T(8,128)S(1)} %get-tuple-element.67), channel_id=1, source_target_pairs={{1,0},{2,1},{3,2},{4,3},{5,4},{6,5},{7,6},{9,8},{10,9},{11,10},{12... | collective-permute-start | bytes 11528 | tf_op jit(solution)/shard_map/ppermute | solution.py:21
  165.8 3.8 collective-permute-start.24
  167.7 6.0 %collective-permute-start.25 = (f32[3,8,1,8,128]{4,1,3,2,0:T(8,128)S(1)}, f32[3,8,1,8,128]{4,1,3,2,0:T(8,128)S(1)}, u32[]{:S(2)}, u32[]{:S(2)}) collective-permute-start(f32[3,8,1,8,128]{4,1,3,2,0:T(8,128)S(1)} %get-tuple-element.83), channel_id=1, source_target_pairs={{64,0},{128,64},{192,128},{65,1},{129,65},{193,129},{66,2},{130,66... | collective-permute-start | bytes 294920 | tf_op jit(solution)/shard_map/ppermute | solution.py:21
  173.7 7.0 %collective-permute-start.26 = (f32[3,8,4,1,128]{4,1,3,2,0:T(8,128)S(1)}, f32[3,8,4,1,128]{4,1,3,2,0:T(8,128)S(1)}, u32[]{:S(2)}, u32[]{:S(2)}) collective-permute-start(f32[3,8,4,1,128]{4,1,3,2,0:T(8,128)S(1)} %get-tuple-element.72), channel_id=1, source_target_pairs={{0,8},{8,16},{16,24},{24,32},{32,40},{40,48},{48,56},{1,9},{9,17},... | collective-permute-start | bytes 147464 | tf_op jit(solution)/shard_map/ppermute | solution.py:18
  178.5 5.4 %collective-permute-start.27 = (f32[3,8,4,1,128]{4,1,3,2,0:T(8,128)S(1)}, f32[3,8,4,1,128]{4,1,3,2,0:T(8,128)S(1)}, u32[]{:S(2)}, u32[]{:S(2)}) collective-permute-start(f32[3,8,4,1,128]{4,1,3,2,0:T(8,128)S(1)} %get-tuple-element.73), channel_id=1, source_target_pairs={{8,0},{16,8},{24,16},{32,24},{40,32},{48,40},{56,48},{9,1},{17,9},... | collective-permute-start | bytes 147464 | tf_op jit(solution)/shard_map/ppermute | solution.py:21
  184.2 13.8 %collective-permute-start.28 = (f32[3,8,4,10,1]{4,1,3,2,0:T(8,128)S(1)}, f32[3,8,4,10,1]{4,1,3,2,0:T(8,128)S(1)}, u32[]{:S(2)}, u32[]{:S(2)}) collective-permute-start(f32[3,8,4,10,1]{4,1,3,2,0:T(8,128)S(1)} %get-tuple-element.64), channel_id=1, source_target_pairs={{0,1},{1,2},{2,3},{3,4},{4,5},{5,6},{6,7},{8,9},{9,10},{10,11},{11... | collective-permute-start | bytes 11528 | tf_op jit(solution)/shard_map/ppermute | solution.py:18
  188.8 13.3 %collective-permute-start.29 = (f32[3,8,4,10,1]{4,1,3,2,0:T(8,128)S(1)}, f32[3,8,4,10,1]{4,1,3,2,0:T(8,128)S(1)}, u32[]{:S(2)}, u32[]{:S(2)}) collective-permute-start(f32[3,8,4,10,1]{4,1,3,2,0:T(8,128)S(1)} %get-tuple-element.65), channel_id=1, source_target_pairs={{1,0},{2,1},{3,2},{4,3},{5,4},{6,5},{7,6},{9,8},{10,9},{11,10},{12... | collective-permute-start | bytes 11528 | tf_op jit(solution)/shard_map/ppermute | solution.py:21
where the time goes:
time: 540 us; the launch traced here: 538 us
  blocking collectives  295 us (55%)
  starting transfers between devices  83.7 us (16%)
  waiting for transfers between devices  70.1 us (13%)
  other arithmetic  38.1 us (7%)
  local copies, waits for them, and re-layouts  27.4 us (5%)
  matrix products  22 us (4%)
    psum x1, blocking collectives, orthonormalize(): lax.psum(project(basis, first_q.astype(jnp.bfloat16)) * dof_weight, ('gx'...  74.7 us
    psum x1, blocking collectives, orthonormalize(): first_coef = lax.psum(partial_coef, ('gx', 'gy', 'gz'))  73.7 us
    psum x1, blocking collectives, orthonormalize(): lax.psum(local_gram(second_resid) * dof_weight, ('gx', 'gy', 'gz'))  73.6 us
    psum x1, blocking collectives, orthonormalize(): lax.psum(local_gram(first_resid) * dof_weight, ('gx', 'gy', 'gz'))  73 us
    ppermute x15, starting transfers between devices, padded_2(): lax.ppermute(lax.slice_in_dim(block, block.shape[dim] - width, None, axis...  60.2 us
    ppermute x15, waiting for transfers between devices, padded_2(): lax.ppermute(lax.slice_in_dim(block, 0, width, axis=dim), axis, backward)  44.8 us
    ppermute x15, waiting for transfers between devices, padded_2(): lax.ppermute(lax.slice_in_dim(block, block.shape[dim] - width, None, axis...  25.3 us
    ppermute x15, starting transfers between devices, padded_2(): lax.ppermute(lax.slice_in_dim(block, 0, width, axis=dim), axis, backward)  23.6 us
  transfers between devices with their start and end apart: 30, of which 19 were waited for; matrix products, arithmetic and copies ran while one was open for 3% of the time, Pallas kernels for 0%

commit v1 on v0

--- a/solution.py
+++ b/solution.py
@@ -4,6 +4,7 @@
 from jax.sharding import PartitionSpec as P
 
 STEPS = 4
+CASES = 8
 
 
 step_squared = 0.1
@@ -60,38 +61,73 @@
     return jnp.einsum("xcyzk,kj->cjxyz", basis, coefficient, preferred_element_type=jnp.float32)
 
 
-def project(basis, field):
-    return jnp.einsum("xcyzk,cjxyz->kj", basis, field, preferred_element_type=jnp.float32)
+def dot_f32(a, b, contract):
+    return lax.dot_general(
+        a, b, ((contract[:1], contract[1:]), ((), ())),
+        precision=lax.Precision.HIGHEST, preferred_element_type=jnp.float32,
+    )
 
 
-def apply_inverse(block, lower_factor):
-    identity_block = jnp.eye(lower_factor.shape[0], dtype=jnp.float32)
-    lower_inverse = jax.scipy.linalg.solve_triangular(lower_factor, identity_block, lower=True)
-    return jnp.einsum("cixyz,ji->cjxyz", block, lower_inverse, precision=lax.Precision.HIGHEST)
+def factor(gram):
+    rows = lax.broadcasted_iota(jnp.int32, (CASES, 2 * CASES), 0)
+    cols = lax.broadcasted_iota(jnp.int32, (CASES, 2 * CASES), 1)
+    work = jnp.concatenate(
+        [gram, (rows[:, :CASES] == cols[:, :CASES]).astype(jnp.float32)], axis=1
+    )
+    for p in range(CASES):
+        scale = 1.0 / jnp.sqrt(work[p : p + 1, p : p + 1])
+        row = work[p : p + 1] * scale
+        below = jnp.where(rows[:, :1] > p, work[:, p : p + 1] * scale, 0.0)
+        work = jnp.where(rows == p, row, work - below * row)
+    upper = jnp.where(rows[:, :CASES] <= cols[:, :CASES], work[:, :CASES], 0.0)
+    return upper, work[:, CASES:]
 
 
-def local_gram(block):
-    return jnp.einsum("cixyz,cjxyz->ij", block, block, precision=lax.Precision.HIGHEST)
+def gather_sum(part, axis):
+    count = lax.axis_size(axis)
+    spread = jnp.broadcast_to(part[None], (count,) + part.shape)
+    return lax.all_to_all(spread, axis, 0, 0, tiled=True)
 
 
-def orthonormalize(following, basis, dof_weight):
-    highest = lax.Precision.HIGHEST
-    snapshot = following.astype(jnp.bfloat16)
-    partial_coef = project(basis, snapshot) * dof_weight
-    first_coef = lax.psum(partial_coef, ("gx", "gy", "gz"))
-    first_resid = snapshot.astype(jnp.float32) - expand(basis, first_coef.astype(jnp.bfloat16))
-    first_gram = lax.psum(local_gram(first_resid) * dof_weight, ("gx", "gy", "gz"))
-    first_lower = jnp.linalg.cholesky(first_gram)
-    first_q = apply_inverse(first_resid, first_lower)
-    second_coef = lax.psum(
-        project(basis, first_q.astype(jnp.bfloat16)) * dof_weight, ("gx", "gy", "gz")
-    )
-    second_resid = first_q - expand(basis, second_coef.astype(jnp.bfloat16))
-    second_gram = lax.psum(local_gram(second_resid) * dof_weight, ("gx", "gy", "gz"))
-    second_lower = jnp.linalg.cholesky(second_gram)
-    modes = apply_inverse(second_resid, second_lower)
-    factor = jnp.dot(first_lower, second_lower, precision=highest).T
-    return (jnp.stack([first_coef, second_coef]), factor, modes)
+def reduced(coefs, squares, gram, weight):
+    modes = gram.shape[0]
+    slabs = lax.axis_size("gx")
+    quarter = lax.all_to_all(gram.reshape(slabs, modes // slabs, modes), "gx", 0, 0, tiled=True)
+    part = jnp.concatenate([coefs, jnp.pad(squares, ((0, 0), (0, modes - squares.shape[1]))), quarter.sum(0)])
+    part = gather_sum(part, "gy").sum(0)
+    part = gather_sum(part, "gz").sum(0)
+    parts = gather_sum(part, "gx")
+    n = coefs.shape[0]
+    own = parts[:, : 2 * n].sum(0) * weight
+    gram = parts[:, 2 * n :].reshape(modes, modes) * weight
+    return own[:n], own[n:, :n], gram
+
+
+def small_math(coef, squares, gram):
+    rounded = lax.reduce_precision(coef, 8, 7)
+    left = coef - dot_f32(rounded, gram, (1, 0))
+    first = squares - dot_f32(coef, rounded, (1, 1)) - dot_f32(rounded, left, (1, 1))
+    upper_1, inverse_1, second_list = [], [], []
+    for s in range(STEPS):
+        at = slice(s * CASES, (s + 1) * CASES)
+        upper, inverse = factor(first[at, at])
+        upper_1.append(upper)
+        inverse_1.append(inverse)
+        second_list.append(dot_f32(inverse, left[at], (1, 0)))
+    second = jnp.concatenate(second_list)
+    rounded_2 = lax.reduce_precision(second, 8, 7)
+    left_2 = second - dot_f32(rounded_2, gram, (1, 0))
+    change = dot_f32(second, rounded_2, (1, 1)) + dot_f32(rounded_2, left_2, (1, 1))
+    factors = []
+    for s in range(STEPS):
+        at = slice(s * CASES, (s + 1) * CASES)
+        whole = dot_f32(dot_f32(inverse_1[s], first[at, at], (1, 0)), inverse_1[s], (1, 1))
+        upper, inverse = factor(whole - change[at, at])
+        factors.append(dot_f32(upper, upper_1[s], (1, 0)))
+    mix = dot_f32(inverse, inverse_1[-1], (1, 0))
+    shift = dot_f32(mix, rounded[at], (1, 0)) + dot_f32(inverse, rounded_2[at], (1, 0))
+    coefficients = jnp.stack([coef, second]).reshape(2, STEPS, CASES, -1).transpose(1, 0, 3, 2)
+    return coefficients, jnp.stack(factors), mix, shift
 
 
 def shards(basis, modal_now, modal_prev, material_ids, moduli, drive_mask, drive):
@@ -107,9 +143,7 @@
     props_near = props_wide[:, 1:-1, 1:-1, 1:-1]
     inverse_mass = material_props[2]
     drive_field = drive[:, :, None, None, None]
-    coefficient_list = []
-    factor_list = []
-    modes = current
+    snapshots = []
     for step in range(STEPS):
         padded = padded_2(current, (("gx", 2), ("gy", 3), ("gz", 4)), 1)
         ramp_level = min(1.0, (step + 1) / ramp_steps)
@@ -121,10 +155,21 @@
         )
         earlier = current
         current = following
-        coefs, factor, modes = orthonormalize(following, basis, dof_weight)
-        coefficient_list.append(coefs)
-        factor_list.append(factor)
-    return (current, modes, jnp.stack(coefficient_list), jnp.stack(factor_list))
+        snapshots.append(following.astype(jnp.bfloat16))
+    fields = jnp.concatenate(snapshots, axis=1)
+    coefs = jnp.einsum("xcyzk,cjxyz->jk", basis, fields, preferred_element_type=jnp.float32)
+    squares = jnp.einsum("cixyz,cjxyz->ij", fields, fields, preferred_element_type=jnp.float32)
+    rows = basis.reshape(-1, basis.shape[-1])
+    gram = jnp.einsum("nk,nl->kl", rows, rows, preferred_element_type=jnp.float32)
+    coefs, squares, gram = reduced(coefs, squares, gram, dof_weight)
+    coefficients, factors, mix, shift = small_math(coefs, squares, gram)
+    last = snapshots[-1].astype(jnp.float32)
+    modes = jnp.einsum("cixyz,ji->cjxyz", last, mix, precision=lax.Precision.HIGHEST)
+    for _ in range(3):
+        part = lax.reduce_precision(shift, 8, 7)
+        shift = shift - part
+        modes = modes - expand(basis, part.astype(jnp.bfloat16).T)
+    return (current, modes, coefficients, factors)
 
 
 def solution(mesh):

time: 540 us -> 357 us (0.66)
  blocking collectives: 295 us -> 0 us
  between operations: 1.47 us -> 46.7 us
  local copies, waits for them, and re-layouts: 27.4 us -> 66.5 us
  waiting for transfers between devices: 70.1 us -> 93.4 us
  starting transfers between devices: 83.7 us -> 99.5 us
  matrix products: 22 us -> 11.3 us
    psum x4 -> x0, blocking collectives: 295 us -> none  [the longest x1 74.7 us: orthonormalize(): lax.psum(project(basis, first_q.astype(jnp.bfloat16)) * dof_weight, ('gx'...]
    slice x0 -> x62, local copies, waits for them, and re-layouts: none -> 35.5 us  [the longest x61 35.4 us: factor(): scale = 1.0 / jnp.sqrt(work[p:p + 1, p:p + 1])]
    all_to_all x0 -> x4, waiting for transfers between devices: none -> 26 us  [the longest x3 26 us: gather_sum(): return lax.all_to_all(spread, axis, 0, 0, tiled=True)]
    another operation x40 -> x3, other arithmetic: 18.9 us -> 0.62 us  [the longest x1 0.61 us: small_math(): return (coefficients, jnp.stack(factors), mix, shift)]
    all_to_all x0 -> x4, starting transfers between devices: none -> 15.8 us  [the longest x3 12.5 us: gather_sum(): return lax.all_to_all(spread, axis, 0, 0, tiled=True)]
    select_n x0 -> x77, other arithmetic: none -> 11.7 us  [the longest x61 10.5 us: factor(): below = jnp.where(rows[:, :1] > p, work[:, p:p + 1] * scale, 0.0)]
    dot_general x25 -> x29, matrix products: 14.4 us -> 6.4 us  [the longest x25 4.39 us: dot_f32(): lax.dot_general(a, b, ((contract[:1], contract[1:]), ((), ())), precision...]
  transfers between devices with their start and end apart: 30 -> 34, of which waited for: 19 -> 20; matrix products, arithmetic and copies ran while one was open for 3% -> 6% of each run, Pallas kernels for 0% -> 0%
where the time goes in v1:
time: 357 us; the launch traced here: 354 us
  starting transfers between devices  99.5 us (28%)
  waiting for transfers between devices  93.4 us (26%)
  local copies, waits for them, and re-layouts  66.5 us (19%)
  between operations  46.7 us (13%)
  other arithmetic  36.3 us (10%)
  matrix products  11.3 us (3%)
    ppermute x15, starting transfers between devices, padded_2(): lax.ppermute(lax.slice_in_dim(block, block.shape[dim] - width, None, axis...  60.1 us
    ppermute x15, waiting for transfers between devices, padded_2(): lax.ppermute(lax.slice_in_dim(block, 0, width, axis=dim), axis, backward)  42.6 us
    slice x61, local copies, waits for them, and re-layouts, factor(): scale = 1.0 / jnp.sqrt(work[p:p + 1, p:p + 1])  35.4 us
    all_to_all x3, waiting for transfers between devices, gather_sum(): return lax.all_to_all(spread, axis, 0, 0, tiled=True)  26 us
    ppermute x15, waiting for transfers between devices, padded_2(): lax.ppermute(lax.slice_in_dim(block, block.shape[dim] - width, None, axis...  24.8 us
    ppermute x15, starting transfers between devices, padded_2(): lax.ppermute(lax.slice_in_dim(block, 0, width, axis=dim), axis, backward)  23.5 us
    concatenate x10, other arithmetic, padded_2(): block = jnp.concatenate([low, block, high], axis=dim)  13 us
    all_to_all x3, starting transfers between devices, gather_sum(): return lax.all_to_all(spread, axis, 0, 0, tiled=True)  12.5 us
  transfers between devices with their start and end apart: 34, of which 20 were waited for; matrix products, arithmetic and copies ran while one was open for 6% of the time, Pallas kernels for 0%

profile of v1, /device:TPU:1, one launch (start us, length us, event | category | flops | bytes accessed | tf_op | source)
XLA Modules:
  0.0 353.6 jit_solution(12866758207193704861)
XLA Ops:
  2.4 4.0 %collective-permute-start = (f32[11,2,8,128]{3,2,1,0:T(8,128)S(1)}, f32[11,2,8,128]{3,2,1,0:T(8,128)S(1)}, u32[]{:S(2)}, u32[]{:S(2)}) collective-permute-start(f32[11,2,8,128]{3,2,1,0:T(8,128)S(1)} %pad_maximum_fusion.11), channel_id=1, source_target_pairs={{0,64},{64,128},{128,192},{1,65},{65,129},{129,193},{2,66},{66,130... | collective-permute-start | bytes 270344 | tf_op jit(solution)/shard_map/ppermute | solution.py:19
  7.7 1.9 convolution_bitcast_fusion.4
  9.7 4.0 %collective-permute-start.6 = (f32[3,8,1,8,128]{4,1,3,2,0:T(8,128)S(1)}, f32[3,8,1,8,128]{4,1,3,2,0:T(8,128)S(1)}, u32[]{:S(2)}, u32[]{:S(2)}) collective-permute-start(f32[3,8,1,8,128]{4,1,3,2,0:T(8,128)S(1)} %copy.249), channel_id=1, source_target_pairs={{0,64},{64,128},{128,192},{1,65},{65,129},{129,193},{2,66},{66,130... | collective-permute-start | bytes 294920 | tf_op jit(solution)/shard_map/ppermute | solution.py:19
  15.4 3.7 %collective-permute-done.7 = f32[3,8,1,8,128]{4,1,3,2,0:T(8,128)S(1)} collective-permute-done((f32[3,8,1,8,128]{4,1,3,2,0:T(8,128)S(1)}, f32[3,8,1,8,128]{4,1,3,2,0:T(8,128)S(1)}, u32[]{:S(2)}, u32[]{:S(2)}) %collective-permute-start.7) | collective-permute-done | bytes 98336 | tf_op jit(solution)/shard_map/ppermute | solution.py:22
  19.1 5.7 %collective-permute-start.8 = (f32[3,8,4,1,128]{4,1,3,2,0:T(8,128)S(1)}, f32[3,8,4,1,128]{4,1,3,2,0:T(8,128)S(1)}, u32[]{:S(2)}, u32[]{:S(2)}) collective-permute-start(f32[3,8,4,1,128]{4,1,3,2,0:T(8,128)S(1)} %get-tuple-element.68), channel_id=1, source_target_pairs={{0,8},{8,16},{16,24},{24,32},{32,40},{40,48},{48,56},{1,9},{9,17},... | collective-permute-start | bytes 147464 | tf_op jit(solution)/shard_map/ppermute | solution.py:19
  24.8 1.9 collective-permute-start.9
  26.8 3.4 collective-permute-done.9
  31.2 3.6 %collective-permute-start.10 = (f32[3,8,4,10,1]{4,1,3,2,0:T(8,128)}, f32[3,8,4,10,1]{4,1,3,2,0:T(8,128)S(1)}, u32[]{:S(2)}, u32[]{:S(2)}) collective-permute-start(f32[3,8,4,10,1]{4,1,3,2,0:T(8,128)} %get-tuple-element.60), channel_id=1, source_target_pairs={{0,1},{1,2},{2,3},{3,4},{4,5},{5,6},{6,7},{8,9},{9,10},{10,11},{11... | collective-permute-start | bytes 11528 | tf_op jit(solution)/shard_map/ppermute | solution.py:19
  36.1 3.8 %copy.175 = f32[11,6,8,128]{2,1,3,0:T(8,128)} copy(f32[11,6,8,128]{3,2,1,0:T(8,128)S(1)} %pad_maximum_fusion.10) | data formatting | bytes 540672 | tf_op jit(solution)/shard_map/concatenate | solution.py:23
  40.0 2.2 collective-permute-start.2
  42.8 2.8 collective-permute-start.3
  45.6 2.5 collective-permute-done.11
  48.6 4.5 %copy.174 = f32[11,6,2,128]{2,1,3,0:T(8,128)} copy(f32[11,6,2,128]{3,1,2,0:T(8,128)} %collective-permute-done.2) | data formatting | bytes 135168 | tf_op jit(solution)/shard_map/ppermute | solution.py:19
  53.1 3.9 %copy.176 = f32[11,6,2,128]{2,1,3,0:T(8,128)} copy(f32[11,6,2,128]{3,1,2,0:T(8,128)S(1)} %collective-permute-done.3) | data formatting | bytes 135168 | tf_op jit(solution)/shard_map/ppermute | solution.py:22
  57.0 9.0 %pad_maximum_fusion = f32[11,6,12,128]{2,1,3,0:T(8,128)S(1)} fusion(f32[11,6,2,128]{2,1,3,0:T(8,128)} %copy.176, f32[11,6,8,128]{2,1,3,0:T(8,128)} %copy.175, f32[11,6,2,128]{2,1,3,0:T(8,128)} %copy.174), kind=kLoop, calls=%fused_computation | loop fusion | flops 202752 | bytes 811008 | tf_op jit(solution)/shard_map/concatenate | solution.py:23
  66.0 2.5 copy-done.2
  68.5 3.5 collective-permute-start.4
  74.4 4.2 %copy.178 = f32[11,6,12,128]{3,2,1,0:T(8,128)S(1)} copy(f32[11,6,12,128]{2,1,3,0:T(8,128)} %copy-done.2) | data formatting | bytes 811008 | tf_op jit(solution)/shard_map/concatenate | solution.py:23
  84.1 3.2 collective-permute-start.12
  89.7 3.9 %collective-permute-done.13 = f32[3,8,1,8,128]{4,1,3,2,0:T(8,128)S(1)} collective-permute-done((f32[3,8,1,8,128]{4,1,3,2,0:T(8,128)S(1)}, f32[3,8,1,8,128]{4,1,3,2,0:T(8,128)S(1)}, u32[]{:S(2)}, u32[]{:S(2)}) %collective-permute-start.13) | collective-permute-done | bytes 98336 | tf_op jit(solution)/shard_map/ppermute | solution.py:22
  93.6 5.8 %collective-permute-start.14 = (f32[3,8,4,1,128]{4,1,3,2,0:T(8,128)S(1)}, f32[3,8,4,1,128]{4,1,3,2,0:T(8,128)S(1)}, u32[]{:S(2)}, u32[]{:S(2)}) collective-permute-start(f32[3,8,4,1,128]{4,1,3,2,0:T(8,128)S(1)} %get-tuple-element.66), channel_id=1, source_target_pairs={{0,8},{8,16},{16,24},{24,32},{32,40},{40,48},{48,56},{1,9},{9,17},... | collective-permute-start | bytes 147464 | tf_op jit(solution)/shard_map/ppermute | solution.py:19
  99.4 1.9 collective-permute-start.15
  101.4 3.5 collective-permute-done.15
  105.1 4.9 %collective-permute-start.16 = (f32[3,8,4,10,1]{4,1,3,2,0:T(8,128)S(1)}, f32[3,8,4,10,1]{4,1,3,2,0:T(8,128)S(1)}, u32[]{:S(2)}, u32[]{:S(2)}) collective-permute-start(f32[3,8,4,10,1]{4,1,3,2,0:T(8,128)S(1)} %get-tuple-element.58), channel_id=1, source_target_pairs={{0,1},{1,2},{2,3},{3,4},{4,5},{5,6},{6,7},{8,9},{9,10},{10,11},{11... | collective-permute-start | bytes 11528 | tf_op jit(solution)/shard_map/ppermute | solution.py:19
  111.2 7.9 %collective-permute-done.16 = f32[3,8,4,10,1]{4,1,3,2,0:T(8,128)S(1)} collective-permute-done((f32[3,8,4,10,1]{4,1,3,2,0:T(8,128)S(1)}, f32[3,8,4,10,1]{4,1,3,2,0:T(8,128)S(1)}, u32[]{:S(2)}, u32[]{:S(2)}) %collective-permute-start.16) | collective-permute-done | bytes 3872 | tf_op jit(solution)/shard_map/ppermute | solution.py:19
  119.1 5.3 %collective-permute-done.17 = f32[3,8,4,10,1]{4,1,3,2,0:T(8,128)S(1)} collective-permute-done((f32[3,8,4,10,1]{4,1,3,2,0:T(8,128)S(1)}, f32[3,8,4,10,1]{4,1,3,2,0:T(8,128)S(1)}, u32[]{:S(2)}, u32[]{:S(2)}) %collective-permute-start.17) | collective-permute-done | bytes 3872 | tf_op jit(solution)/shard_map/ppermute | solution.py:22
  126.5 2.9 collective-permute-start.18
  131.3 4.1 %collective-permute-done.19 = f32[3,8,1,8,128]{4,1,3,2,0:T(8,128)S(1)} collective-permute-done((f32[3,8,1,8,128]{4,1,3,2,0:T(8,128)S(1)}, f32[3,8,1,8,128]{4,1,3,2,0:T(8,128)S(1)}, u32[]{:S(2)}, u32[]{:S(2)}) %collective-permute-start.19) | collective-permute-done | bytes 98336 | tf_op jit(solution)/shard_map/ppermute | solution.py:22
  135.4 5.3 %collective-permute-start.20 = (f32[3,8,4,1,128]{4,1,3,2,0:T(8,128)S(1)}, f32[3,8,4,1,128]{4,1,3,2,0:T(8,128)S(1)}, u32[]{:S(2)}, u32[]{:S(2)}) collective-permute-start(f32[3,8,4,1,128]{4,1,3,2,0:T(8,128)S(1)} %get-tuple-element.64), channel_id=1, source_target_pairs={{0,8},{8,16},{16,24},{24,32},{32,40},{40,48},{48,56},{1,9},{9,17},... | collective-permute-start | bytes 147464 | tf_op jit(solution)/shard_map/ppermute | solution.py:19
  140.7 1.9 collective-permute-start.21
  142.7 3.5 collective-permute-done.21
  146.4 3.7 %collective-permute-start.22 = (f32[3,8,4,10,1]{4,1,3,2,0:T(8,128)S(1)}, f32[3,8,4,10,1]{4,1,3,2,0:T(8,128)S(1)}, u32[]{:S(2)}, u32[]{:S(2)}) collective-permute-start(f32[3,8,4,10,1]{4,1,3,2,0:T(8,128)S(1)} %get-tuple-element.56), channel_id=1, source_target_pairs={{0,1},{1,2},{2,3},{3,4},{4,5},{5,6},{6,7},{8,9},{9,10},{10,11},{11... | collective-permute-start | bytes 11528 | tf_op jit(solution)/shard_map/ppermute | solution.py:19
  151.5 7.7 %collective-permute-done.22 = f32[3,8,4,10,1]{4,1,3,2,0:T(8,128)S(1)} collective-permute-done((f32[3,8,4,10,1]{4,1,3,2,0:T(8,128)S(1)}, f32[3,8,4,10,1]{4,1,3,2,0:T(8,128)S(1)}, u32[]{:S(2)}, u32[]{:S(2)}) %collective-permute-start.22) | collective-permute-done | bytes 3872 | tf_op jit(solution)/shard_map/ppermute | solution.py:19
  159.2 4.1 %collective-permute-done.23 = f32[3,8,4,10,1]{4,1,3,2,0:T(8,128)S(1)} collective-permute-done((f32[3,8,4,10,1]{4,1,3,2,0:T(8,128)S(1)}, f32[3,8,4,10,1]{4,1,3,2,0:T(8,128)S(1)}, u32[]{:S(2)}, u32[]{:S(2)}) %collective-permute-start.23) | collective-permute-done | bytes 3872 | tf_op jit(solution)/shard_map/ppermute | solution.py:22
  166.1 2.5 collective-permute-start.24
  170.6 4.3 %collective-permute-done.25 = f32[3,8,1,8,128]{4,1,3,2,0:T(8,128)} collective-permute-done((f32[3,8,1,8,128]{4,1,3,2,0:T(8,128)}, f32[3,8,1,8,128]{4,1,3,2,0:T(8,128)}, u32[]{:S(2)}, u32[]{:S(2)}) %collective-permute-start.25) | collective-permute-done | bytes 98336 | tf_op jit(solution)/shard_map/ppermute | solution.py:22
  176.3 4.3 %collective-permute-start.26 = (f32[3,8,4,1,128]{4,1,3,2,0:T(8,128)}, f32[3,8,4,1,128]{4,1,3,2,0:T(8,128)}, u32[]{:S(2)}, u32[]{:S(2)}) collective-permute-start(f32[3,8,4,1,128]{4,1,3,2,0:T(8,128)} %get-tuple-element.62), channel_id=1, source_target_pairs={{0,8},{8,16},{16,24},{24,32},{32,40},{40,48},{48,56},{1,9},{9,17},... | collective-permute-start | bytes 147464 | tf_op jit(solution)/shard_map/ppermute | solution.py:19
  180.6 1.9 collective-permute-start.27
  183.7 3.3 all-to-all-start
  189.0 4.6 %collective-permute-start.28 = (f32[3,8,4,10,1]{4,1,3,2,0:T(8,128)}, f32[3,8,4,10,1]{4,1,3,2,0:T(8,128)S(1)}, u32[]{:S(2)}, u32[]{:S(2)}) collective-permute-start(f32[3,8,4,10,1]{4,1,3,2,0:T(8,128)} %get-tuple-element.54), channel_id=1, source_target_pairs={{0,1},{1,2},{2,3},{3,4},{4,5},{5,6},{6,7},{8,9},{9,10},{10,11},{11... | collective-permute-start | bytes 11528 | tf_op jit(solution)/shard_map/ppermute | solution.py:19
  195.5 7.4 %collective-permute-done.28 = f32[3,8,4,10,1]{4,1,3,2,0:T(8,128)S(1)} collective-permute-done((f32[3,8,4,10,1]{4,1,3,2,0:T(8,128)}, f32[3,8,4,10,1]{4,1,3,2,0:T(8,128)S(1)}, u32[]{:S(2)}, u32[]{:S(2)}) %collective-permute-start.28) | collective-permute-done | bytes 3872 | tf_op jit(solution)/shard_map/ppermute | solution.py:19
  202.9 4.3 %collective-permute-done.29 = f32[3,8,4,10,1]{4,1,3,2,0:T(8,128)} collective-permute-done((f32[3,8,4,10,1]{4,1,3,2,0:T(8,128)S(1)}, f32[3,8,4,10,1]{4,1,3,2,0:T(8,128)}, u32[]{:S(2)}, u32[]{:S(2)}) %collective-permute-start.29) | collective-permute-done | bytes 3872 | tf_op jit(solution)/shard_map/ppermute | solution.py:22
  212.1 3.7 %all-to-all-start.1 = ((f32[8,96,128]{2,1,0:T(8,128)}), f32[8,96,128]{2,1,0:T(8,128)S(1)}, u32[]{:S(2)}, u32[]{:S(2)}) async-start(f32[8,96,128]{2,1,0:T(8,128)} %broadcast_in_dim.630), calls=%async_computation.1 | async-start | bytes 786432 | tf_op jit(solution)/shard_map/all_to_all | solution.py:89
  215.8 8.1 %all-to-all-done.1 = f32[8,96,128]{2,1,0:T(8,128)S(1)} async-done(((f32[8,96,128]{2,1,0:T(8,128)}), f32[8,96,128]{2,1,0:T(8,128)S(1)}, u32[]{:S(2)}, u32[]{:S(2)}) %all-to-all-start.1) | async-done | bytes 393248 | tf_op jit(solution)/shard_map/all_to_all | solution.py:89
  224.7 4.6 %all-to-all-start.2 = ((f32[8,96,128]{2,1,0:T(8,128)}), f32[8,96,128]{2,1,0:T(8,128)S(1)}, u32[]{:S(2)}, u32[]{:S(2)}) async-start(f32[8,96,128]{2,1,0:T(8,128)} %broadcast_in_dim.631), calls=%async_computation.2 | async-start | bytes 786432 | tf_op jit(solution)/shard_map/all_to_all | solution.py:89
  229.3 13.5 %all-to-all-done.2 = f32[8,96,128]{2,1,0:T(8,128)S(1)} async-done(((f32[8,96,128]{2,1,0:T(8,128)}), f32[8,96,128]{2,1,0:T(8,128)S(1)}, u32[]{:S(2)}, u32[]{:S(2)}) %all-to-all-start.2) | async-done | bytes 393248 | tf_op jit(solution)/shard_map/all_to_all | solution.py:89
  243.5 4.2 %all-to-all-start.3 = ((f32[4,96,128]{2,1,0:T(8,128)}), f32[4,96,128]{2,1,0:T(8,128)S(1)}, u32[]{:S(2)}, u32[]{:S(2)}) async-start(f32[4,96,128]{2,1,0:T(8,128)} %broadcast_in_dim.632), calls=%async_computation.3 | async-start | bytes 393216 | tf_op jit(solution)/shard_map/all_to_all | solution.py:89
  248.4 4.5 %all-to-all-done.3 = f32[4,96,128]{2,1,0:T(8,128)S(1)} async-done(((f32[4,96,128]{2,1,0:T(8,128)}), f32[4,96,128]{2,1,0:T(8,128)S(1)}, u32[]{:S(2)}, u32[]{:S(2)}) %all-to-all-start.3) | async-done | bytes 196640 | tf_op jit(solution)/shard_map/all_to_all | solution.py:89
  (428 shorter events, 99.1 us)
Async XLA Ops:
  0.6 82.9 %copy-start = (bf16[128,8]{0,1:T(8,128)(2,1)S(1)}, bf16[128,8]{0,1:T(8,128)(2,1)}, u32[]{:S(2)}) copy-start(bf16[128,8]{0,1:T(8,128)(2,1)} %param.9) | copy-start | bytes 6148
  2.4 24.3 %collective-permute-start = (f32[11,2,8,128]{3,2,1,0:T(8,128)S(1)}, f32[11,2,8,128]{3,2,1,0:T(8,128)S(1)}, u32[]{:S(2)}, u32[]{:S(2)}) collective-permute-start(f32[11,2,8,128]{3,2,1,0:T(8,128)S(1)} %pad_maximum_fusion.11), channel_id=1, source_target_pairs={{0,64},{64,128},{128,192},{1,65},{65,129},{129,193},{2,66},{66,130... | collective-permute-start | bytes 270344 | tf_op jit(solution)/shard_map/ppermute | solution.py:19
  6.4 20.3 %collective-permute-start.1 = (f32[11,2,8,128]{3,2,1,0:T(8,128)S(1)}, f32[11,2,8,128]{3,2,1,0:T(8,128)S(1)}, u32[]{:S(2)}, u32[]{:S(2)}) collective-permute-start(f32[11,2,8,128]{3,2,1,0:T(8,128)S(1)} %pad_maximum_fusion.11), channel_id=1, source_target_pairs={{64,0},{128,64},{192,128},{65,1},{129,65},{193,129},{66,2},{130,66... | collective-permute-start | bytes 270344 | tf_op jit(solution)/shard_map/ppermute | solution.py:22
  9.7 5.6 %collective-permute-start.6 = (f32[3,8,1,8,128]{4,1,3,2,0:T(8,128)S(1)}, f32[3,8,1,8,128]{4,1,3,2,0:T(8,128)S(1)}, u32[]{:S(2)}, u32[]{:S(2)}) collective-permute-start(f32[3,8,1,8,128]{4,1,3,2,0:T(8,128)S(1)} %copy.249), channel_id=1, source_target_pairs={{0,64},{64,128},{128,192},{1,65},{65,129},{129,193},{2,66},{66,130... | collective-permute-start | bytes 294920 | tf_op jit(solution)/shard_map/ppermute | solution.py:19
  13.7 5.4 %collective-permute-start.7 = (f32[3,8,1,8,128]{4,1,3,2,0:T(8,128)S(1)}, f32[3,8,1,8,128]{4,1,3,2,0:T(8,128)S(1)}, u32[]{:S(2)}, u32[]{:S(2)}) collective-permute-start(f32[3,8,1,8,128]{4,1,3,2,0:T(8,128)S(1)} %copy.250), channel_id=1, source_target_pairs={{64,0},{128,64},{192,128},{65,1},{129,65},{193,129},{66,2},{130,66... | collective-permute-start | bytes 294920 | tf_op jit(solution)/shard_map/ppermute | solution.py:22
  15.0 68.4 %copy-start.17 = (f32[1,2,8,128]{3,0,2,1:T(1,128)}, f32[1,2,8,128]{3,0,2,1:T(1,128)S(1)}, u32[]{:S(2)}) copy-start(f32[1,2,8,128]{3,0,2,1:T(1,128)S(1)} %slice_multiply_fusion.1) | copy-start | bytes 24580
  15.1 68.4 %copy-start.4 = (f32[8,2,8,128]{3,0,2,1:T(8,128)}, f32[8,2,8,128]{3,0,2,1:T(8,128)S(1)}, u32[]{:S(2)}) copy-start(f32[8,2,8,128]{3,0,2,1:T(8,128)S(1)} %copy.170) | copy-start | bytes 196612
  19.1 7.7 %collective-permute-start.8 = (f32[3,8,4,1,128]{4,1,3,2,0:T(8,128)S(1)}, f32[3,8,4,1,128]{4,1,3,2,0:T(8,128)S(1)}, u32[]{:S(2)}, u32[]{:S(2)}) collective-permute-start(f32[3,8,4,1,128]{4,1,3,2,0:T(8,128)S(1)} %get-tuple-element.68), channel_id=1, source_target_pairs={{0,8},{8,16},{16,24},{24,32},{32,40},{40,48},{48,56},{1,9},{9,17},... | collective-permute-start | bytes 147464 | tf_op jit(solution)/shard_map/ppermute | solution.py:19
  24.8 5.4 %collective-permute-start.9 = (f32[3,8,4,1,128]{4,1,3,2,0:T(8,128)S(1)}, f32[3,8,4,1,128]{4,1,3,2,0:T(8,128)S(1)}, u32[]{:S(2)}, u32[]{:S(2)}) collective-permute-start(f32[3,8,4,1,128]{4,1,3,2,0:T(8,128)S(1)} %get-tuple-element.69), channel_id=1, source_target_pairs={{8,0},{16,8},{24,16},{32,24},{40,32},{48,40},{56,48},{9,1},{17,9},... | collective-permute-start | bytes 147464 | tf_op jit(solution)/shard_map/ppermute | solution.py:22
  31.2 14.4 %collective-permute-start.10 = (f32[3,8,4,10,1]{4,1,3,2,0:T(8,128)}, f32[3,8,4,10,1]{4,1,3,2,0:T(8,128)S(1)}, u32[]{:S(2)}, u32[]{:S(2)}) collective-permute-start(f32[3,8,4,10,1]{4,1,3,2,0:T(8,128)} %get-tuple-element.60), channel_id=1, source_target_pairs={{0,1},{1,2},{2,3},{3,4},{4,5},{5,6},{6,7},{8,9},{9,10},{10,11},{11... | collective-permute-start | bytes 11528 | tf_op jit(solution)/shard_map/ppermute | solution.py:19
  34.8 13.3 %collective-permute-start.11 = (f32[3,8,4,10,1]{4,1,3,2,0:T(8,128)S(1)}, f32[3,8,4,10,1]{4,1,3,2,0:T(8,128)S(1)}, u32[]{:S(2)}, u32[]{:S(2)}) collective-permute-start(f32[3,8,4,10,1]{4,1,3,2,0:T(8,128)S(1)} %get-tuple-element.61), channel_id=1, source_target_pairs={{1,0},{2,1},{3,2},{4,3},{5,4},{6,5},{7,6},{9,8},{10,9},{11,10},{12... | collective-permute-start | bytes 11528 | tf_op jit(solution)/shard_map/ppermute | solution.py:22
  40.0 8.6 %collective-permute-start.2 = (f32[11,6,2,128]{3,1,2,0:T(8,128)S(1)}, f32[11,6,2,128]{3,1,2,0:T(8,128)}, u32[]{:S(2)}, u32[]{:S(2)}) collective-permute-start(f32[11,6,2,128]{3,1,2,0:T(8,128)S(1)} %copy.219), channel_id=1, source_target_pairs={{0,8},{8,16},{16,24},{24,32},{32,40},{40,48},{48,56},{1,9},{9,17},... | collective-permute-start | bytes 202760 | tf_op jit(solution)/shard_map/ppermute | solution.py:19
  42.8 10.3 %collective-permute-start.3 = (f32[11,6,2,128]{3,1,2,0:T(8,128)}, f32[11,6,2,128]{3,1,2,0:T(8,128)S(1)}, u32[]{:S(2)}, u32[]{:S(2)}) collective-permute-start(f32[11,6,2,128]{3,1,2,0:T(8,128)} %copy.220), channel_id=1, source_target_pairs={{8,0},{16,8},{24,16},{32,24},{40,32},{48,40},{56,48},{9,1},{17,9},... | collective-permute-start | bytes 202760 | tf_op jit(solution)/shard_map/ppermute | solution.py:22
  68.5 10.1 %collective-permute-start.4 = (f32[11,6,12,2]{2,1,3,0:T(8,128)S(1)}, f32[11,6,12,2]{2,1,3,0:T(8,128)S(1)}, u32[]{:S(2)}, u32[]{:S(2)}) collective-permute-start(f32[11,6,12,2]{2,1,3,0:T(8,128)S(1)} %get-tuple-element.34), channel_id=1, source_target_pairs={{0,1},{1,2},{2,3},{3,4},{4,5},{5,6},{6,7},{8,9},{9,10},{10,11},{11... | collective-permute-start | bytes 19016 | tf_op jit(solution)/shard_map/ppermute | solution.py:19
  72.1 7.1 %collective-permute-start.5 = (f32[11,6,12,2]{2,1,3,0:T(8,128)S(1)}, f32[11,6,12,2]{2,1,3,0:T(8,128)S(1)}, u32[]{:S(2)}, u32[]{:S(2)}) collective-permute-start(f32[11,6,12,2]{2,1,3,0:T(8,128)S(1)} %get-tuple-element.35), channel_id=1, source_target_pairs={{1,0},{2,1},{3,2},{4,3},{5,4},{6,5},{7,6},{9,8},{10,9},{11,10},{12... | collective-permute-start | bytes 19016 | tf_op jit(solution)/shard_map/ppermute | solution.py:22
  79.9 84.1 %copy-start.13 = (f32[2,8,128]{2,1,0:T(8,128)}, f32[2,8,128]{2,1,0:T(8,128)S(1)}, u32[]{:S(2)}) copy-start(f32[2,8,128]{2,1,0:T(8,128)S(1)} %get-tuple-element.90) | copy-start | bytes 24580
  80.0 84.1 %copy-start.15 = (f32[2,8,128]{2,1,0:T(8,128)}, f32[2,8,128]{2,1,0:T(8,128)S(1)}, u32[]{:S(2)}) copy-start(f32[2,8,128]{2,1,0:T(8,128)S(1)} %get-tuple-element.92) | copy-start | bytes 24580
  80.0 84.3 %copy-start.7 = (f32[2,8,128]{2,1,0:T(8,128)}, f32[2,8,128]{2,1,0:T(8,128)S(1)}, u32[]{:S(2)}) copy-start(f32[2,8,128]{2,1,0:T(8,128)S(1)} %get-tuple-element.93) | copy-start | bytes 24580
  80.0 84.3 %copy-start.9 = (f32[2,8,128]{2,1,0:T(8,128)}, f32[2,8,128]{2,1,0:T(8,128)S(1)}, u32[]{:S(2)}) copy-start(f32[2,8,128]{2,1,0:T(8,128)S(1)} %get-tuple-element.94) | copy-start | bytes 24580
  80.0 84.3 %copy-start.11 = (f32[2,8,128]{2,1,0:T(8,128)}, f32[2,8,128]{2,1,0:T(8,128)S(1)}, u32[]{:S(2)}) copy-start(f32[2,8,128]{2,1,0:T(8,128)S(1)} %get-tuple-element.95) | copy-start | bytes 24580
  80.1 83.8 %copy-start.28 = (f32[2,8,128]{2,1,0:T(8,128)}, f32[2,8,128]{2,1,0:T(8,128)S(1)}, u32[]{:S(2)}) copy-start(f32[2,8,128]{2,1,0:T(8,128)S(1)} %get-tuple-element.84) | copy-start | bytes 24580
  80.1 83.8 %copy-start.30 = (f32[2,8,128]{2,1,0:T(8,128)}, f32[2,8,128]{2,1,0:T(8,128)S(1)}, u32[]{:S(2)}) copy-start(f32[2,8,128]{2,1,0:T(8,128)S(1)} %get-tuple-element.85) | copy-start | bytes 24580
  80.1 84.0 %copy-start.24 = (f32[2,8,128]{2,1,0:T(8,128)}, f32[2,8,128]{2,1,0:T(8,128)S(1)}, u32[]{:S(2)}) copy-start(f32[2,8,128]{2,1,0:T(8,128)S(1)} %get-tuple-element.88) | copy-start | bytes 24580
  80.1 84.0 %copy-start.26 = (f32[2,8,128]{2,1,0:T(8,128)}, f32[2,8,128]{2,1,0:T(8,128)S(1)}, u32[]{:S(2)}) copy-start(f32[2,8,128]{2,1,0:T(8,128)S(1)} %get-tuple-element.89) | copy-start | bytes 24580
  80.1 84.2 %copy-start.20 = (f32[2,8,128]{2,1,0:T(8,128)}, f32[2,8,128]{2,1,0:T(8,128)S(1)}, u32[]{:S(2)}) copy-start(f32[2,8,128]{2,1,0:T(8,128)S(1)} %get-tuple-element.86) | copy-start | bytes 24580
  80.1 84.2 %copy-start.22 = (f32[2,8,128]{2,1,0:T(8,128)}, f32[2,8,128]{2,1,0:T(8,128)S(1)}, u32[]{:S(2)}) copy-start(f32[2,8,128]{2,1,0:T(8,128)S(1)} %get-tuple-element.87) | copy-start | bytes 24580
  84.1 5.6 %collective-permute-start.12 = (f32[3,8,1,8,128]{4,1,3,2,0:T(8,128)S(1)}, f32[3,8,1,8,128]{4,1,3,2,0:T(8,128)S(1)}, u32[]{:S(2)}, u32[]{:S(2)}) collective-permute-start(f32[3,8,1,8,128]{4,1,3,2,0:T(8,128)S(1)} %get-tuple-element.77), channel_id=1, source_target_pairs={{0,64},{64,128},{128,192},{1,65},{65,129},{129,193},{2,66},{66,130... | collective-permute-start | bytes 294920 | tf_op jit(solution)/shard_map/ppermute | solution.py:19
  87.3 6.3 %collective-permute-start.13 = (f32[3,8,1,8,128]{4,1,3,2,0:T(8,128)S(1)}, f32[3,8,1,8,128]{4,1,3,2,0:T(8,128)S(1)}, u32[]{:S(2)}, u32[]{:S(2)}) collective-permute-start(f32[3,8,1,8,128]{4,1,3,2,0:T(8,128)S(1)} %get-tuple-element.78), channel_id=1, source_target_pairs={{64,0},{128,64},{192,128},{65,1},{129,65},{193,129},{66,2},{130,66... | collective-permute-start | bytes 294920 | tf_op jit(solution)/shard_map/ppermute | solution.py:22
  93.6 7.7 %collective-permute-start.14 = (f32[3,8,4,1,128]{4,1,3,2,0:T(8,128)S(1)}, f32[3,8,4,1,128]{4,1,3,2,0:T(8,128)S(1)}, u32[]{:S(2)}, u32[]{:S(2)}) collective-permute-start(f32[3,8,4,1,128]{4,1,3,2,0:T(8,128)S(1)} %get-tuple-element.66), channel_id=1, source_target_pairs={{0,8},{8,16},{16,24},{24,32},{32,40},{40,48},{48,56},{1,9},{9,17},... | collective-permute-start | bytes 147464 | tf_op jit(solution)/shard_map/ppermute | solution.py:19
  99.4 5.4 %collective-permute-start.15 = (f32[3,8,4,1,128]{4,1,3,2,0:T(8,128)S(1)}, f32[3,8,4,1,128]{4,1,3,2,0:T(8,128)S(1)}, u32[]{:S(2)}, u32[]{:S(2)}) collective-permute-start(f32[3,8,4,1,128]{4,1,3,2,0:T(8,128)S(1)} %get-tuple-element.67), channel_id=1, source_target_pairs={{8,0},{16,8},{24,16},{32,24},{40,32},{48,40},{56,48},{9,1},{17,9},... | collective-permute-start | bytes 147464 | tf_op jit(solution)/shard_map/ppermute | solution.py:22
  105.1 14.1 %collective-permute-start.16 = (f32[3,8,4,10,1]{4,1,3,2,0:T(8,128)S(1)}, f32[3,8,4,10,1]{4,1,3,2,0:T(8,128)S(1)}, u32[]{:S(2)}, u32[]{:S(2)}) collective-permute-start(f32[3,8,4,10,1]{4,1,3,2,0:T(8,128)S(1)} %get-tuple-element.58), channel_id=1, source_target_pairs={{0,1},{1,2},{2,3},{3,4},{4,5},{5,6},{6,7},{8,9},{9,10},{10,11},{11... | collective-permute-start | bytes 11528 | tf_op jit(solution)/shard_map/ppermute | solution.py:19
  109.9 14.4 %collective-permute-start.17 = (f32[3,8,4,10,1]{4,1,3,2,0:T(8,128)S(1)}, f32[3,8,4,10,1]{4,1,3,2,0:T(8,128)S(1)}, u32[]{:S(2)}, u32[]{:S(2)}) collective-permute-start(f32[3,8,4,10,1]{4,1,3,2,0:T(8,128)S(1)} %get-tuple-element.59), channel_id=1, source_target_pairs={{1,0},{2,1},{3,2},{4,3},{5,4},{6,5},{7,6},{9,8},{10,9},{11,10},{12... | collective-permute-start | bytes 11528 | tf_op jit(solution)/shard_map/ppermute | solution.py:22
  126.5 4.8 %collective-permute-start.18 = (f32[3,8,1,8,128]{4,1,3,2,0:T(8,128)S(1)}, f32[3,8,1,8,128]{4,1,3,2,0:T(8,128)S(1)}, u32[]{:S(2)}, u32[]{:S(2)}) collective-permute-start(f32[3,8,1,8,128]{4,1,3,2,0:T(8,128)S(1)} %copy.251), channel_id=1, source_target_pairs={{0,64},{64,128},{128,192},{1,65},{65,129},{129,193},{2,66},{66,130... | collective-permute-start | bytes 294920 | tf_op jit(solution)/shard_map/ppermute | solution.py:19
  129.4 6.0 %collective-permute-start.19 = (f32[3,8,1,8,128]{4,1,3,2,0:T(8,128)S(1)}, f32[3,8,1,8,128]{4,1,3,2,0:T(8,128)S(1)}, u32[]{:S(2)}, u32[]{:S(2)}) collective-permute-start(f32[3,8,1,8,128]{4,1,3,2,0:T(8,128)S(1)} %copy.252), channel_id=1, source_target_pairs={{64,0},{128,64},{192,128},{65,1},{129,65},{193,129},{66,2},{130,66... | collective-permute-start | bytes 294920 | tf_op jit(solution)/shard_map/ppermute | solution.py:22
  135.4 7.2 %collective-permute-start.20 = (f32[3,8,4,1,128]{4,1,3,2,0:T(8,128)S(1)}, f32[3,8,4,1,128]{4,1,3,2,0:T(8,128)S(1)}, u32[]{:S(2)}, u32[]{:S(2)}) collective-permute-start(f32[3,8,4,1,128]{4,1,3,2,0:T(8,128)S(1)} %get-tuple-element.64), channel_id=1, source_target_pairs={{0,8},{8,16},{16,24},{24,32},{32,40},{40,48},{48,56},{1,9},{9,17},... | collective-permute-start | bytes 147464 | tf_op jit(solution)/shard_map/ppermute | solution.py:19
  140.7 5.4 %collective-permute-start.21 = (f32[3,8,4,1,128]{4,1,3,2,0:T(8,128)S(1)}, f32[3,8,4,1,128]{4,1,3,2,0:T(8,128)S(1)}, u32[]{:S(2)}, u32[]{:S(2)}) collective-permute-start(f32[3,8,4,1,128]{4,1,3,2,0:T(8,128)S(1)} %get-tuple-element.65), channel_id=1, source_target_pairs={{8,0},{16,8},{24,16},{32,24},{40,32},{48,40},{56,48},{9,1},{17,9},... | collective-permute-start | bytes 147464 | tf_op jit(solution)/shard_map/ppermute | solution.py:22
  146.4 12.9 %collective-permute-start.22 = (f32[3,8,4,10,1]{4,1,3,2,0:T(8,128)S(1)}, f32[3,8,4,10,1]{4,1,3,2,0:T(8,128)S(1)}, u32[]{:S(2)}, u32[]{:S(2)}) collective-permute-start(f32[3,8,4,10,1]{4,1,3,2,0:T(8,128)S(1)} %get-tuple-element.56), channel_id=1, source_target_pairs={{0,1},{1,2},{2,3},{3,4},{4,5},{5,6},{6,7},{8,9},{9,10},{10,11},{11... | collective-permute-start | bytes 11528 | tf_op jit(solution)/shard_map/ppermute | solution.py:19
  150.0 13.3 %collective-permute-start.23 = (f32[3,8,4,10,1]{4,1,3,2,0:T(8,128)S(1)}, f32[3,8,4,10,1]{4,1,3,2,0:T(8,128)S(1)}, u32[]{:S(2)}, u32[]{:S(2)}) collective-permute-start(f32[3,8,4,10,1]{4,1,3,2,0:T(8,128)S(1)} %get-tuple-element.57), channel_id=1, source_target_pairs={{1,0},{2,1},{3,2},{4,3},{5,4},{6,5},{7,6},{9,8},{10,9},{11,10},{12... | collective-permute-start | bytes 11528 | tf_op jit(solution)/shard_map/ppermute | solution.py:22
  166.1 4.5 %collective-permute-start.24 = (f32[3,8,1,8,128]{4,1,3,2,0:T(8,128)}, f32[3,8,1,8,128]{4,1,3,2,0:T(8,128)}, u32[]{:S(2)}, u32[]{:S(2)}) collective-permute-start(f32[3,8,1,8,128]{4,1,3,2,0:T(8,128)} %get-tuple-element.73), channel_id=1, source_target_pairs={{0,64},{64,128},{128,192},{1,65},{65,129},{129,193},{2,66},{66,130... | collective-permute-start | bytes 294920 | tf_op jit(solution)/shard_map/ppermute | solution.py:19
  168.6 6.3 %collective-permute-start.25 = (f32[3,8,1,8,128]{4,1,3,2,0:T(8,128)}, f32[3,8,1,8,128]{4,1,3,2,0:T(8,128)}, u32[]{:S(2)}, u32[]{:S(2)}) collective-permute-start(f32[3,8,1,8,128]{4,1,3,2,0:T(8,128)} %get-tuple-element.74), channel_id=1, source_target_pairs={{64,0},{128,64},{192,128},{65,1},{129,65},{193,129},{66,2},{130,66... | collective-permute-start | bytes 294920 | tf_op jit(solution)/shard_map/ppermute | solution.py:22
  176.3 10.7 %collective-permute-start.26 = (f32[3,8,4,1,128]{4,1,3,2,0:T(8,128)}, f32[3,8,4,1,128]{4,1,3,2,0:T(8,128)}, u32[]{:S(2)}, u32[]{:S(2)}) collective-permute-start(f32[3,8,4,1,128]{4,1,3,2,0:T(8,128)} %get-tuple-element.62), channel_id=1, source_target_pairs={{0,8},{8,16},{16,24},{24,32},{32,40},{40,48},{48,56},{1,9},{9,17},... | collective-permute-start | bytes 147464 | tf_op jit(solution)/shard_map/ppermute | solution.py:19
  180.6 6.4 %collective-permute-start.27 = (f32[3,8,4,1,128]{4,1,3,2,0:T(8,128)}, f32[3,8,4,1,128]{4,1,3,2,0:T(8,128)}, u32[]{:S(2)}, u32[]{:S(2)}) collective-permute-start(f32[3,8,4,1,128]{4,1,3,2,0:T(8,128)} %get-tuple-element.63), channel_id=1, source_target_pairs={{8,0},{16,8},{24,16},{32,24},{40,32},{48,40},{56,48},{9,1},{17,9},... | collective-permute-start | bytes 147464 | tf_op jit(solution)/shard_map/ppermute | solution.py:22
  183.7 11.2 %all-to-all-start = ((f32[4,32,128]{2,1,0:T(8,128)}), f32[4,32,128]{2,1,0:T(8,128)S(1)}, u32[]{:S(2)}, u32[]{:S(2)}) async-start(f32[4,32,128]{2,1,0:T(8,128)} %fusion.288), calls=%async_computation | async-start | bytes 131072 | tf_op jit(solution)/shard_map/all_to_all | solution.py:95
  189.0 13.9 %collective-permute-start.28 = (f32[3,8,4,10,1]{4,1,3,2,0:T(8,128)}, f32[3,8,4,10,1]{4,1,3,2,0:T(8,128)S(1)}, u32[]{:S(2)}, u32[]{:S(2)}) collective-permute-start(f32[3,8,4,10,1]{4,1,3,2,0:T(8,128)} %get-tuple-element.54), channel_id=1, source_target_pairs={{0,1},{1,2},{2,3},{3,4},{4,5},{5,6},{6,7},{8,9},{9,10},{10,11},{11... | collective-permute-start | bytes 11528 | tf_op jit(solution)/shard_map/ppermute | solution.py:19
  193.6 13.6 %collective-permute-start.29 = (f32[3,8,4,10,1]{4,1,3,2,0:T(8,128)S(1)}, f32[3,8,4,10,1]{4,1,3,2,0:T(8,128)}, u32[]{:S(2)}, u32[]{:S(2)}) collective-permute-start(f32[3,8,4,10,1]{4,1,3,2,0:T(8,128)S(1)} %get-tuple-element.55), channel_id=1, source_target_pairs={{1,0},{2,1},{3,2},{4,3},{5,4},{6,5},{7,6},{9,8},{10,9},{11,10},{12... | collective-permute-start | bytes 11528 | tf_op jit(solution)/shard_map/ppermute | solution.py:22
  212.1 11.8 %all-to-all-start.1 = ((f32[8,96,128]{2,1,0:T(8,128)}), f32[8,96,128]{2,1,0:T(8,128)S(1)}, u32[]{:S(2)}, u32[]{:S(2)}) async-start(f32[8,96,128]{2,1,0:T(8,128)} %broadcast_in_dim.630), calls=%async_computation.1 | async-start | bytes 786432 | tf_op jit(solution)/shard_map/all_to_all | solution.py:89
  224.7 18.1 %all-to-all-start.2 = ((f32[8,96,128]{2,1,0:T(8,128)}), f32[8,96,128]{2,1,0:T(8,128)S(1)}, u32[]{:S(2)}, u32[]{:S(2)}) async-start(f32[8,96,128]{2,1,0:T(8,128)} %broadcast_in_dim.631), calls=%async_computation.2 | async-start | bytes 786432 | tf_op jit(solution)/shard_map/all_to_all | solution.py:89
  243.5 9.4 %all-to-all-start.3 = ((f32[4,96,128]{2,1,0:T(8,128)}), f32[4,96,128]{2,1,0:T(8,128)S(1)}, u32[]{:S(2)}, u32[]{:S(2)}) async-start(f32[4,96,128]{2,1,0:T(8,128)} %broadcast_in_dim.632), calls=%async_computation.3 | async-start | bytes 393216 | tf_op jit(solution)/shard_map/all_to_all | solution.py:89
  (23 other events, 31.5 us)

commit v2 on v0

v2 whole, which is shorter than its diff:
```python
import jax
import jax.numpy as jnp
from jax import lax
from jax.experimental import pallas as pl
from jax.experimental.pallas import tpu as pltpu
from jax.sharding import PartitionSpec as P

STEPS = 4
CASES = 8
step_squared = 0.1
ramp_steps = 4.0

PAIR = 2
FIELDS = 3 * PAIR
MASKS = 2 * FIELDS
MATERIAL = MASKS + PAIR
COUNT = MATERIAL + 1
EDGE = 2 * COUNT
GRAM = EDGE + 2
REACH = 4
f32 = jnp.float32
bf16 = jnp.bfloat16


def dot(a, b, contract, precision=None):
    return lax.dot_general(
        a, b, ((contract[:1], contract[1:]), ((), ())),
        precision=precision, preferred_element_type=f32,
    )


def lanes_of(shape):
    return lax.broadcasted_iota(jnp.int32, shape, len(shape) - 1)


def rows_of(shape):
    return lax.broadcasted_iota(jnp.int32, shape, len(shape) - 2)


def start_kernel(now, prev, basis, ids, mask, out, down, up, stage):
    modal = jnp.concatenate([now[...].astype(f32), prev[...].astype(f32)], axis=1).T.astype(bf16)
    layers, comps, ny, nz, modes = basis.shape
    slabs = out.shape[0]
    gram = jnp.zeros((modes, modes), f32)
    for x in range(layers):
        for c in range(comps):
            rows = basis[x, c].reshape(ny * nz, modes)
            both = dot(modal, rows, (1, 1))
            at = x * comps + c
            for y in range(ny):
                stage[at, pl.ds(y, 2 * CASES, stride=ny), :] = both[:, y * nz : (y + 1) * nz]
            for r in range(2 * CASES):
                j = r % CASES
                field = (r // CASES) * FIELDS + (j % PAIR) * comps + c
                out[j // PAIR, 2 * field + x] = stage[at, r * ny : (r + 1) * ny, :]
            gram = gram + dot(rows, rows, (0, 0))
    share = modes // slabs
    for p in range(slabs):
        for x in range(layers):
            for i in range(PAIR):
                out[p, 2 * (MASKS + i) + x] = mask[PAIR * p + i, x].astype(f32)
            out[p, 2 * MATERIAL + x] = (ids[x] + 1).astype(f32)
        for t in range(share // 8):
            out[p, GRAM + t] = gram[share * p + 8 * t : share * p + 8 * t + 8]
        quarter = lanes_of((ny, nz)) // REACH
        for t in range(2):
            low = jnp.zeros((ny, nz), f32)
            high = jnp.zeros((ny, nz), f32)
            for g in range(16):
                tile = 16 * t + g
                if tile < 2 * COUNT:
                    v = out[p, tile]
                    low = jnp.where(quarter == 2 * g, pltpu.roll(v, 8 * g, 1) if g else v, low)
                    turn = (8 * g + 8) % nz
                    high = jnp.where(quarter == 2 * g + 1, pltpu.roll(v, turn, 1) if turn else v, high)
            down[p, t] = low
            up[p, t] = high
            out[p, EDGE + t] = jnp.zeros((ny, nz), f32)


def faces_kernel(block, down, up):
    slabs = block.shape[0]
    first = rows_of(block.shape[2:]) < REACH
    for g in range(slabs):
        for q in range(COUNT + 1):
            a = block[g, 2 * q]
            b = pltpu.roll(block[g, 2 * q + 1], REACH, 0)
            down[g, q] = jnp.where(first, a, b)
            up[g, q] = jnp.where(first, b, a)


def steps_kernel(place, drive, moduli, block, above, below, out, share, fields, masks, stiff, weight, couple, diagonal):
    slabs, _, ny, nz = block.shape
    nx = 2 * slabs
    first = rows_of((ny, nz)) < REACH
    lane = lanes_of((ny, nz))
    zero = jnp.zeros((ny, nz), f32)
    wide_zero = jnp.zeros((2 * ny, 2 * nz), f32)
    for g in range(slabs):
        edges = [
            (block[g, EDGE], jnp.where(first, above[g, COUNT], below[g, COUNT])),
            (block[g, EDGE + 1], pltpu.roll(jnp.where(first, below[g, COUNT], above[g, COUNT]), REACH, 0)),
        ]
        for q in range(COUNT):
            beside = (
                jnp.where(first, above[g, q], below[g, q]),
                pltpu.roll(jnp.where(first, below[g, q], above[g, q]), REACH, 0),
            )
            for i in range(2):
                x = 2 * g + i
                spot = 2 * q + i
                ends = []
                for edge in edges[spot // 16]:
                    turn = 8 * (spot % 16)
                    right = pltpu.roll(edge, (nz - turn) % nz, 1) if turn else edge
                    left = pltpu.roll(edge, (2 * nz - 8 - turn) % nz, 1) if (nz - 8 - turn) % nz else edge
                    ends.append(jnp.where(lane < REACH, right, jnp.where(lane >= nz - REACH, left, zero)))
                parts = ((block[g, spot], ends[0]), (beside[i], ends[1]))
                for k in range(2):
                    for h in range(2):
                        here = (slice(k * ny, (k + 1) * ny), slice(h * nz, (h + 1) * nz))
                        value = parts[k][h]
                        if q < FIELDS:
                            fields[0, q, 1 + x, here[0], here[1]] = value
                        elif q < MASKS:
                            fields[1, q - FIELDS, 1 + x, here[0], here[1]] = value
                        elif q < MATERIAL:
                            masks[q - MASKS, x, here[0], here[1]] = value
                        else:
                            for prop in range(3):
                                level = zero
                                for m in range(moduli.shape[1]):
                                    level = jnp.where(value == m + 1.0, moduli[prop, m], level)
                                if prop < 2:
                                    stiff[prop, 1 + x, here[0], here[1]] = level
                                else:
                                    weight[x, here[0], here[1]] = step_squared * level
    for x in (0, nx + 1):
        for f in range(FIELDS):
            fields[0, f, x] = wide_zero
            fields[1, f, x] = wide_zero
        stiff[0, x] = wide_zero
        stiff[1, x] = wide_zero
    for t in range(share.shape[0]):
        total = block[0, GRAM + t]
        for g in range(1, slabs):
            total = total + block[g, GRAM + t]
        share[t] = total

    def beside_of(ref, lead, x):
        v = ref[lead + (x + 1,)]
        return v, (
            ref[lead + (x,)], ref[lead + (x + 2,)],
            pltpu.roll(v, 1, 0), pltpu.roll(v, 2 * ny - 1, 0),
            pltpu.roll(v, 1, 1), pltpu.roll(v, 2 * nz - 1, 1),
        )

    def prepare(x, carry):
        half = 0.5 * weight[x]
        sums = []
        for kind in range(2):
            v, near = beside_of(stiff, (kind,), x)
            pairs = []
            for d in range(6):
                value = half * (v + near[d])
                couple[kind, d, x] = value
                pairs.append(value)
            sums.append([pairs[2 * a] + pairs[2 * a + 1] for a in range(3)])
        for c in range(3):
            total = sums[0][c] + sums[1][(c + 1) % 3] + sums[1][(c + 2) % 3]
            diagonal[c, x] = 2.0 - total
        for i in range(PAIR):
            masks[i, x] = masks[i, x] * weight[x]
        return carry

    lax.fori_loop(0, nx, prepare, 0)
    slab = place[0]
    for s in range(STEPS):
        ramp = min(1.0, (s + 1) / ramp_steps)

        def step(x, carry):
            for i in range(PAIR):
                for c in range(3):
                    f = 3 * i + c
                    v, near = beside_of(fields, (s % 2, f), x)
                    value = diagonal[c, x] * v - fields[1 - s % 2, f, x + 1]
                    value = value + masks[i, x] * (drive[c, PAIR * slab + i] * ramp)
                    for d in range(6):
                        kind = 0 if d // 2 == c else 1
                        value = value + couple[kind, d, x] * near[d]
                    fields[1 - s % 2, f, x + 1] = value
                    out[x // 2, s, f, x % 2] = value[:ny, :nz]
            return carry

        lax.fori_loop(0, nx, step, 0)


def project_kernel(basis, states, share, out, stage):
    layers, comps, ny, nz, modes = basis.shape
    count = STEPS * CASES
    coef = jnp.zeros((count, modes), f32)
    square = jnp.zeros((count, count), f32)
    for x in range(layers):
        for c in range(comps):
            at = x * comps + c
            for s in range(STEPS):
                for j in range(CASES):
                    r = s * CASES + j
                    stage[at, r * ny : (r + 1) * ny, :] = states[j // PAIR, s, (j % PAIR) * comps + c, x]
            block = jnp.concatenate(
                [stage[at, pl.ds(y, count, stride=ny), :].astype(bf16) for y in range(ny)], axis=1
            )
            coef = coef + dot(block, basis[x, c].reshape(ny * nz, modes), (1, 0))
            square = square + dot(block, block, (1, 1))
    lane = lanes_of((CASES, count))
    tile = jnp.zeros((CASES, count), f32)
    for s in range(STEPS):
        tile = jnp.where(lane // CASES == s, square[s * CASES : (s + 1) * CASES], tile)
    tile = jnp.concatenate([tile, jnp.zeros((CASES, modes - count), f32)], axis=1)
    for g in range(out.shape[0]):
        out[g, :count] = coef
        out[g, count : count + CASES] = tile
        for t in range(share.shape[0]):
            out[g, count + CASES + 8 * t : count + CASES + 8 * t + 8] = share[t]


def sum_kernel(parts, out):
    total = parts[0]
    for g in range(1, parts.shape[0]):
        total = total + parts[g]
    for g in range(out.shape[0]):
        out[g] = total


def factor(gram):
    rows = rows_of(gram.shape)
    lane = lanes_of(gram.shape)
    work = jnp.where(lane < CASES, gram, jnp.where(lane == rows + CASES, 1.0, 0.0))
    for p in range(CASES):
        scale = 1.0 / jnp.sqrt(work[p : p + 1, p : p + 1])
        row = work[p : p + 1] * scale
        below = jnp.where(rows[:, :1] > p, work[:, p : p + 1] * scale, 0.0)
        work = jnp.where(rows == p, row, work - below * row)
    upper = jnp.where((rows <= lane) & (lane < CASES), work, 0.0)
    inverse = jnp.where(lane < CASES, pltpu.roll(work, gram.shape[1] - CASES, 1), 0.0)
    return upper, inverse


def mixed(small, rows):
    total = small[:, :1] * rows[:1]
    for i in range(1, CASES):
        total = total + small[:, i : i + 1] * rows[i : i + 1]
    return total


def padded(rows):
    return jnp.concatenate([rows, jnp.zeros((rows.shape[1] - rows.shape[0], rows.shape[1]), f32)])


def finish_kernel(weight, parts, basis, states, displacement, modes_out, coefficients, factors, stage):
    layers, comps, ny, nz, modes = basis.shape
    count = STEPS * CASES
    high = lax.Precision.HIGHEST
    own = parts[0, : count + CASES]
    for g in range(1, parts.shape[0]):
        own = own + parts[g, : count + CASES]
    own = own * weight
    gram = jnp.concatenate([parts[g, count + CASES :] for g in range(parts.shape[0])]) * weight
    coef, square = own[:count], own[count:]
    lane = lanes_of(square.shape)

    def block_of(rows, s):
        turn = (modes - s * CASES) % modes
        rows = pltpu.roll(rows, turn, 1) if turn else rows
        return jnp.where(lane < CASES, rows, 0.0)

    rounded = coef.astype(bf16).astype(f32)
    left = coef - dot(rounded, gram, (1, 0), high)
    change = dot(coef, padded(rounded), (1, 1), high) + dot(rounded, padded(left), (1, 1), high)
    first, second = [], []
    for s in range(STEPS):
        at = slice(s * CASES, (s + 1) * CASES)
        first.append(factor(block_of(square - change[at], s)))
        second.append(mixed(first[s][1], left[at]))
    second = jnp.concatenate(second)
    rounded_2 = second.astype(bf16).astype(f32)
    left_2 = second - dot(rounded_2, gram, (1, 0), high)
    change = dot(second, padded(rounded_2), (1, 1), high) + dot(rounded_2, padded(left_2), (1, 1), high)
    for s in range(STEPS):
        at = slice(s * CASES, (s + 1) * CASES)
        whole = dot(first[s][0], padded(first[s][1]), (1, 1), high)
        upper, inverse = factor(whole - block_of(change[at], s))
        factors[s] = mixed(upper, first[s][0])[:, :CASES]
        coefficients[s, 0] = coef[at].T
        coefficients[s, 1] = second[at].T
    mix = mixed(inverse, first[-1][1])
    shift = mixed(mix, rounded[at]) + mixed(inverse, rounded_2[at])
    pieces = []
    for _ in range(3):
        piece = shift.astype(bf16)
        pieces.append(piece.astype(f32))
        shift = shift - piece.astype(f32)
    pieces = jnp.concatenate(pieces).astype(bf16)
    scalars = [[mix[i : i + 1, j : j + 1] for j in range(CASES)] for i in range(CASES)]
    for x in range(layers):
        for c in range(comps):
            at = x * comps + c
            taken = dot(pieces, basis[x, c].reshape(ny * nz, modes), (1, 1))
            taken = taken[:CASES] + taken[CASES : 2 * CASES] + taken[2 * CASES :]
            for y in range(ny):
                stage[at, pl.ds(y, CASES, stride=ny), :] = taken[:, y * nz : (y + 1) * nz]
            final = [states[j // PAIR, STEPS - 1, (j % PAIR) * comps + c, x] for j in range(CASES)]
            snapshot = [v.astype(bf16).astype(f32) for v in final]
            for i in range(CASES):
                displacement[c, i, x] = final[i]
                total = scalars[i][0] * snapshot[0]
                for j in range(1, CASES):
                    total = total + scalars[i][j] * snapshot[j]
                modes_out[c, i, x] = total - stage[at, i * ny : (i + 1) * ny, :]


def call(kernel, outs, inputs, scratch=(), scalars=0):
    vmem = pl.BlockSpec(memory_space=pltpu.VMEM)
    smem = pl.BlockSpec(memory_space=pltpu.SMEM)
    return pl.pallas_call(
        kernel,
        out_shape=[jax.ShapeDtypeStruct(shape, f32) for shape in outs],
        in_specs=[smem] * scalars + [vmem] * (len(inputs) - scalars),
        out_specs=[vmem] * len(outs),
        scratch_shapes=[pltpu.VMEM(shape, f32) for shape in scratch],
        compiler_params=pltpu.CompilerParams(vmem_limit_bytes=40 << 20),
    )(*inputs)


def sent(block, axis, forward):
    count = lax.axis_size(axis)
    pairs = [(i, i + 1) for i in range(count - 1)]
    return lax.ppermute(block, axis, pairs if forward else [(b, a) for a, b in pairs])


def turned(parts, axis):
    return lax.all_to_all(parts, axis, 0, 0, tiled=True)


def shards(basis, modal_now, modal_prev, material_ids, moduli, drive_mask, drive):
    layers, comps, ny, nz, modes = basis.shape
    slabs, rows, depth = (lax.axis_size(a) for a in ("gx", "gy", "gz"))
    dof_weight = 1.0 / (3.0 * layers * ny * nz * slabs * rows * depth)
    tile = (ny, nz)
    share = modes // slabs // 8
    blocks = layers * comps
    block, down, up = call(
        start_kernel,
        [(slabs, GRAM + share) + tile, (slabs, 2) + tile, (slabs, 2) + tile],
        [modal_now, modal_prev, basis, material_ids, drive_mask],
        [(blocks, 2 * CASES * ny, nz)],
    )
    edge = sent(down, "gz", False) + sent(up, "gz", True)
    block = turned(lax.dynamic_update_slice(block, edge, (0, EDGE, 0, 0)), "gx")
    down, up = call(faces_kernel, [(slabs, COUNT + 1) + tile] * 2, [block])
    above, below = sent(down, "gy", False), sent(up, "gy", True)
    nx = layers * slabs
    wide = (2 * ny, 2 * nz)
    place = lax.axis_index("gx").astype(jnp.int32)[None]
    states, gram = call(
        steps_kernel,
        [(slabs, STEPS, FIELDS, layers) + tile, (share,) + tile],
        [place, drive, moduli, block, above, below],
        [
            (2, FIELDS, nx + 2) + wide, (PAIR, nx) + wide, (2, nx + 2) + wide, (nx,) + wide,
            (2, 6, nx) + wide, (3, nx) + wide,
        ],
        3,
    )
    states = turned(states, "gx")
    count = STEPS * CASES
    width = count + CASES + 8 * share
    parts, = call(
        project_kernel, [(rows, width, modes)], [basis, states, gram], [(blocks, count * ny, nz)]
    )
    parts, = call(sum_kernel, [(depth, width, modes)], [turned(parts, "gy")])
    parts, = call(sum_kernel, [(slabs, width, modes)], [turned(parts, "gz")])
    return call(
        lambda *refs: finish_kernel(dof_weight, *refs),
        [(comps, CASES, layers) + tile] * 2 + [(STEPS, 2, modes, CASES), (STEPS, CASES, CASES)],
        [turned(parts, "gx"), basis, states],
        [(blocks, CASES * ny, nz)],
    )


def solution(mesh):
    in_specs = (
        P("gx", None, "gy", "gz", None),
        P(),
        P(),
        P("gx", "gy", "gz"),
        P(),
        P(None, "gx", "gy", "gz"),
        P(),
    )
    out_specs = (P(None, None, "gx", "gy", "gz"), P(None, None, "gx", "gy", "gz"), P(), P())
    return jax.shard_map(
        lambda *args: tuple(shards(*args)), mesh=mesh, in_specs=in_specs, out_specs=out_specs, check_vma=False
    )
```

time: 540 us -> 106 us (0.20)
  blocking collectives: 295 us -> 66.6 us
  starting transfers between devices: 83.7 us -> 14.2 us
  waiting for transfers between devices: 70.1 us -> 4.29 us
  other arithmetic: 38.1 us -> 0.01 us
  local copies, waits for them, and re-layouts: 27.4 us -> 5.34 us
  matrix products: 22 us -> 0 us
  Pallas kernels: 0 us -> 12.9 us
    psum x4 -> x0, blocking collectives: 295 us -> none  [the longest x1 74.7 us: orthonormalize(): lax.psum(project(basis, first_q.astype(jnp.bfloat16)) * dof_weight, ('gx'...]
    ppermute x30 -> x4, starting transfers between devices: 83.7 us -> 14.2 us  [sent(): lax.ppermute(block, axis, pairs if forward else [(b, a) for a, b in pairs])]
    all_to_all x0 -> x5, blocking collectives: none -> 66.6 us  [turned(): return lax.all_to_all(parts, axis, 0, 0, tiled=True)]
    ppermute x30 -> x4, waiting for transfers between devices: 70.1 us -> 4.29 us  [sent(): lax.ppermute(block, axis, pairs if forward else [(b, a) for a, b in pairs])]
    another operation x52 -> x0, other arithmetic: 23.5 us -> none  [the longest x10 6.42 us: apply_inverse(): jax.scipy.linalg.solve_triangular(lower_factor, identity_block, lower=True)]
    dot_general x36 -> x0, matrix products: 21.1 us -> none  [the longest x4 5.97 us: orthonormalize(): factor = jnp.dot(first_lower, second_lower, precision=highest).T]
    pallas_call x0 -> x7, Pallas kernels: none -> 12.9 us  [call(): pl.pallas_call(kernel, out_shape=[jax.ShapeDtypeStruct(shape, f32) for sh...]
    concatenate x11 -> x0, other arithmetic: 12.1 us -> none  [the longest x10 12.1 us: padded_2(): block = jnp.concatenate([low, block, high], axis=dim)]
  transfers between devices with their start and end apart: 30 -> 4, of which waited for: 19 -> 3; matrix products, arithmetic and copies ran while one was open for 3% -> 0% of each run, Pallas kernels for 0% -> 0%
where the time goes in v2:
time: 106 us; the launch traced here: 104 us
  blocking collectives  66.6 us (63%)
  starting transfers between devices  14.2 us (13%)
  Pallas kernels  12.9 us (12%)
  local copies, waits for them, and re-layouts  5.34 us (5%)
  waiting for transfers between devices  4.29 us (4%)
    all_to_all x5, blocking collectives, turned(): return lax.all_to_all(parts, axis, 0, 0, tiled=True)  66.6 us
    ppermute x4, starting transfers between devices, sent(): lax.ppermute(block, axis, pairs if forward else [(b, a) for a, b in pairs])  14.2 us
    pallas_call x7, Pallas kernels, call(): pl.pallas_call(kernel, out_shape=[jax.ShapeDtypeStruct(shape, f32) for sh...  12.9 us
    unnamed x14, local copies, waits for them, and re-layouts  4.55 us
    ppermute x4, waiting for transfers between devices, sent(): lax.ppermute(block, axis, pairs if forward else [(b, a) for a, b in pairs])  4.29 us
  transfers between devices with their start and end apart: 4, of which 3 were waited for; matrix products, arithmetic and copies ran while one was open for 0% of the time, Pallas kernels for 0%

profile of v2, /device:TPU:1, one launch (start us, length us, event | category | flops | bytes accessed | tf_op | source)
XLA Modules:
  0.0 104.1 jit_solution(5193418209619584465)
XLA Ops:
  0.6 0.8 copy.11.now
  1.4 0.8 copy.12.prev
  2.2 0.0 copy-start
  2.2 1.4 %copy-done = bf16[2,3,8,128,128]{4,3,2,1,0:T(8,128)(2,1)S(1)} copy-done((bf16[2,3,8,128,128]{4,3,2,1,0:T(8,128)(2,1)S(1)}, bf16[2,3,8,128,128]{4,3,2,1,0:T(8,128)(2,1)}, u32[]{:S(2)}) %copy-start) | copy-done | bytes 1572888
  3.6 0.0 copy-start.2
  3.6 0.8 copy-done.2
  4.5 0.0 copy-start.3
  4.5 0.7 copy-done.3
  5.2 0.0 copy-start.4
  5.2 0.0 copy-start.5
  5.2 1.2 %shard_map.102 = (f32[4,36,8,128]{3,2,1,0:T(8,128)S(1)}, f32[4,2,8,128]{3,2,1,0:T(8,128)S(1)}, f32[4,2,8,128]{3,2,1,0:T(8,128)S(1)}) custom-call(bf16[128,8]{1,0:T(8,128)(2,1)S(1)} %copy.11.now, bf16[128,8]{1,0:T(8,128)(2,1)S(1)} %copy.12.prev, bf16[2,3,8,128,128]{4,3,2,1,0:T(8,128)(2,1)S(1)} %copy-done, s32[2,8,128]{2,1,0:T(8,128)S(1)} %copy-done.3, ...), custom_call_target="tpu_custom_call" | custom-call | tf_op jit(solution)/shard_map/pallas_call | solution.py:325
  6.4 1.3 %collective-permute-start = (f32[4,2,8,128]{3,2,1,0:T(8,128)S(1)}, f32[4,2,8,128]{3,2,1,0:T(8,128)S(1)}, u32[]{:S(2)}, u32[]{:S(2)}) collective-permute-start(f32[4,2,8,128]{3,2,1,0:T(8,128)S(1)} %get-tuple-element.12), channel_id=1, source_target_pairs={{1,0},{2,1},{3,2},{4,3},{5,4},{6,5},{7,6},{9,8},{10,9},{11,10},{12... | collective-permute-start | bytes 98312 | tf_op jit(solution)/shard_map/ppermute | solution.py:338
  7.7 5.0 %collective-permute-start.1 = (f32[4,2,8,128]{3,2,1,0:T(8,128)S(1)}, f32[4,2,8,128]{3,2,1,0:T(8,128)S(1)}, u32[]{:S(2)}, u32[]{:S(2)}) collective-permute-start(f32[4,2,8,128]{3,2,1,0:T(8,128)S(1)} %get-tuple-element.13), channel_id=1, source_target_pairs={{0,1},{1,2},{2,3},{3,4},{4,5},{5,6},{6,7},{8,9},{9,10},{10,11},{11... | collective-permute-start | bytes 98312 | tf_op jit(solution)/shard_map/ppermute | solution.py:338
  12.7 0.0 collective-permute-done
  12.7 1.0 collective-permute-done.1
  13.7 12.2 %all_to_all.25.block = f32[4,36,8,128]{3,2,1,0:T(8,128)S(1)} all-to-all(f32[4,36,8,128]{3,2,1,0:T(8,128)S(1)} %add_dynamic-update-slice_fusion), channel_id=1, replica_groups=mesh['gx'=4,'gy'=8,'gz'=8] {'gx'}, dimensions={0} | all-to-all | bytes 1179648 | tf_op jit(solution)/shard_map/all_to_all | solution.py:342
  25.9 0.0 copy-start.1
  25.9 4.9 %collective-permute-start.2 = (f32[4,16,8,128]{3,2,1,0:T(8,128)S(1)}, f32[4,16,8,128]{3,2,1,0:T(8,128)S(1)}, u32[]{:S(2)}, u32[]{:S(2)}) collective-permute-start(f32[4,16,8,128]{3,2,1,0:T(8,128)S(1)} %get-tuple-element.14), channel_id=1, source_target_pairs={{8,0},{16,8},{24,16},{32,24},{40,32},{48,40},{56,48},{9,1},{17,9},... | collective-permute-start | bytes 786440 | tf_op jit(solution)/shard_map/ppermute | solution.py:338
  30.9 3.0 %collective-permute-start.3 = (f32[4,16,8,128]{3,2,1,0:T(8,128)S(1)}, f32[4,16,8,128]{3,2,1,0:T(8,128)S(1)}, u32[]{:S(2)}, u32[]{:S(2)}) collective-permute-start(f32[4,16,8,128]{3,2,1,0:T(8,128)S(1)} %get-tuple-element.15), channel_id=1, source_target_pairs={{0,8},{8,16},{16,24},{24,32},{32,40},{40,48},{48,56},{1,9},{9,17},... | collective-permute-start | bytes 786440 | tf_op jit(solution)/shard_map/ppermute | solution.py:338
  33.9 2.1 %collective-permute-done.2.above = f32[4,16,8,128]{3,2,1,0:T(8,128)S(1)} collective-permute-done((f32[4,16,8,128]{3,2,1,0:T(8,128)S(1)}, f32[4,16,8,128]{3,2,1,0:T(8,128)S(1)}, u32[]{:S(2)}, u32[]{:S(2)}) %collective-permute-start.2) | collective-permute-done | bytes 262176 | tf_op jit(solution)/shard_map/ppermute | solution.py:338
  36.0 1.2 %collective-permute-done.3.below = f32[4,16,8,128]{3,2,1,0:T(8,128)S(1)} collective-permute-done((f32[4,16,8,128]{3,2,1,0:T(8,128)S(1)}, f32[4,16,8,128]{3,2,1,0:T(8,128)S(1)}, u32[]{:S(2)}, u32[]{:S(2)}) %collective-permute-start.3) | collective-permute-done | bytes 262176 | tf_op jit(solution)/shard_map/ppermute | solution.py:338
  37.2 0.0 copy-done.4
  37.2 0.0 copy-done.5
  37.2 5.7 %shard_map.104 = (f32[4,4,6,2,8,128]{5,4,3,2,1,0:T(8,128)S(1)}, f32[4,8,128]{2,1,0:T(8,128)S(1)}) custom-call(s32[1]{0:T(128)} %bitcast.place, f32[3,8]{1,0:T(4,128)S(1)} %copy-done.4, f32[3,4]{1,0:T(4,128)S(1)} %copy-done.5, f32[4,36,8,128]{3,2,1,0:T(8,128)S(1)} %all_to_all.25.block, f32[4,16,8,128]{3,2,1,0:T(8,128)S(1)} %collective-permute-done.2.above, ...), custom_call_target="tpu_custom_call" | custom-call | tf_op jit(solution)/shard_map/pallas_call | solution.py:325
  42.9 12.7 %all_to_all.26.states.refs_2_ = f32[4,4,6,2,8,128]{5,4,3,2,1,0:T(8,128)S(1)} all-to-all(f32[4,4,6,2,8,128]{5,4,3,2,1,0:T(8,128)S(1)} %get-tuple-element.16), channel_id=1, replica_groups=mesh['gx'=4,'gy'=8,'gz'=8] {'gx'}, dimensions={0} | all-to-all | bytes 1572864 | tf_op jit(solution)/shard_map/all_to_all | solution.py:342
  55.5 0.0 copy-done.1
  55.5 0.5 shard_map.105
  56.0 14.1 %all_to_all.27.parts = f32[8,72,128]{2,1,0:T(8,128)S(1)} all-to-all(f32[8,72,128]{2,1,0:T(8,128)S(1)} %shard_map.105), channel_id=1, replica_groups=mesh['gx'=4,'gy'=8,'gz'=8] {'gy'}, dimensions={0} | all-to-all | bytes 589824 | tf_op jit(solution)/shard_map/all_to_all | solution.py:342
  70.2 20.4 %all_to_all.28.parts = f32[8,72,128]{2,1,0:T(8,128)S(1)} all-to-all(f32[8,72,128]{2,1,0:T(8,128)S(1)} %shard_map.106), channel_id=1, replica_groups=mesh['gx'=4,'gy'=8,'gz'=8] {'gz'}, dimensions={0} | all-to-all | bytes 589824 | tf_op jit(solution)/shard_map/all_to_all | solution.py:342
  90.6 7.3 %all_to_all.29.refs_0_ = f32[4,72,128]{2,1,0:T(8,128)S(1)} all-to-all(f32[4,72,128]{2,1,0:T(8,128)S(1)} %shard_map.107), channel_id=1, replica_groups=mesh['gx'=4,'gy'=8,'gz'=8] {'gx'}, dimensions={0} | all-to-all | bytes 294912 | tf_op jit(solution)/shard_map/all_to_all | solution.py:342
  97.8 5.5 %shard_map.108 = (f32[3,8,2,8,128]{4,3,2,1,0:T(8,128)}, f32[3,8,2,8,128]{4,3,2,1,0:T(8,128)}, f32[4,2,128,8]{3,2,1,0:T(8,128)S(1)}, f32[4,8,8]{2,1,0:T(8,128)}) custom-call(f32[4,72,128]{2,1,0:T(8,128)S(1)} %all_to_all.29.refs_0_, bf16[2,3,8,128,128]{4,3,2,1,0:T(8,128)(2,1)S(1)} %copy-done.1, f32[4,4,6,2,8,128]{5,4,3,2,1,0:T(8,128)S(1)} %all_to_all.26.states.refs_2_), custom_call_target="tpu_custom_call" | custom-call | tf_op jit(solution)/shard_map/pallas_call | solution.py:325
  103.3 0.8 copy.13
  (4 shorter events, 0.1 us)
Async XLA Ops:
  2.2 1.4 %copy-start = (bf16[2,3,8,128,128]{4,3,2,1,0:T(8,128)(2,1)S(1)}, bf16[2,3,8,128,128]{4,3,2,1,0:T(8,128)(2,1)}, u32[]{:S(2)}) copy-start(bf16[2,3,8,128,128]{4,3,2,1,0:T(8,128)(2,1)} %refs_1_.1) | copy-start | bytes 4718596
  3.6 0.8 copy-start.2
  4.5 0.7 copy-start.3
  5.2 32.0 %copy-start.4 = (f32[3,8]{1,0:T(4,128)S(1)}, f32[3,8]{1,0:T(4,128)}, u32[]{:S(2)}) copy-start(f32[3,8]{1,0:T(4,128)} %drive.1) | copy-start | bytes 292
  5.2 32.0 %copy-start.5 = (f32[3,4]{1,0:T(4,128)S(1)}, f32[3,4]{1,0:T(4,128)}, u32[]{:S(2)}) copy-start(f32[3,4]{1,0:T(4,128)} %moduli.1) | copy-start | bytes 148
  6.4 6.3 %collective-permute-start = (f32[4,2,8,128]{3,2,1,0:T(8,128)S(1)}, f32[4,2,8,128]{3,2,1,0:T(8,128)S(1)}, u32[]{:S(2)}, u32[]{:S(2)}) collective-permute-start(f32[4,2,8,128]{3,2,1,0:T(8,128)S(1)} %get-tuple-element.12), channel_id=1, source_target_pairs={{1,0},{2,1},{3,2},{4,3},{5,4},{6,5},{7,6},{9,8},{10,9},{11,10},{12... | collective-permute-start | bytes 98312 | tf_op jit(solution)/shard_map/ppermute | solution.py:338
  7.7 6.0 %collective-permute-start.1 = (f32[4,2,8,128]{3,2,1,0:T(8,128)S(1)}, f32[4,2,8,128]{3,2,1,0:T(8,128)S(1)}, u32[]{:S(2)}, u32[]{:S(2)}) collective-permute-start(f32[4,2,8,128]{3,2,1,0:T(8,128)S(1)} %get-tuple-element.13), channel_id=1, source_target_pairs={{0,1},{1,2},{2,3},{3,4},{4,5},{5,6},{6,7},{8,9},{9,10},{10,11},{11... | collective-permute-start | bytes 98312 | tf_op jit(solution)/shard_map/ppermute | solution.py:338
  25.9 29.6 %copy-start.1 = (bf16[2,3,8,128,128]{4,3,2,1,0:T(8,128)(2,1)S(1)}, bf16[2,3,8,128,128]{4,3,2,1,0:T(8,128)(2,1)}, u32[]{:S(2)}) copy-start(bf16[2,3,8,128,128]{4,3,2,1,0:T(8,128)(2,1)} %refs_1_.1) | copy-start | bytes 4718596
  25.9 10.1 %collective-permute-start.2 = (f32[4,16,8,128]{3,2,1,0:T(8,128)S(1)}, f32[4,16,8,128]{3,2,1,0:T(8,128)S(1)}, u32[]{:S(2)}, u32[]{:S(2)}) collective-permute-start(f32[4,16,8,128]{3,2,1,0:T(8,128)S(1)} %get-tuple-element.14), channel_id=1, source_target_pairs={{8,0},{16,8},{24,16},{32,24},{40,32},{48,40},{56,48},{9,1},{17,9},... | collective-permute-start | bytes 786440 | tf_op jit(solution)/shard_map/ppermute | solution.py:338
  30.9 6.3 %collective-permute-start.3 = (f32[4,16,8,128]{3,2,1,0:T(8,128)S(1)}, f32[4,16,8,128]{3,2,1,0:T(8,128)S(1)}, u32[]{:S(2)}, u32[]{:S(2)}) collective-permute-start(f32[4,16,8,128]{3,2,1,0:T(8,128)S(1)} %get-tuple-element.15), channel_id=1, source_target_pairs={{0,8},{8,16},{16,24},{24,32},{32,40},{40,48},{48,56},{1,9},{9,17},... | collective-permute-start | bytes 786440 | tf_op jit(solution)/shard_map/ppermute | solution.py:338

commit v3 on v2

--- a/solution.py
+++ b/solution.py
@@ -37,16 +37,25 @@
     return lax.broadcasted_iota(jnp.int32, shape, len(shape) - 2)
 
 
-def start_kernel(now, prev, basis, ids, mask, out, down, up, stage):
-    modal = jnp.concatenate([now[...].astype(f32), prev[...].astype(f32)], axis=1).T.astype(bf16)
+def start_kernel(now, prev, basis, ids, mask, out, down, up, local, now_in, prev_in, basis_in, ids_in, mask_in, stage, sems):
     layers, comps, ny, nz, modes = basis.shape
     slabs = out.shape[0]
+    moved = [(now, now_in), (prev, prev_in)]
+    moved += [(basis.at[x, c], basis_in.at[x, c]) for x in range(layers) for c in range(comps)]
+    moved += [(ids, ids_in), (mask, mask_in)]
+    moved = [pltpu.make_async_copy(*pair, sems.at[k]) for k, pair in enumerate(moved)]
+    for copy in moved:
+        copy.start()
+    moved[0].wait()
+    moved[1].wait()
+    modal = jnp.concatenate([now_in[...].astype(f32), prev_in[...].astype(f32)]).astype(bf16)
     gram = jnp.zeros((modes, modes), f32)
     for x in range(layers):
         for c in range(comps):
-            rows = basis[x, c].reshape(ny * nz, modes)
+            at = x * comps + c
+            moved[2 + at].wait()
+            rows = basis_in[x, c].reshape(ny * nz, modes)
             both = dot(modal, rows, (1, 1))
-            at = x * comps + c
             for y in range(ny):
                 stage[at, pl.ds(y, 2 * CASES, stride=ny), :] = both[:, y * nz : (y + 1) * nz]
             for r in range(2 * CASES):
@@ -54,14 +63,23 @@
                 field = (r // CASES) * FIELDS + (j % PAIR) * comps + c
                 out[j // PAIR, 2 * field + x] = stage[at, r * ny : (r + 1) * ny, :]
             gram = gram + dot(rows, rows, (0, 0))
-    share = modes // slabs
+    moved[-2].wait()
+    moved[-1].wait()
+    half = modes // 2
+    share = half // slabs
+    lane = lanes_of((half, modes))
+    packed = jnp.where((lane < half) & (lane <= rows_of((half, modes))), pltpu.roll(gram[half:], half, 1), gram[:half])
+    own = jnp.sum(jnp.where(rows_of(gram.shape) == lanes_of(gram.shape), gram, 0.0), axis=0, keepdims=True)
+    local[...] = jnp.zeros(local.shape, f32)
+    local[0:1] = pltpu.roll(own, half, 1)
+    local[1:2] = own
     for p in range(slabs):
         for x in range(layers):
             for i in range(PAIR):
-                out[p, 2 * (MASKS + i) + x] = mask[PAIR * p + i, x].astype(f32)
-            out[p, 2 * MATERIAL + x] = (ids[x] + 1).astype(f32)
+                out[p, 2 * (MASKS + i) + x] = mask_in[PAIR * p + i, x].astype(f32)
+            out[p, 2 * MATERIAL + x] = (ids_in[x] + 1).astype(f32)
         for t in range(share // 8):
-            out[p, GRAM + t] = gram[share * p + 8 * t : share * p + 8 * t + 8]
+            out[p, GRAM + t] = packed[share * p + 8 * t : share * p + 8 * t + 8]
         quarter = lanes_of((ny, nz)) // REACH
         for t in range(2):
             low = jnp.zeros((ny, nz), f32)
@@ -177,25 +195,31 @@
     slab = place[0]
     for s in range(STEPS):
         ramp = min(1.0, (s + 1) / ramp_steps)
+        last = s == STEPS - 1
+        own = (slice(0, ny), slice(0, nz)) if last else (slice(None), slice(None))
 
         def step(x, carry):
             for i in range(PAIR):
                 for c in range(3):
                     f = 3 * i + c
-                    v, near = beside_of(fields, (s % 2, f), x)
-                    value = diagonal[c, x] * v - fields[1 - s % 2, f, x + 1]
-                    value = value + masks[i, x] * (drive[c, PAIR * slab + i] * ramp)
+                    now, to = fields.at[s % 2, f], fields.at[1 - s % 2, f]
+                    v, near = beside_of(now, (), x)
+                    if last:
+                        v, near = v[own], [n[own] for n in near]
+                    value = diagonal[(c, x) + own] * v - to[(x + 1,) + own]
+                    value = value + masks[(i, x) + own] * (drive[c, PAIR * slab + i] * ramp)
                     for d in range(6):
                         kind = 0 if d // 2 == c else 1
-                        value = value + couple[kind, d, x] * near[d]
-                    fields[1 - s % 2, f, x + 1] = value
+                        value = value + couple[(kind, d, x) + own] * near[d]
+                    if not last:
+                        to[x + 1] = value
                     out[x // 2, s, f, x % 2] = value[:ny, :nz]
             return carry
 
         lax.fori_loop(0, nx, step, 0)
 
 
-def project_kernel(basis, states, share, out, stage):
+def project_kernel(basis, states, share, local, out, stage):
     layers, comps, ny, nz, modes = basis.shape
     count = STEPS * CASES
     coef = jnp.zeros((count, modes), f32)
@@ -217,6 +241,7 @@
     for s in range(STEPS):
         tile = jnp.where(lane // CASES == s, square[s * CASES : (s + 1) * CASES], tile)
     tile = jnp.concatenate([tile, jnp.zeros((CASES, modes - count), f32)], axis=1)
+    tile = jnp.where(lanes_of(tile.shape) < modes // 2, tile, local[...])
     for g in range(out.shape[0]):
         out[g, :count] = coef
         out[g, count : count + CASES] = tile
@@ -236,11 +261,11 @@
     rows = rows_of(gram.shape)
     lane = lanes_of(gram.shape)
     work = jnp.where(lane < CASES, gram, jnp.where(lane == rows + CASES, 1.0, 0.0))
-    for p in range(CASES):
-        scale = 1.0 / jnp.sqrt(work[p : p + 1, p : p + 1])
-        row = work[p : p + 1] * scale
-        below = jnp.where(rows[:, :1] > p, work[:, p : p + 1] * scale, 0.0)
-        work = jnp.where(rows == p, row, work - below * row)
+    for p in range(CASES - 1):
+        ratio = work[:, p : p + 1] * (1.0 / work[p : p + 1, p : p + 1])
+        work = work - jnp.where(rows > p, ratio, 0.0) * work[p : p + 1]
+    pivots = jnp.sum(jnp.where(lane == rows, work, 0.0), axis=1, keepdims=True)
+    work = work * (1.0 / jnp.sqrt(pivots))
     upper = jnp.where((rows <= lane) & (lane < CASES), work, 0.0)
     inverse = jnp.where(lane < CASES, pltpu.roll(work, gram.shape[1] - CASES, 1), 0.0)
     return upper, inverse
@@ -257,16 +282,47 @@
     return jnp.concatenate([rows, jnp.zeros((rows.shape[1] - rows.shape[0], rows.shape[1]), f32)])
 
 
-def finish_kernel(weight, parts, basis, states, displacement, modes_out, coefficients, factors, stage):
+def pieces_of(value):
+    pieces = []
+    for _ in range(3):
+        piece = value.astype(bf16)
+        pieces.append(piece)
+        value = value - piece.astype(f32)
+    return pieces
+
+
+def exact(rounded, pieces, contract):
+    total = dot(rounded, pieces[2], contract)
+    return total + dot(rounded, pieces[1], contract) + dot(rounded, pieces[0], contract)
+
+
+def finish_kernel(weight, parts, basis, states, displacement, modes_out, coefficients, factors, stage, held, sems):
     layers, comps, ny, nz, modes = basis.shape
+    moved = []
+    for c in range(comps):
+        for j in range(CASES):
+            moved.append(pltpu.make_async_copy(
+                states.at[j // PAIR, STEPS - 1, (j % PAIR) * comps + c], displacement.at[c, j], sems.at[len(moved)]
+            ))
+            moved[-1].start()
     count = STEPS * CASES
+    half = modes // 2
     high = lax.Precision.HIGHEST
     own = parts[0, : count + CASES]
     for g in range(1, parts.shape[0]):
         own = own + parts[g, : count + CASES]
     own = own * weight
-    gram = jnp.concatenate([parts[g, count + CASES :] for g in range(parts.shape[0])]) * weight
     coef, square = own[:count], own[count:]
+    packed = jnp.concatenate([parts[g, count + CASES :] for g in range(parts.shape[0])]) * weight
+    lane, row = lanes_of(packed.shape), rows_of(packed.shape)
+    flipped = padded(packed).T
+    diagonal = jnp.where(lane[:1] < half, pltpu.roll(square[:1], half, 1), square[1:2])
+    top = jnp.where(lane < row, flipped[:half], packed)
+    top = jnp.where(lane == row, diagonal, top)
+    bottom = jnp.where(lane - half <= row, pltpu.roll(packed, half, 1), pltpu.roll(flipped[:half], half, 1))
+    bottom = jnp.where(lane < half, flipped[half:], bottom)
+    bottom = jnp.where(lane - half == row, diagonal, bottom)
+    gram = pieces_of(jnp.concatenate([top, bottom]))
     lane = lanes_of(square.shape)
 
     def block_of(rows, s):
@@ -274,61 +330,67 @@
         rows = pltpu.roll(rows, turn, 1) if turn else rows
         return jnp.where(lane < CASES, rows, 0.0)
 
-    rounded = coef.astype(bf16).astype(f32)
-    left = coef - dot(rounded, gram, (1, 0), high)
-    change = dot(coef, padded(rounded), (1, 1), high) + dot(rounded, padded(left), (1, 1), high)
+    def change_of(coef):
+        rounded = coef.astype(bf16)
+        left = coef - exact(rounded, gram, (1, 0))
+        wide = padded(rounded.astype(f32)).astype(bf16)
+        change = exact(rounded, pieces_of(padded(left)), (1, 1))
+        for piece in pieces_of(coef)[::-1]:
+            change = change + dot(piece, wide, (1, 1))
+        return rounded.astype(f32), left, change
+
+    rounded, left, change = change_of(coef)
     first, second = [], []
     for s in range(STEPS):
         at = slice(s * CASES, (s + 1) * CASES)
         first.append(factor(block_of(square - change[at], s)))
         second.append(mixed(first[s][1], left[at]))
     second = jnp.concatenate(second)
-    rounded_2 = second.astype(bf16).astype(f32)
-    left_2 = second - dot(rounded_2, gram, (1, 0), high)
-    change = dot(second, padded(rounded_2), (1, 1), high) + dot(rounded_2, padded(left_2), (1, 1), high)
+    rounded_2, left_2, change = change_of(second)
     for s in range(STEPS):
         at = slice(s * CASES, (s + 1) * CASES)
         whole = dot(first[s][0], padded(first[s][1]), (1, 1), high)
         upper, inverse = factor(whole - block_of(change[at], s))
         factors[s] = mixed(upper, first[s][0])[:, :CASES]
-        coefficients[s, 0] = coef[at].T
-        coefficients[s, 1] = second[at].T
+        coefficients[s, 0] = coef[at]
+        coefficients[s, 1] = second[at]
     mix = mixed(inverse, first[-1][1])
     shift = mixed(mix, rounded[at]) + mixed(inverse, rounded_2[at])
-    pieces = []
-    for _ in range(3):
-        piece = shift.astype(bf16)
-        pieces.append(piece.astype(f32))
-        shift = shift - piece.astype(f32)
-    pieces = jnp.concatenate(pieces).astype(bf16)
+    pieces = jnp.concatenate([piece.astype(f32) for piece in pieces_of(shift)]).astype(bf16)
     scalars = [[mix[i : i + 1, j : j + 1] for j in range(CASES)] for i in range(CASES)]
-    for x in range(layers):
-        for c in range(comps):
+    for c in range(comps):
+        for x in range(layers):
             at = x * comps + c
             taken = dot(pieces, basis[x, c].reshape(ny * nz, modes), (1, 1))
             taken = taken[:CASES] + taken[CASES : 2 * CASES] + taken[2 * CASES :]
             for y in range(ny):
                 stage[at, pl.ds(y, CASES, stride=ny), :] = taken[:, y * nz : (y + 1) * nz]
-            final = [states[j // PAIR, STEPS - 1, (j % PAIR) * comps + c, x] for j in range(CASES)]
-            snapshot = [v.astype(bf16).astype(f32) for v in final]
+            snapshot = [
+                states[j // PAIR, STEPS - 1, (j % PAIR) * comps + c, x].astype(bf16).astype(f32) for j in range(CASES)
+            ]
             for i in range(CASES):
-                displacement[c, i, x] = final[i]
                 total = scalars[i][0] * snapshot[0]
                 for j in range(1, CASES):
                     total = total + scalars[i][j] * snapshot[j]
-                modes_out[c, i, x] = total - stage[at, i * ny : (i + 1) * ny, :]
-
-
-def call(kernel, outs, inputs, scratch=(), scalars=0):
+                held[c, i, x] = total - stage[at, i * ny : (i + 1) * ny, :]
+        moved.append(pltpu.make_async_copy(held.at[c], modes_out.at[c], sems.at[len(moved)]))
+        moved[-1].start()
+    for copy in moved:
+        copy.wait()
+
+
+def call(kernel, outs, inputs, scratch=(), scalars=0, copies=0, ins_away=0, outs_away=0, room=40):
     vmem = pl.BlockSpec(memory_space=pltpu.VMEM)
     smem = pl.BlockSpec(memory_space=pltpu.SMEM)
+    away = pl.BlockSpec(memory_space=pltpu.HBM)
+    scratch = [pltpu.VMEM(shape, f32) if isinstance(shape, tuple) else shape for shape in scratch]
     return pl.pallas_call(
         kernel,
         out_shape=[jax.ShapeDtypeStruct(shape, f32) for shape in outs],
-        in_specs=[smem] * scalars + [vmem] * (len(inputs) - scalars),
-        out_specs=[vmem] * len(outs),
-        scratch_shapes=[pltpu.VMEM(shape, f32) for shape in scratch],
-        compiler_params=pltpu.CompilerParams(vmem_limit_bytes=40 << 20),
+        in_specs=[smem] * scalars + [away] * ins_away + [vmem] * (len(inputs) - scalars - ins_away),
+        out_specs=[away] * outs_away + [vmem] * (len(outs) - outs_away),
+        scratch_shapes=scratch + ([pltpu.SemaphoreType.DMA((copies,))] if copies else []),
+        compiler_params=pltpu.CompilerParams(vmem_limit_bytes=room << 20),
     )(*inputs)
 
 
@@ -347,13 +409,16 @@
     slabs, rows, depth = (lax.axis_size(a) for a in ("gx", "gy", "gz"))
     dof_weight = 1.0 / (3.0 * layers * ny * nz * slabs * rows * depth)
     tile = (ny, nz)
-    share = modes // slabs // 8
+    share = modes // 2 // slabs // 8
     blocks = layers * comps
-    block, down, up = call(
+    inputs = [pltpu.with_memory_space_constraint(a, pltpu.HBM) for a in (modal_now.T, modal_prev.T, basis, material_ids, drive_mask)]
+    block, down, up, local = call(
         start_kernel,
-        [(slabs, GRAM + share) + tile, (slabs, 2) + tile, (slabs, 2) + tile],
-        [modal_now, modal_prev, basis, material_ids, drive_mask],
-        [(blocks, 2 * CASES * ny, nz)],
+        [(slabs, GRAM + share) + tile, (slabs, 2) + tile, (slabs, 2) + tile, (CASES, modes)],
+        inputs,
+        [pltpu.VMEM(a.shape, a.dtype) for a in inputs] + [(blocks, 2 * CASES * ny, nz)],
+        copies=blocks + 4,
+        ins_away=5,
     )
     edge = sent(down, "gz", False) + sent(up, "gz", True)
     block = turned(lax.dynamic_update_slice(block, edge, (0, EDGE, 0, 0)), "gx")
@@ -376,16 +441,20 @@
     count = STEPS * CASES
     width = count + CASES + 8 * share
     parts, = call(
-        project_kernel, [(rows, width, modes)], [basis, states, gram], [(blocks, count * ny, nz)]
+        project_kernel, [(rows, width, modes)], [basis, states, gram, local], [(blocks, count * ny, nz)]
     )
     parts, = call(sum_kernel, [(depth, width, modes)], [turned(parts, "gy")])
     parts, = call(sum_kernel, [(slabs, width, modes)], [turned(parts, "gz")])
-    return call(
+    held = (comps, CASES, layers) + tile
+    displacement, modes_out, coefficients, factors = call(
         lambda *refs: finish_kernel(dof_weight, *refs),
-        [(comps, CASES, layers) + tile] * 2 + [(STEPS, 2, modes, CASES), (STEPS, CASES, CASES)],
+        [held, held, (STEPS, 2, CASES, modes), (STEPS, CASES, CASES)],
         [turned(parts, "gx"), basis, states],
-        [(blocks, CASES * ny, nz)],
-    )
+        [(blocks, CASES * ny, nz), held],
+        copies=comps * CASES + comps,
+        outs_away=2,
+    )
+    return displacement, modes_out, coefficients.transpose(0, 1, 3, 2), factors
 
 
 def solution(mesh):
@@ -400,5 +469,5 @@
     )
     out_specs = (P(None, None, "gx", "gy", "gz"), P(None, None, "gx", "gy", "gz"), P(), P())
     return jax.shard_map(
-        lambda *args: tuple(shards(*args)), mesh=mesh, in_specs=in_specs, out_specs=out_specs, check_vma=False
-    )
+        shards, mesh=mesh, in_specs=in_specs, out_specs=out_specs, check_vma=False
+    )

time: 106 us -> 99.1 us (0.935)
  local copies, waits for them, and re-layouts: 5.34 us -> 0.01 us
  blocking collectives: 66.6 us -> 63.4 us
  Pallas kernels: 12.9 us -> 14.7 us
    unnamed x14 -> x6, local copies, waits for them, and re-layouts: 4.55 us -> 0.01 us
    all_to_all x5, blocking collectives: 66.6 us -> 63.4 us  [turned(): return lax.all_to_all(parts, axis, 0, 0, tiled=True)]
    pallas_call x7, Pallas kernels: 12.9 us -> 14.7 us  [call(): pl.pallas_call(kernel, out_shape=[jax.ShapeDtypeStruct(shape, f32) for sh...]
where the time goes in v3:
time: 99.1 us; the launch traced here: 97.3 us
  blocking collectives  63.4 us (64%)
  Pallas kernels  14.7 us (15%)
  starting transfers between devices  14.2 us (14%)
  waiting for transfers between devices  4.29 us (4%)
    all_to_all x5, blocking collectives, turned(): return lax.all_to_all(parts, axis, 0, 0, tiled=True)  63.4 us
    pallas_call x7, Pallas kernels, call(): pl.pallas_call(kernel, out_shape=[jax.ShapeDtypeStruct(shape, f32) for sh...  14.7 us
    ppermute x4, starting transfers between devices, sent(): lax.ppermute(block, axis, pairs if forward else [(b, a) for a, b in pairs])  14.2 us
    ppermute x4, waiting for transfers between devices, sent(): lax.ppermute(block, axis, pairs if forward else [(b, a) for a, b in pairs])  4.29 us
  transfers between devices with their start and end apart: 4, of which 3 were waited for; matrix products, arithmetic and copies ran while one was open for 0% of the time, Pallas kernels for 0%

profile of v3, /device:TPU:1, one launch (start us, length us, event | category | flops | bytes accessed | tf_op | source)
XLA Modules:
  0.0 97.3 jit_solution(2108716935630790183)
XLA Ops:
  0.6 0.0 copy-start.1
  0.6 0.0 copy-start.2
  0.7 3.1 %shard_map.102 = (f32[4,34,8,128]{3,2,1,0:T(8,128)S(1)}, f32[4,2,8,128]{3,2,1,0:T(8,128)S(1)}, f32[4,2,8,128]{3,2,1,0:T(8,128)S(1)}, f32[8,128]{1,0:T(8,128)S(1)}) custom-call(bf16[8,128]{1,0:T(8,128)(2,1)} %bitcast.4, bf16[8,128]{1,0:T(8,128)(2,1)} %bitcast.5, bf16[2,3,8,128,128]{4,3,2,1,0:T(8,128)(2,1)} %refs_1_.1, s32[2,8,128]{2,1,0:T(8,128)} %ids.1, ...), custom_call_target="tpu_custom_call" | custom-call | tf_op jit(solution)/shard_map/pallas_call | solution.py:387
  3.8 1.3 %collective-permute-start = (f32[4,2,8,128]{3,2,1,0:T(8,128)S(1)}, f32[4,2,8,128]{3,2,1,0:T(8,128)S(1)}, u32[]{:S(2)}, u32[]{:S(2)}) collective-permute-start(f32[4,2,8,128]{3,2,1,0:T(8,128)S(1)} %get-tuple-element.17), channel_id=1, source_target_pairs={{1,0},{2,1},{3,2},{4,3},{5,4},{6,5},{7,6},{9,8},{10,9},{11,10},{12... | collective-permute-start | bytes 98312 | tf_op jit(solution)/shard_map/ppermute | solution.py:400
  5.1 5.0 %collective-permute-start.1 = (f32[4,2,8,128]{3,2,1,0:T(8,128)S(1)}, f32[4,2,8,128]{3,2,1,0:T(8,128)S(1)}, u32[]{:S(2)}, u32[]{:S(2)}) collective-permute-start(f32[4,2,8,128]{3,2,1,0:T(8,128)S(1)} %get-tuple-element.18), channel_id=1, source_target_pairs={{0,1},{1,2},{2,3},{3,4},{4,5},{5,6},{6,7},{8,9},{9,10},{10,11},{11... | collective-permute-start | bytes 98312 | tf_op jit(solution)/shard_map/ppermute | solution.py:400
  10.1 0.0 collective-permute-done
  10.1 1.0 %collective-permute-done.1 = f32[4,2,8,128]{3,2,1,0:T(8,128)S(1)} collective-permute-done((f32[4,2,8,128]{3,2,1,0:T(8,128)S(1)}, f32[4,2,8,128]{3,2,1,0:T(8,128)S(1)}, u32[]{:S(2)}, u32[]{:S(2)}) %collective-permute-start.1) | collective-permute-done | bytes 32800 | tf_op jit(solution)/shard_map/ppermute | solution.py:400
  11.1 11.9 %all_to_all.25.block = f32[4,34,8,128]{3,2,1,0:T(8,128)S(1)} all-to-all(f32[4,34,8,128]{3,2,1,0:T(8,128)S(1)} %add_dynamic-update-slice_fusion), channel_id=1, replica_groups=mesh['gx'=4,'gy'=8,'gz'=8] {'gx'}, dimensions={0} | all-to-all | bytes 1114112 | tf_op jit(solution)/shard_map/all_to_all | solution.py:404
  23.0 0.0 copy-start
  23.1 4.9 %collective-permute-start.2 = (f32[4,16,8,128]{3,2,1,0:T(8,128)S(1)}, f32[4,16,8,128]{3,2,1,0:T(8,128)S(1)}, u32[]{:S(2)}, u32[]{:S(2)}) collective-permute-start(f32[4,16,8,128]{3,2,1,0:T(8,128)S(1)} %get-tuple-element.19), channel_id=1, source_target_pairs={{8,0},{16,8},{24,16},{32,24},{40,32},{48,40},{56,48},{9,1},{17,9},... | collective-permute-start | bytes 786440 | tf_op jit(solution)/shard_map/ppermute | solution.py:400
  27.9 3.0 %collective-permute-start.3 = (f32[4,16,8,128]{3,2,1,0:T(8,128)S(1)}, f32[4,16,8,128]{3,2,1,0:T(8,128)S(1)}, u32[]{:S(2)}, u32[]{:S(2)}) collective-permute-start(f32[4,16,8,128]{3,2,1,0:T(8,128)S(1)} %get-tuple-element.20), channel_id=1, source_target_pairs={{0,8},{8,16},{16,24},{24,32},{32,40},{40,48},{48,56},{1,9},{9,17},... | collective-permute-start | bytes 786440 | tf_op jit(solution)/shard_map/ppermute | solution.py:400
  31.0 2.1 %collective-permute-done.2.above = f32[4,16,8,128]{3,2,1,0:T(8,128)S(1)} collective-permute-done((f32[4,16,8,128]{3,2,1,0:T(8,128)S(1)}, f32[4,16,8,128]{3,2,1,0:T(8,128)S(1)}, u32[]{:S(2)}, u32[]{:S(2)}) %collective-permute-start.2) | collective-permute-done | bytes 262176 | tf_op jit(solution)/shard_map/ppermute | solution.py:400
  33.1 1.2 %collective-permute-done.3.below = f32[4,16,8,128]{3,2,1,0:T(8,128)S(1)} collective-permute-done((f32[4,16,8,128]{3,2,1,0:T(8,128)S(1)}, f32[4,16,8,128]{3,2,1,0:T(8,128)S(1)}, u32[]{:S(2)}, u32[]{:S(2)}) %collective-permute-start.3) | collective-permute-done | bytes 262176 | tf_op jit(solution)/shard_map/ppermute | solution.py:400
  34.3 0.0 copy-done.1
  34.3 0.0 copy-done.2
  34.3 5.5 %shard_map.104 = (f32[4,4,6,2,8,128]{5,4,3,2,1,0:T(8,128)S(1)}, f32[2,8,128]{2,1,0:T(8,128)S(1)}) custom-call(s32[1]{0:T(128)} %bitcast.place, f32[3,8]{1,0:T(4,128)S(1)} %copy-done.1, f32[3,4]{1,0:T(4,128)S(1)} %copy-done.2, f32[4,34,8,128]{3,2,1,0:T(8,128)S(1)} %all_to_all.25.block, f32[4,16,8,128]{3,2,1,0:T(8,128)S(1)} %collective-permute-done.2.above, ...), custom_call_target="tpu_custom_call" | custom-call | tf_op jit(solution)/shard_map/pallas_call | solution.py:387
  39.7 12.7 %all_to_all.26.states.refs_2_ = f32[4,4,6,2,8,128]{5,4,3,2,1,0:T(8,128)S(1)} all-to-all(f32[4,4,6,2,8,128]{5,4,3,2,1,0:T(8,128)S(1)} %get-tuple-element.21), channel_id=1, replica_groups=mesh['gx'=4,'gy'=8,'gz'=8] {'gx'}, dimensions={0} | all-to-all | bytes 1572864 | tf_op jit(solution)/shard_map/all_to_all | solution.py:404
  52.4 0.0 copy-done
  52.4 0.5 shard_map.105
  52.9 13.0 %all_to_all.27.parts = f32[8,56,128]{2,1,0:T(8,128)S(1)} all-to-all(f32[8,56,128]{2,1,0:T(8,128)S(1)} %shard_map.105), channel_id=1, replica_groups=mesh['gx'=4,'gy'=8,'gz'=8] {'gy'}, dimensions={0} | all-to-all | bytes 458752 | tf_op jit(solution)/shard_map/all_to_all | solution.py:404
  65.9 18.7 %all_to_all.28.parts = f32[8,56,128]{2,1,0:T(8,128)S(1)} all-to-all(f32[8,56,128]{2,1,0:T(8,128)S(1)} %shard_map.106), channel_id=1, replica_groups=mesh['gx'=4,'gy'=8,'gz'=8] {'gz'}, dimensions={0} | all-to-all | bytes 458752 | tf_op jit(solution)/shard_map/all_to_all | solution.py:404
  84.6 7.1 %all_to_all.29.refs_0_ = f32[4,56,128]{2,1,0:T(8,128)S(1)} all-to-all(f32[4,56,128]{2,1,0:T(8,128)S(1)} %shard_map.107), channel_id=1, replica_groups=mesh['gx'=4,'gy'=8,'gz'=8] {'gx'}, dimensions={0} | all-to-all | bytes 229376 | tf_op jit(solution)/shard_map/all_to_all | solution.py:404
  91.8 5.5 %shard_map.108 = (f32[3,8,2,8,128]{4,3,2,1,0:T(8,128)}, f32[3,8,2,8,128]{4,3,2,1,0:T(8,128)}, f32[4,2,8,128]{3,2,1,0:T(8,128)}, f32[4,8,8]{2,1,0:T(8,128)}) custom-call(f32[4,56,128]{2,1,0:T(8,128)S(1)} %all_to_all.29.refs_0_, bf16[2,3,8,128,128]{4,3,2,1,0:T(8,128)(2,1)S(1)} %copy-done, f32[4,4,6,2,8,128]{5,4,3,2,1,0:T(8,128)S(1)} %all_to_all.26.states.refs_2_), custom_call_target="tpu_custom_call" | custom-call | tf_op jit(solution)/shard_map/pallas_call | solution.py:387
  (4 shorter events, 0.1 us)
Async XLA Ops:
  0.6 33.6 %copy-start.1 = (f32[3,8]{1,0:T(4,128)S(1)}, f32[3,8]{1,0:T(4,128)}, u32[]{:S(2)}) copy-start(f32[3,8]{1,0:T(4,128)} %drive.1) | copy-start | bytes 292
  0.6 33.6 %copy-start.2 = (f32[3,4]{1,0:T(4,128)S(1)}, f32[3,4]{1,0:T(4,128)}, u32[]{:S(2)}) copy-start(f32[3,4]{1,0:T(4,128)} %moduli.1) | copy-start | bytes 148
  3.8 6.3 %collective-permute-start = (f32[4,2,8,128]{3,2,1,0:T(8,128)S(1)}, f32[4,2,8,128]{3,2,1,0:T(8,128)S(1)}, u32[]{:S(2)}, u32[]{:S(2)}) collective-permute-start(f32[4,2,8,128]{3,2,1,0:T(8,128)S(1)} %get-tuple-element.17), channel_id=1, source_target_pairs={{1,0},{2,1},{3,2},{4,3},{5,4},{6,5},{7,6},{9,8},{10,9},{11,10},{12... | collective-permute-start | bytes 98312 | tf_op jit(solution)/shard_map/ppermute | solution.py:400
  5.1 6.0 %collective-permute-start.1 = (f32[4,2,8,128]{3,2,1,0:T(8,128)S(1)}, f32[4,2,8,128]{3,2,1,0:T(8,128)S(1)}, u32[]{:S(2)}, u32[]{:S(2)}) collective-permute-start(f32[4,2,8,128]{3,2,1,0:T(8,128)S(1)} %get-tuple-element.18), channel_id=1, source_target_pairs={{0,1},{1,2},{2,3},{3,4},{4,5},{5,6},{6,7},{8,9},{9,10},{10,11},{11... | collective-permute-start | bytes 98312 | tf_op jit(solution)/shard_map/ppermute | solution.py:400
  23.0 29.4 %copy-start = (bf16[2,3,8,128,128]{4,3,2,1,0:T(8,128)(2,1)S(1)}, bf16[2,3,8,128,128]{4,3,2,1,0:T(8,128)(2,1)}, u32[]{:S(2)}) copy-start(bf16[2,3,8,128,128]{4,3,2,1,0:T(8,128)(2,1)} %refs_1_.1) | copy-start | bytes 4718596
  23.1 10.0 %collective-permute-start.2 = (f32[4,16,8,128]{3,2,1,0:T(8,128)S(1)}, f32[4,16,8,128]{3,2,1,0:T(8,128)S(1)}, u32[]{:S(2)}, u32[]{:S(2)}) collective-permute-start(f32[4,16,8,128]{3,2,1,0:T(8,128)S(1)} %get-tuple-element.19), channel_id=1, source_target_pairs={{8,0},{16,8},{24,16},{32,24},{40,32},{48,40},{56,48},{9,1},{17,9},... | collective-permute-start | bytes 786440 | tf_op jit(solution)/shard_map/ppermute | solution.py:400
  27.9 6.3 %collective-permute-start.3 = (f32[4,16,8,128]{3,2,1,0:T(8,128)S(1)}, f32[4,16,8,128]{3,2,1,0:T(8,128)S(1)}, u32[]{:S(2)}, u32[]{:S(2)}) collective-permute-start(f32[4,16,8,128]{3,2,1,0:T(8,128)S(1)} %get-tuple-element.20), channel_id=1, source_target_pairs={{0,8},{8,16},{16,24},{24,32},{32,40},{40,48},{48,56},{1,9},{9,17},... | collective-permute-start | bytes 786440 | tf_op jit(solution)/shard_map/ppermute | solution.py:400

commit v4 on v3

--- a/solution.py
+++ b/solution.py
@@ -37,7 +37,7 @@
     return lax.broadcasted_iota(jnp.int32, shape, len(shape) - 2)
 
 
-def start_kernel(now, prev, basis, ids, mask, out, down, up, local, now_in, prev_in, basis_in, ids_in, mask_in, stage, sems):
+def start_kernel(now, prev, basis, ids, mask, out, down, up, now_in, prev_in, basis_in, ids_in, mask_in, stage, sems):
     layers, comps, ny, nz, modes = basis.shape
     slabs = out.shape[0]
     moved = [(now, now_in), (prev, prev_in)]
@@ -49,7 +49,6 @@
     moved[0].wait()
     moved[1].wait()
     modal = jnp.concatenate([now_in[...].astype(f32), prev_in[...].astype(f32)]).astype(bf16)
-    gram = jnp.zeros((modes, modes), f32)
     for x in range(layers):
         for c in range(comps):
             at = x * comps + c
@@ -62,24 +61,13 @@
                 j = r % CASES
                 field = (r // CASES) * FIELDS + (j % PAIR) * comps + c
                 out[j // PAIR, 2 * field + x] = stage[at, r * ny : (r + 1) * ny, :]
-            gram = gram + dot(rows, rows, (0, 0))
     moved[-2].wait()
     moved[-1].wait()
-    half = modes // 2
-    share = half // slabs
-    lane = lanes_of((half, modes))
-    packed = jnp.where((lane < half) & (lane <= rows_of((half, modes))), pltpu.roll(gram[half:], half, 1), gram[:half])
-    own = jnp.sum(jnp.where(rows_of(gram.shape) == lanes_of(gram.shape), gram, 0.0), axis=0, keepdims=True)
-    local[...] = jnp.zeros(local.shape, f32)
-    local[0:1] = pltpu.roll(own, half, 1)
-    local[1:2] = own
     for p in range(slabs):
         for x in range(layers):
             for i in range(PAIR):
                 out[p, 2 * (MASKS + i) + x] = mask_in[PAIR * p + i, x].astype(f32)
             out[p, 2 * MATERIAL + x] = (ids_in[x] + 1).astype(f32)
-        for t in range(share // 8):
-            out[p, GRAM + t] = packed[share * p + 8 * t : share * p + 8 * t + 8]
         quarter = lanes_of((ny, nz)) // REACH
         for t in range(2):
             low = jnp.zeros((ny, nz), f32)
@@ -93,7 +81,29 @@
                     high = jnp.where(quarter == 2 * g + 1, pltpu.roll(v, turn, 1) if turn else v, high)
             down[p, t] = low
             up[p, t] = high
-            out[p, EDGE + t] = jnp.zeros((ny, nz), f32)
+        for t in range(EDGE, out.shape[1]):
+            out[p, t] = jnp.zeros((ny, nz), f32)
+
+
+def gram_kernel(basis, out, local):
+    layers, comps, ny, nz, modes = basis.shape
+    slabs = out.shape[0]
+    gram = jnp.zeros((modes, modes), f32)
+    for x in range(layers):
+        for c in range(comps):
+            rows = basis[x, c].reshape(ny * nz, modes)
+            gram = gram + dot(rows, rows, (0, 0))
+    half = modes // 2
+    share = half // slabs
+    lane = lanes_of((half, modes))
+    packed = jnp.where((lane < half) & (lane <= rows_of((half, modes))), pltpu.roll(gram[half:], half, 1), gram[:half])
+    own = jnp.sum(jnp.where(rows_of(gram.shape) == lanes_of(gram.shape), gram, 0.0), axis=0, keepdims=True)
+    local[...] = jnp.zeros(local.shape, f32)
+    local[0:1] = pltpu.roll(own, half, 1)
+    local[1:2] = own
+    for p in range(slabs):
+        for t in range(share // 8):
+            out[p, t] = packed[share * p + 8 * t : share * p + 8 * t + 8]
 
 
 def faces_kernel(block, down, up):
@@ -107,13 +117,25 @@
             up[g, q] = jnp.where(first, b, a)
 
 
-def steps_kernel(place, drive, moduli, block, above, below, out, share, fields, masks, stiff, weight, couple, diagonal):
+def steps_kernel(
+    place, drive, moduli, block, above, below, out, share, fields, masks, stiff, weight, couple, diagonal,
+    side, side_mask, side_stiff, side_couple, side_diagonal,
+):
     slabs, _, ny, nz = block.shape
     nx = 2 * slabs
     first = rows_of((ny, nz)) < REACH
-    lane = lanes_of((ny, nz))
     zero = jnp.zeros((ny, nz), f32)
-    wide_zero = jnp.zeros((2 * ny, 2 * nz), f32)
+    plane_zero = jnp.zeros((2 * ny, nz), f32)
+    halves = (slice(0, ny), slice(ny, 2 * ny))
+
+    def level_of(value, prop):
+        level = zero
+        for m in range(moduli.shape[1]):
+            level = jnp.where(value == m + 1.0, moduli[prop, m], level)
+        return level
+
+    group = lanes_of((ny, nz)) // 16
+    sides = {}
     for g in range(slabs):
         edges = [
             (block[g, EDGE], jnp.where(first, above[g, COUNT], below[g, COUNT])),
@@ -126,97 +148,142 @@
             )
             for i in range(2):
                 x = 2 * g + i
-                spot = 2 * q + i
-                ends = []
-                for edge in edges[spot // 16]:
-                    turn = 8 * (spot % 16)
-                    right = pltpu.roll(edge, (nz - turn) % nz, 1) if turn else edge
-                    left = pltpu.roll(edge, (2 * nz - 8 - turn) % nz, 1) if (nz - 8 - turn) % nz else edge
-                    ends.append(jnp.where(lane < REACH, right, jnp.where(lane >= nz - REACH, left, zero)))
-                parts = ((block[g, spot], ends[0]), (beside[i], ends[1]))
-                for k in range(2):
-                    for h in range(2):
-                        here = (slice(k * ny, (k + 1) * ny), slice(h * nz, (h + 1) * nz))
-                        value = parts[k][h]
-                        if q < FIELDS:
-                            fields[0, q, 1 + x, here[0], here[1]] = value
-                        elif q < MASKS:
-                            fields[1, q - FIELDS, 1 + x, here[0], here[1]] = value
-                        elif q < MATERIAL:
-                            masks[q - MASKS, x, here[0], here[1]] = value
-                        else:
-                            for prop in range(3):
-                                level = zero
-                                for m in range(moduli.shape[1]):
-                                    level = jnp.where(value == m + 1.0, moduli[prop, m], level)
-                                if prop < 2:
-                                    stiff[prop, 1 + x, here[0], here[1]] = level
-                                else:
-                                    weight[x, here[0], here[1]] = step_squared * level
+                for rows, value in zip(halves, (block[g, 2 * q + i], beside[i])):
+                    if q < FIELDS:
+                        fields[0, q, 1 + x, rows] = value
+                    elif q < MASKS:
+                        fields[1, q - FIELDS, 1 + x, rows] = value
+                    elif q < MATERIAL:
+                        masks[q - MASKS, x, rows] = value
+                    else:
+                        stiff[0, 1 + x, rows] = level_of(value, 0)
+                        stiff[1, 1 + x, rows] = level_of(value, 1)
+                        weight[x, rows] = step_squared * level_of(value, 2)
+            if q < MASKS:
+                key, cases = (q // FIELDS, q % 3), (q % FIELDS // 3,)
+            elif q < MATERIAL:
+                key, cases = "mask", (q - MASKS,)
+            else:
+                key, cases = "material", (0, 1)
+            for k in range(2):
+                for i in cases:
+                    turn = (64 * i + 16 * g - 16 * (q % 8)) % nz
+                    edge = edges[q // 8][k]
+                    edge = pltpu.roll(edge, turn, 1) if turn else edge
+                    sides[key, k] = jnp.where(group == 4 * i + g, edge, sides.get((key, k), zero))
+    side_weight = []
+    for k, rows in enumerate(halves):
+        for t in range(2):
+            for c in range(3):
+                side[t, c, rows] = sides[(t, c), k]
+        side_stiff[0, rows] = level_of(sides["material", k], 0)
+        side_stiff[1, rows] = level_of(sides["material", k], 1)
+        heavy = step_squared * level_of(sides["material", k], 2)
+        side_weight.append(heavy)
+        side_mask[rows] = sides["mask", k] * heavy
     for x in (0, nx + 1):
         for f in range(FIELDS):
-            fields[0, f, x] = wide_zero
-            fields[1, f, x] = wide_zero
-        stiff[0, x] = wide_zero
-        stiff[1, x] = wide_zero
+            fields[0, f, x] = plane_zero
+            fields[1, f, x] = plane_zero
+        stiff[0, x] = plane_zero
+        stiff[1, x] = plane_zero
     for t in range(share.shape[0]):
         total = block[0, GRAM + t]
         for g in range(1, slabs):
             total = total + block[g, GRAM + t]
         share[t] = total
 
-    def beside_of(ref, lead, x):
-        v = ref[lead + (x + 1,)]
-        return v, (
-            ref[lead + (x,)], ref[lead + (x + 2,)],
+    lane = lanes_of((2 * ny, nz))
+    spot = lane % 8
+    layer = lane % 64 // 8
+
+    def turned_by(v, shift):
+        return pltpu.roll(v, shift % nz, 1) if shift % nz else v
+
+    def near_main(get, edge, base, x, rows):
+        v = get(x + 1)
+        part = lambda a: a[:rows]
+        lanes = lane[:rows]
+        low = jnp.where(lanes == 0, turned_by(edge[:rows], -(base + 7)), pltpu.roll(part(v), 1, 1))
+        high = jnp.where(lanes == nz - 1, turned_by(edge[:rows], nz - 1 - base), pltpu.roll(part(v), nz - 1, 1))
+        return part(v), (
+            part(get(x)), part(get(x + 2)), part(pltpu.roll(v, 1, 0)), part(pltpu.roll(v, 2 * ny - 1, 0)), low, high
+        )
+
+    def near_side(v, gets):
+        low, high = plane_zero, plane_zero
+        for i in range(PAIR):
+            for x in range(nx):
+                base = 64 * i + 8 * x
+                main = gets[i](x + 1)
+                low = jnp.where(lane == base, turned_by(main, base + 1), low)
+                high = jnp.where(lane == base + 7, turned_by(main, base + 7), high)
+        return (
+            jnp.where(layer == 0, 0.0, pltpu.roll(v, 8, 1)), jnp.where(layer == nx - 1, 0.0, pltpu.roll(v, nz - 8, 1)),
             pltpu.roll(v, 1, 0), pltpu.roll(v, 2 * ny - 1, 0),
-            pltpu.roll(v, 1, 1), pltpu.roll(v, 2 * nz - 1, 1),
+            jnp.where(spot == 0, low, pltpu.roll(v, 1, 1)), jnp.where(spot == 7, high, pltpu.roll(v, nz - 1, 1)),
         )
 
-    def prepare(x, carry):
-        half = 0.5 * weight[x]
+    def coupled(half, kinds, store, store_diagonal):
         sums = []
         for kind in range(2):
-            v, near = beside_of(stiff, (kind,), x)
+            v, near = kinds[kind]
             pairs = []
             for d in range(6):
                 value = half * (v + near[d])
-                couple[kind, d, x] = value
+                store(kind, d, value)
                 pairs.append(value)
             sums.append([pairs[2 * a] + pairs[2 * a + 1] for a in range(3)])
         for c in range(3):
-            total = sums[0][c] + sums[1][(c + 1) % 3] + sums[1][(c + 2) % 3]
-            diagonal[c, x] = 2.0 - total
+            store_diagonal(c, 2.0 - (sums[0][c] + sums[1][(c + 1) % 3] + sums[1][(c + 2) % 3]))
+
+    def setter(ref, *tail):
+        def put(*at):
+            ref[at[:-1] + tail] = at[-1]
+        return put
+
+    for x in range(nx):
+        kinds = [near_main(lambda at: stiff[kind, at], side_stiff[kind], 8 * x, x, 2 * ny) for kind in range(2)]
+        coupled(0.5 * weight[x], kinds, setter(couple, x), setter(diagonal, x))
         for i in range(PAIR):
             masks[i, x] = masks[i, x] * weight[x]
-        return carry
-
-    lax.fori_loop(0, nx, prepare, 0)
+    kinds = [(side_stiff[k], near_side(side_stiff[k], [lambda at: stiff[k, at]] * PAIR)) for k in range(2)]
+    coupled(0.5 * jnp.concatenate(side_weight), kinds, setter(side_couple), setter(side_diagonal))
+
     slab = place[0]
+
+    def advanced(v, near, before, centre, forced, pairs, c):
+        value = centre * v - before + forced
+        for d in range(6):
+            value = value + pairs(0 if d // 2 == c else 1, d) * near[d]
+        return value
+
     for s in range(STEPS):
         ramp = min(1.0, (s + 1) / ramp_steps)
         last = s == STEPS - 1
-        own = (slice(0, ny), slice(0, nz)) if last else (slice(None), slice(None))
-
-        def step(x, carry):
-            for i in range(PAIR):
-                for c in range(3):
+        rows = ny if last else 2 * ny
+        now, to = s % 2, 1 - s % 2
+        force = [[drive[c, PAIR * slab + i] * ramp for c in range(3)] for i in range(PAIR)]
+        for c in range(3):
+            gets = [lambda at, f=3 * i + c: fields[now, f, at] for i in range(PAIR)]
+            edge = side[now, c]
+            if not last:
+                push = jnp.where(lane < 64, force[0][c], force[1][c])
+                side[to, c] = advanced(
+                    edge, near_side(edge, gets), side[to, c], side_diagonal[c], side_mask[...] * push,
+                    lambda kind, d: side_couple[kind, d], c,
+                )
+            for x in range(nx):
+                for i in range(PAIR):
                     f = 3 * i + c
-                    now, to = fields.at[s % 2, f], fields.at[1 - s % 2, f]
-                    v, near = beside_of(now, (), x)
-                    if last:
-                        v, near = v[own], [n[own] for n in near]
-                    value = diagonal[(c, x) + own] * v - to[(x + 1,) + own]
-                    value = value + masks[(i, x) + own] * (drive[c, PAIR * slab + i] * ramp)
-                    for d in range(6):
-                        kind = 0 if d // 2 == c else 1
-                        value = value + couple[(kind, d, x) + own] * near[d]
+                    v, near = near_main(gets[i], edge, 64 * i + 8 * x, x, rows)
+                    value = advanced(
+                        v, near, fields[to, f, x + 1, :rows], diagonal[c, x, :rows], masks[i, x, :rows] * force[i][c],
+                        lambda kind, d: couple[kind, d, x, :rows], c,
+                    )
                     if not last:
-                        to[x + 1] = value
-                    out[x // 2, s, f, x % 2] = value[:ny, :nz]
-            return carry
-
-        lax.fori_loop(0, nx, step, 0)
+                        fields[to, f, x + 1] = value
+                    out[x // 2, s, f, x % 2] = value[:ny]
 
 
 def project_kernel(basis, states, share, local, out, stage):
@@ -242,11 +309,12 @@
         tile = jnp.where(lane // CASES == s, square[s * CASES : (s + 1) * CASES], tile)
     tile = jnp.concatenate([tile, jnp.zeros((CASES, modes - count), f32)], axis=1)
     tile = jnp.where(lanes_of(tile.shape) < modes // 2, tile, local[...])
+    half = count // 2
     for g in range(out.shape[0]):
-        out[g, :count] = coef
-        out[g, count : count + CASES] = tile
-        for t in range(share.shape[0]):
-            out[g, count + CASES + 8 * t : count + CASES + 8 * t + 8] = share[t]
+        h = g % 2
+        out[g, :half] = coef[h * half : (h + 1) * half]
+        out[g, half : half + CASES] = tile
+        out[g, half + CASES :] = share[h]
 
 
 def sum_kernel(parts, out):
@@ -308,12 +376,16 @@
     count = STEPS * CASES
     half = modes // 2
     high = lax.Precision.HIGHEST
-    own = parts[0, : count + CASES]
-    for g in range(1, parts.shape[0]):
-        own = own + parts[g, : count + CASES]
-    own = own * weight
-    coef, square = own[:count], own[count:]
-    packed = jnp.concatenate([parts[g, count + CASES :] for g in range(parts.shape[0])]) * weight
+    members, upto = parts.shape[0], count // 2 + CASES
+    owns = []
+    for h in range(2):
+        own = parts[h, :upto]
+        for g in range(h + 2, members, 2):
+            own = own + parts[g, :upto]
+        owns.append(own * weight)
+    coef = jnp.concatenate([own[: count // 2] for own in owns])
+    square = owns[0][count // 2 :]
+    packed = jnp.concatenate([parts[g, upto:] for g in range(members)]) * weight
     lane, row = lanes_of(packed.shape), rows_of(packed.shape)
     flipped = padded(packed).T
     diagonal = jnp.where(lane[:1] < half, pltpu.roll(square[:1], half, 1), square[1:2])
@@ -339,7 +411,16 @@
             change = change + dot(piece, wide, (1, 1))
         return rounded.astype(f32), left, change
 
+    def expanded(rounded, slot):
+        for c in range(comps):
+            for x in range(layers):
+                at = x * comps + c
+                taken = dot(rounded.astype(bf16), basis[x, c].reshape(ny * nz, modes), (1, 1))
+                for y in range(ny):
+                    stage[slot, at, pl.ds(y, CASES, stride=ny), :] = taken[:, y * nz : (y + 1) * nz]
+
     rounded, left, change = change_of(coef)
+    expanded(rounded[count - CASES :], 0)
     first, second = [], []
     for s in range(STEPS):
         at = slice(s * CASES, (s + 1) * CASES)
@@ -347,6 +428,7 @@
         second.append(mixed(first[s][1], left[at]))
     second = jnp.concatenate(second)
     rounded_2, left_2, change = change_of(second)
+    expanded(rounded_2[count - CASES :], 1)
     for s in range(STEPS):
         at = slice(s * CASES, (s + 1) * CASES)
         whole = dot(first[s][0], padded(first[s][1]), (1, 1), high)
@@ -355,24 +437,24 @@
         coefficients[s, 0] = coef[at]
         coefficients[s, 1] = second[at]
     mix = mixed(inverse, first[-1][1])
-    shift = mixed(mix, rounded[at]) + mixed(inverse, rounded_2[at])
-    pieces = jnp.concatenate([piece.astype(f32) for piece in pieces_of(shift)]).astype(bf16)
-    scalars = [[mix[i : i + 1, j : j + 1] for j in range(CASES)] for i in range(CASES)]
+    wide = lambda small: [
+        [jnp.broadcast_to(small[i : i + 1, j : j + 1], (ny, nz)) for j in range(i + 1)] for i in range(CASES)
+    ]
+    mix, inverse = wide(mix), wide(inverse)
     for c in range(comps):
         for x in range(layers):
             at = x * comps + c
-            taken = dot(pieces, basis[x, c].reshape(ny * nz, modes), (1, 1))
-            taken = taken[:CASES] + taken[CASES : 2 * CASES] + taken[2 * CASES :]
-            for y in range(ny):
-                stage[at, pl.ds(y, CASES, stride=ny), :] = taken[:, y * nz : (y + 1) * nz]
-            snapshot = [
-                states[j // PAIR, STEPS - 1, (j % PAIR) * comps + c, x].astype(bf16).astype(f32) for j in range(CASES)
-            ]
+            resid, extra = [], []
+            for j in range(CASES):
+                here = slice(j * ny, (j + 1) * ny)
+                snapshot = states[j // PAIR, STEPS - 1, (j % PAIR) * comps + c, x].astype(bf16).astype(f32)
+                resid.append(snapshot - stage[0, at, here])
+                extra.append(stage[1, at, here])
             for i in range(CASES):
-                total = scalars[i][0] * snapshot[0]
-                for j in range(1, CASES):
-                    total = total + scalars[i][j] * snapshot[j]
-                held[c, i, x] = total - stage[at, i * ny : (i + 1) * ny, :]
+                total = mix[i][0] * resid[0] - inverse[i][0] * extra[0]
+                for j in range(1, i + 1):
+                    total = total + (mix[i][j] * resid[j] - inverse[i][j] * extra[j])
+                held[c, i, x] = total
         moved.append(pltpu.make_async_copy(held.at[c], modes_out.at[c], sems.at[len(moved)]))
         moved[-1].start()
     for copy in moved:
@@ -412,20 +494,22 @@
     share = modes // 2 // slabs // 8
     blocks = layers * comps
     inputs = [pltpu.with_memory_space_constraint(a, pltpu.HBM) for a in (modal_now.T, modal_prev.T, basis, material_ids, drive_mask)]
-    block, down, up, local = call(
+    block, down, up = call(
         start_kernel,
-        [(slabs, GRAM + share) + tile, (slabs, 2) + tile, (slabs, 2) + tile, (CASES, modes)],
+        [(slabs, GRAM + share) + tile, (slabs, 2) + tile, (slabs, 2) + tile],
         inputs,
         [pltpu.VMEM(a.shape, a.dtype) for a in inputs] + [(blocks, 2 * CASES * ny, nz)],
         copies=blocks + 4,
         ins_away=5,
     )
     edge = sent(down, "gz", False) + sent(up, "gz", True)
-    block = turned(lax.dynamic_update_slice(block, edge, (0, EDGE, 0, 0)), "gx")
+    gram, local = call(gram_kernel, [(slabs, share) + tile, (CASES, modes)], [basis])
+    block = lax.dynamic_update_slice(block, jnp.concatenate([edge, gram], axis=1), (0, EDGE, 0, 0))
+    block = turned(block, "gx")
     down, up = call(faces_kernel, [(slabs, COUNT + 1) + tile] * 2, [block])
     above, below = sent(down, "gy", False), sent(up, "gy", True)
     nx = layers * slabs
-    wide = (2 * ny, 2 * nz)
+    wide = (2 * ny, nz)
     place = lax.axis_index("gx").astype(jnp.int32)[None]
     states, gram = call(
         steps_kernel,
@@ -433,24 +517,30 @@
         [place, drive, moduli, block, above, below],
         [
             (2, FIELDS, nx + 2) + wide, (PAIR, nx) + wide, (2, nx + 2) + wide, (nx,) + wide,
-            (2, 6, nx) + wide, (3, nx) + wide,
+            (2, 6, nx) + wide, (3, nx) + wide, (2, 3) + wide, wide, (2,) + wide, (2, 6) + wide, (3,) + wide,
         ],
         3,
     )
     states = turned(states, "gx")
     count = STEPS * CASES
-    width = count + CASES + 8 * share
+    width = count // 2 + CASES + 8
     parts, = call(
         project_kernel, [(rows, width, modes)], [basis, states, gram, local], [(blocks, count * ny, nz)]
     )
     parts, = call(sum_kernel, [(depth, width, modes)], [turned(parts, "gy")])
-    parts, = call(sum_kernel, [(slabs, width, modes)], [turned(parts, "gz")])
+    parts, = call(sum_kernel, [(2 * slabs, width, modes)], [turned(parts, "gz")])
+    groups = [
+        [(a * rows + 2 * h + core) * depth + z for a in range(slabs) for core in range(2)]
+        for h in range(rows // 2)
+        for z in range(depth)
+    ]
+    parts = lax.all_to_all(parts, ("gx", "gy", "gz"), 0, 0, tiled=True, axis_index_groups=groups)
     held = (comps, CASES, layers) + tile
     displacement, modes_out, coefficients, factors = call(
         lambda *refs: finish_kernel(dof_weight, *refs),
         [held, held, (STEPS, 2, CASES, modes), (STEPS, CASES, CASES)],
-        [turned(parts, "gx"), basis, states],
-        [(blocks, CASES * ny, nz), held],
+        [parts, basis, states],
+        [(2, blocks, CASES * ny, nz), held],
         copies=comps * CASES + comps,
         outs_away=2,
     )

time: 99.1 us -> 94.6 us (0.955); the launches traced: 97.3 us -> 94.2 us
  Pallas kernels: 14.7 us -> 12 us
    all_to_all x0 -> x1, blocking collectives: none -> 10 us  [shards(): lax.all_to_all(parts, ('gx', 'gy', 'gz'), 0, 0, tiled=True, axis_index_gr...]
    all_to_all x5 -> x4, blocking collectives: 63.4 us -> 53.8 us  [turned(): return lax.all_to_all(parts, axis, 0, 0, tiled=True)]
    pallas_call x7 -> x8, Pallas kernels: 14.7 us -> 12 us  [call(): pl.pallas_call(kernel, out_shape=[jax.ShapeDtypeStruct(shape, f32) for sh...]
  transfers between devices with their start and end apart: 4 -> 4, of which waited for: 3 -> 3; matrix products, arithmetic and copies ran while one was open for 0% -> 0% of each run, Pallas kernels for 0% -> 1%
where the time goes in v4:
time: 94.6 us; the launch traced here: 94.2 us
  blocking collectives  63.8 us (67%)
  starting transfers between devices  14 us (15%)
  Pallas kernels  12 us (13%)
  waiting for transfers between devices  3.58 us (4%)
    all_to_all x4, blocking collectives, turned(): return lax.all_to_all(parts, axis, 0, 0, tiled=True)  53.8 us
    ppermute x4, starting transfers between devices, sent(): lax.ppermute(block, axis, pairs if forward else [(b, a) for a, b in pairs])  14 us
    pallas_call x8, Pallas kernels, call(): pl.pallas_call(kernel, out_shape=[jax.ShapeDtypeStruct(shape, f32) for sh...  12 us
    all_to_all x1, blocking collectives, shards(): lax.all_to_all(parts, ('gx', 'gy', 'gz'), 0, 0, tiled=True, axis_index_gr...  10 us
    ppermute x4, waiting for transfers between devices, sent(): lax.ppermute(block, axis, pairs if forward else [(b, a) for a, b in pairs])  3.58 us
  transfers between devices with their start and end apart: 4, of which 3 were waited for; matrix products, arithmetic and copies ran while one was open for 0% of the time, Pallas kernels for 1%

profile of v4, /device:TPU:1, one launch (start us, length us, event | category | flops | bytes accessed | tf_op | source)
XLA Modules:
  0.0 94.2 jit_solution(17888516262351053976)
XLA Ops:
  0.6 0.0 copy-start
  0.6 2.7 %shard_map.102 = (f32[4,34,8,128]{3,2,1,0:T(8,128)S(1)}, f32[4,2,8,128]{3,2,1,0:T(8,128)S(1)}, f32[4,2,8,128]{3,2,1,0:T(8,128)S(1)}) custom-call(bf16[8,128]{1,0:T(8,128)(2,1)} %bitcast.4, bf16[8,128]{1,0:T(8,128)(2,1)} %bitcast.5, bf16[2,3,8,128,128]{4,3,2,1,0:T(8,128)(2,1)} %refs_1_.1, s32[2,8,128]{2,1,0:T(8,128)} %ids.1, s32[8,2,8,128]{3,2,1,0:T(8,128)} %mask.1), custom_call_target="tpu_custom_call" | custom-call | tf_op jit(solution)/shard_map/pallas_call | solution.py:469
  3.3 1.3 %collective-permute-start = (f32[4,2,8,128]{3,2,1,0:T(8,128)S(1)}, f32[4,2,8,128]{3,2,1,0:T(8,128)S(1)}, u32[]{:S(2)}, u32[]{:S(2)}) collective-permute-start(f32[4,2,8,128]{3,2,1,0:T(8,128)S(1)} %get-tuple-element.18), channel_id=1, source_target_pairs={{1,0},{2,1},{3,2},{4,3},{5,4},{6,5},{7,6},{9,8},{10,9},{11,10},{12... | collective-permute-start | bytes 98312 | tf_op jit(solution)/shard_map/ppermute | solution.py:482
  4.6 0.0 copy-start.1
  4.6 0.0 copy-start.2
  4.6 5.0 %collective-permute-start.1 = (f32[4,2,8,128]{3,2,1,0:T(8,128)S(1)}, f32[4,2,8,128]{3,2,1,0:T(8,128)S(1)}, u32[]{:S(2)}, u32[]{:S(2)}) collective-permute-start(f32[4,2,8,128]{3,2,1,0:T(8,128)S(1)} %get-tuple-element.19), channel_id=1, source_target_pairs={{0,1},{1,2},{2,3},{3,4},{4,5},{5,6},{6,7},{8,9},{9,10},{10,11},{11... | collective-permute-start | bytes 98312 | tf_op jit(solution)/shard_map/ppermute | solution.py:482
  9.6 0.0 copy-done
  9.7 0.7 shard_map.103
  10.4 0.0 collective-permute-done
  10.4 0.3 collective-permute-done.1
  10.7 11.9 %all_to_all.25.block = f32[4,34,8,128]{3,2,1,0:T(8,128)S(1)} all-to-all(f32[4,34,8,128]{3,2,1,0:T(8,128)S(1)} %maximum_dynamic-update-slice_fusion), channel_id=1, replica_groups=mesh['gx'=4,'gy'=8,'gz'=8] {'gx'}, dimensions={0} | all-to-all | bytes 1114112 | tf_op jit(solution)/shard_map/all_to_all | solution.py:486
  22.6 4.7 %collective-permute-start.2 = (f32[4,16,8,128]{3,2,1,0:T(8,128)S(1)}, f32[4,16,8,128]{3,2,1,0:T(8,128)S(1)}, u32[]{:S(2)}, u32[]{:S(2)}) collective-permute-start(f32[4,16,8,128]{3,2,1,0:T(8,128)S(1)} %get-tuple-element.21), channel_id=1, source_target_pairs={{8,0},{16,8},{24,16},{32,24},{40,32},{48,40},{56,48},{9,1},{17,9},... | collective-permute-start | bytes 786440 | tf_op jit(solution)/shard_map/ppermute | solution.py:482
  27.4 3.0 %collective-permute-start.3 = (f32[4,16,8,128]{3,2,1,0:T(8,128)S(1)}, f32[4,16,8,128]{3,2,1,0:T(8,128)S(1)}, u32[]{:S(2)}, u32[]{:S(2)}) collective-permute-start(f32[4,16,8,128]{3,2,1,0:T(8,128)S(1)} %get-tuple-element.22), channel_id=1, source_target_pairs={{0,8},{8,16},{16,24},{24,32},{32,40},{40,48},{48,56},{1,9},{9,17},... | collective-permute-start | bytes 786440 | tf_op jit(solution)/shard_map/ppermute | solution.py:482
  30.4 2.1 %collective-permute-done.2.above = f32[4,16,8,128]{3,2,1,0:T(8,128)S(1)} collective-permute-done((f32[4,16,8,128]{3,2,1,0:T(8,128)S(1)}, f32[4,16,8,128]{3,2,1,0:T(8,128)S(1)}, u32[]{:S(2)}, u32[]{:S(2)}) %collective-permute-start.2) | collective-permute-done | bytes 262176 | tf_op jit(solution)/shard_map/ppermute | solution.py:482
  32.5 1.2 %collective-permute-done.3.below = f32[4,16,8,128]{3,2,1,0:T(8,128)S(1)} collective-permute-done((f32[4,16,8,128]{3,2,1,0:T(8,128)S(1)}, f32[4,16,8,128]{3,2,1,0:T(8,128)S(1)}, u32[]{:S(2)}, u32[]{:S(2)}) %collective-permute-start.3) | collective-permute-done | bytes 262176 | tf_op jit(solution)/shard_map/ppermute | solution.py:482
  33.7 0.0 copy-done.1
  33.7 0.0 copy-done.2
  33.7 3.2 %shard_map.105 = (f32[4,4,6,2,8,128]{5,4,3,2,1,0:T(8,128)S(1)}, f32[2,8,128]{2,1,0:T(8,128)S(1)}) custom-call(s32[1]{0:T(128)} %bitcast.place, f32[3,8]{1,0:T(4,128)S(1)} %copy-done.1, f32[3,4]{1,0:T(4,128)S(1)} %copy-done.2, f32[4,34,8,128]{3,2,1,0:T(8,128)S(1)} %all_to_all.25.block, f32[4,16,8,128]{3,2,1,0:T(8,128)S(1)} %collective-permute-done.2.above, ...), custom_call_target="tpu_custom_call" | custom-call | tf_op jit(solution)/shard_map/pallas_call | solution.py:469
  36.9 12.7 %all_to_all.26.states.refs_2_ = f32[4,4,6,2,8,128]{5,4,3,2,1,0:T(8,128)S(1)} all-to-all(f32[4,4,6,2,8,128]{5,4,3,2,1,0:T(8,128)S(1)} %get-tuple-element.23), channel_id=1, replica_groups=mesh['gx'=4,'gy'=8,'gz'=8] {'gx'}, dimensions={0} | all-to-all | bytes 1572864 | tf_op jit(solution)/shard_map/all_to_all | solution.py:486
  49.6 0.5 shard_map.106
  50.1 12.1 %all_to_all.27.parts = f32[8,32,128]{2,1,0:T(8,128)S(1)} all-to-all(f32[8,32,128]{2,1,0:T(8,128)S(1)} %shard_map.106), channel_id=1, replica_groups=mesh['gx'=4,'gy'=8,'gz'=8] {'gy'}, dimensions={0} | all-to-all | bytes 262144 | tf_op jit(solution)/shard_map/all_to_all | solution.py:486
  62.2 17.1 %all_to_all.28.parts = f32[8,32,128]{2,1,0:T(8,128)S(1)} all-to-all(f32[8,32,128]{2,1,0:T(8,128)S(1)} %shard_map.107), channel_id=1, replica_groups=mesh['gx'=4,'gy'=8,'gz'=8] {'gz'}, dimensions={0} | all-to-all | bytes 262144 | tf_op jit(solution)/shard_map/all_to_all | solution.py:486
  79.3 10.0 %all_to_all.29.refs_0_ = f32[8,32,128]{2,1,0:T(8,128)S(1)} all-to-all(f32[8,32,128]{2,1,0:T(8,128)S(1)} %shard_map.108), channel_id=1, replica_groups={{0,8,64,72,128,136,192,200},{1,9,65,73,129,137,193,201},{2,10,66,74,130..., dimensions={0} | all-to-all | bytes 262144 | tf_op jit(solution)/shard_map/all_to_all | solution.py:537
  89.4 4.9 %shard_map.109 = (f32[3,8,2,8,128]{4,3,2,1,0:T(8,128)}, f32[3,8,2,8,128]{4,3,2,1,0:T(8,128)}, f32[4,2,8,128]{3,2,1,0:T(8,128)}, f32[4,8,8]{2,1,0:T(8,128)}) custom-call(f32[8,32,128]{2,1,0:T(8,128)S(1)} %all_to_all.29.refs_0_, bf16[2,3,8,128,128]{4,3,2,1,0:T(8,128)(2,1)S(1)} %copy-done, f32[4,4,6,2,8,128]{5,4,3,2,1,0:T(8,128)S(1)} %all_to_all.26.states.refs_2_), custom_call_target="tpu_custom_call" | custom-call | tf_op jit(solution)/shard_map/pallas_call | solution.py:469
  (5 shorter events, 0.1 us)
Async XLA Ops:
  0.6 9.0 %copy-start = (bf16[2,3,8,128,128]{4,3,2,1,0:T(8,128)(2,1)S(1)}, bf16[2,3,8,128,128]{4,3,2,1,0:T(8,128)(2,1)}, u32[]{:S(2)}) copy-start(bf16[2,3,8,128,128]{4,3,2,1,0:T(8,128)(2,1)} %refs_1_.1) | copy-start | bytes 4718596
  3.3 7.0 %collective-permute-start = (f32[4,2,8,128]{3,2,1,0:T(8,128)S(1)}, f32[4,2,8,128]{3,2,1,0:T(8,128)S(1)}, u32[]{:S(2)}, u32[]{:S(2)}) collective-permute-start(f32[4,2,8,128]{3,2,1,0:T(8,128)S(1)} %get-tuple-element.18), channel_id=1, source_target_pairs={{1,0},{2,1},{3,2},{4,3},{5,4},{6,5},{7,6},{9,8},{10,9},{11,10},{12... | collective-permute-start | bytes 98312 | tf_op jit(solution)/shard_map/ppermute | solution.py:482
  4.6 29.1 %copy-start.1 = (f32[3,8]{1,0:T(4,128)S(1)}, f32[3,8]{1,0:T(4,128)}, u32[]{:S(2)}) copy-start(f32[3,8]{1,0:T(4,128)} %drive.1) | copy-start | bytes 292
  4.6 29.1 %copy-start.2 = (f32[3,4]{1,0:T(4,128)S(1)}, f32[3,4]{1,0:T(4,128)}, u32[]{:S(2)}) copy-start(f32[3,4]{1,0:T(4,128)} %moduli.1) | copy-start | bytes 148
  4.6 6.0 %collective-permute-start.1 = (f32[4,2,8,128]{3,2,1,0:T(8,128)S(1)}, f32[4,2,8,128]{3,2,1,0:T(8,128)S(1)}, u32[]{:S(2)}, u32[]{:S(2)}) collective-permute-start(f32[4,2,8,128]{3,2,1,0:T(8,128)S(1)} %get-tuple-element.19), channel_id=1, source_target_pairs={{0,1},{1,2},{2,3},{3,4},{4,5},{5,6},{6,7},{8,9},{9,10},{10,11},{11... | collective-permute-start | bytes 98312 | tf_op jit(solution)/shard_map/ppermute | solution.py:482
  22.6 9.9 %collective-permute-start.2 = (f32[4,16,8,128]{3,2,1,0:T(8,128)S(1)}, f32[4,16,8,128]{3,2,1,0:T(8,128)S(1)}, u32[]{:S(2)}, u32[]{:S(2)}) collective-permute-start(f32[4,16,8,128]{3,2,1,0:T(8,128)S(1)} %get-tuple-element.21), channel_id=1, source_target_pairs={{8,0},{16,8},{24,16},{32,24},{40,32},{48,40},{56,48},{9,1},{17,9},... | collective-permute-start | bytes 786440 | tf_op jit(solution)/shard_map/ppermute | solution.py:482
  27.4 6.3 %collective-permute-start.3 = (f32[4,16,8,128]{3,2,1,0:T(8,128)S(1)}, f32[4,16,8,128]{3,2,1,0:T(8,128)S(1)}, u32[]{:S(2)}, u32[]{:S(2)}) collective-permute-start(f32[4,16,8,128]{3,2,1,0:T(8,128)S(1)} %get-tuple-element.22), channel_id=1, source_target_pairs={{0,8},{8,16},{16,24},{24,32},{32,40},{40,48},{48,56},{1,9},{9,17},... | collective-permute-start | bytes 786440 | tf_op jit(solution)/shard_map/ppermute | solution.py:482

commit v5 on v4

--- a/solution.py
+++ b/solution.py
@@ -37,7 +37,7 @@
     return lax.broadcasted_iota(jnp.int32, shape, len(shape) - 2)
 
 
-def start_kernel(now, prev, basis, ids, mask, out, down, up, now_in, prev_in, basis_in, ids_in, mask_in, stage, sems):
+def start_kernel(place, odd, turn_z, now, prev, basis, ids, mask, out, even_pairs, odd_pairs, basis_in, now_in, prev_in, ids_in, mask_in, stage, sems):
     layers, comps, ny, nz, modes = basis.shape
     slabs = out.shape[0]
     moved = [(now, now_in), (prev, prev_in)]
@@ -69,6 +69,7 @@
                 out[p, 2 * (MASKS + i) + x] = mask_in[PAIR * p + i, x].astype(f32)
             out[p, 2 * MATERIAL + x] = (ids_in[x] + 1).astype(f32)
         quarter = lanes_of((ny, nz)) // REACH
+        upper = jnp.full((ny, nz), turn_z[0], jnp.int32) == 1
         for t in range(2):
             low = jnp.zeros((ny, nz), f32)
             high = jnp.zeros((ny, nz), f32)
@@ -79,8 +80,8 @@
                     low = jnp.where(quarter == 2 * g, pltpu.roll(v, 8 * g, 1) if g else v, low)
                     turn = (8 * g + 8) % nz
                     high = jnp.where(quarter == 2 * g + 1, pltpu.roll(v, turn, 1) if turn else v, high)
-            down[p, t] = low
-            up[p, t] = high
+            even_pairs[p, t] = jnp.where(upper, low, high)
+            odd_pairs[p, t] = jnp.where(upper, high, low)
         for t in range(EDGE, out.shape[1]):
             out[p, t] = jnp.zeros((ny, nz), f32)
 
@@ -106,24 +107,24 @@
             out[p, t] = packed[share * p + 8 * t : share * p + 8 * t + 8]
 
 
-def faces_kernel(block, down, up):
+def faces_kernel(odd, block, far, near):
     slabs = block.shape[0]
-    first = rows_of(block.shape[2:]) < REACH
+    first = (rows_of(block.shape[2:]) < REACH).astype(jnp.int32) != odd[0]
     for g in range(slabs):
         for q in range(COUNT + 1):
             a = block[g, 2 * q]
             b = pltpu.roll(block[g, 2 * q + 1], REACH, 0)
-            down[g, q] = jnp.where(first, a, b)
-            up[g, q] = jnp.where(first, b, a)
+            far[g, q] = jnp.where(first, a, b)
+            near[g, q] = jnp.where(first, b, a)
 
 
 def steps_kernel(
-    place, drive, moduli, block, above, below, out, share, fields, masks, stiff, weight, couple, diagonal,
+    place, odd, drive, moduli, block, far, near, out, share, fields, masks, stiff, weight, couple, diagonal,
     side, side_mask, side_stiff, side_couple, side_diagonal,
 ):
     slabs, _, ny, nz = block.shape
     nx = 2 * slabs
-    first = rows_of((ny, nz)) < REACH
+    first = (rows_of((ny, nz)) < REACH).astype(jnp.int32) == odd[0]
     zero = jnp.zeros((ny, nz), f32)
     plane_zero = jnp.zeros((2 * ny, nz), f32)
     halves = (slice(0, ny), slice(ny, 2 * ny))
@@ -138,13 +139,13 @@
     sides = {}
     for g in range(slabs):
         edges = [
-            (block[g, EDGE], jnp.where(first, above[g, COUNT], below[g, COUNT])),
-            (block[g, EDGE + 1], pltpu.roll(jnp.where(first, below[g, COUNT], above[g, COUNT]), REACH, 0)),
+            (block[g, EDGE], jnp.where(first, far[g, COUNT], near[g, COUNT])),
+            (block[g, EDGE + 1], pltpu.roll(jnp.where(first, near[g, COUNT], far[g, COUNT]), REACH, 0)),
         ]
         for q in range(COUNT):
             beside = (
-                jnp.where(first, above[g, q], below[g, q]),
-                pltpu.roll(jnp.where(first, below[g, q], above[g, q]), REACH, 0),
+                jnp.where(first, far[g, q], near[g, q]),
+                pltpu.roll(jnp.where(first, near[g, q], far[g, q]), REACH, 0),
             )
             for i in range(2):
                 x = 2 * g + i
@@ -468,7 +469,7 @@
     scratch = [pltpu.VMEM(shape, f32) if isinstance(shape, tuple) else shape for shape in scratch]
     return pl.pallas_call(
         kernel,
-        out_shape=[jax.ShapeDtypeStruct(shape, f32) for shape in outs],
+        out_shape=[jax.ShapeDtypeStruct(shape, f32) if isinstance(shape, tuple) else shape for shape in outs],
         in_specs=[smem] * scalars + [away] * ins_away + [vmem] * (len(inputs) - scalars - ins_away),
         out_specs=[away] * outs_away + [vmem] * (len(outs) - outs_away),
         scratch_shapes=scratch + ([pltpu.SemaphoreType.DMA((copies,))] if copies else []),
@@ -476,10 +477,9 @@
     )(*inputs)
 
 
-def sent(block, axis, forward):
-    count = lax.axis_size(axis)
-    pairs = [(i, i + 1) for i in range(count - 1)]
-    return lax.ppermute(block, axis, pairs if forward else [(b, a) for a, b in pairs])
+def swapped(block, axis, start):
+    pairs = [(i, i + 1) for i in range(start, lax.axis_size(axis) - 1, 2)]
+    return lax.ppermute(block, axis, pairs + [(b, a) for a, b in pairs])
 
 
 def turned(parts, axis):
@@ -494,32 +494,36 @@
     share = modes // 2 // slabs // 8
     blocks = layers * comps
     inputs = [pltpu.with_memory_space_constraint(a, pltpu.HBM) for a in (modal_now.T, modal_prev.T, basis, material_ids, drive_mask)]
-    block, down, up = call(
+    place = lax.axis_index("gx").astype(jnp.int32)[None]
+    odd = (lax.axis_index("gy") & 1).astype(jnp.int32)[None]
+    above_z = (lax.axis_index("gz") & 1).astype(jnp.int32)[None]
+    block, even_pairs, odd_pairs, basis = call(
         start_kernel,
-        [(slabs, GRAM + share) + tile, (slabs, 2) + tile, (slabs, 2) + tile],
-        inputs,
-        [pltpu.VMEM(a.shape, a.dtype) for a in inputs] + [(blocks, 2 * CASES * ny, nz)],
+        [(slabs, GRAM + share) + tile, (slabs, 2) + tile, (slabs, 2) + tile, jax.ShapeDtypeStruct(basis.shape, bf16)],
+        [place, odd, above_z] + inputs,
+        [pltpu.VMEM(a.shape, a.dtype) for i, a in enumerate(inputs) if i != 2] + [(blocks, 2 * CASES * ny, nz)],
+        scalars=3,
         copies=blocks + 4,
         ins_away=5,
     )
-    edge = sent(down, "gz", False) + sent(up, "gz", True)
+    edge = swapped(even_pairs, "gz", 0) + swapped(odd_pairs, "gz", 1)
     gram, local = call(gram_kernel, [(slabs, share) + tile, (CASES, modes)], [basis])
     block = lax.dynamic_update_slice(block, jnp.concatenate([edge, gram], axis=1), (0, EDGE, 0, 0))
     block = turned(block, "gx")
-    down, up = call(faces_kernel, [(slabs, COUNT + 1) + tile] * 2, [block])
-    above, below = sent(down, "gy", False), sent(up, "gy", True)
+    far, near = call(faces_kernel, [(slabs, COUNT + 1) + tile] * 2, [odd, block], scalars=1)
+    far = swapped(far, "gy", 1)
+    near = swapped(near, "gy", 0)
     nx = layers * slabs
     wide = (2 * ny, nz)
-    place = lax.axis_index("gx").astype(jnp.int32)[None]
     states, gram = call(
         steps_kernel,
         [(slabs, STEPS, FIELDS, layers) + tile, (share,) + tile],
-        [place, drive, moduli, block, above, below],
+        [place, odd, drive, moduli, block, far, near],
         [
             (2, FIELDS, nx + 2) + wide, (PAIR, nx) + wide, (2, nx + 2) + wide, (nx,) + wide,
             (2, 6, nx) + wide, (3, nx) + wide, (2, 3) + wide, wide, (2,) + wide, (2, 6) + wide, (3,) + wide,
         ],
-        3,
+        4,
     )
     states = turned(states, "gx")
     count = STEPS * CASES

time: 94.6 us -> 92.4 us (0.977)
  starting transfers between devices: 14 us -> 9.06 us
  blocking collectives: 63.8 us -> 66.4 us
    ppermute x4, starting transfers between devices: 14 us -> 9.06 us  [swapped(): return lax.ppermute(block, axis, pairs + [(b, a) for a, b in pairs])]
    all_to_all x4, blocking collectives: 53.8 us -> 56.4 us  [turned(): return lax.all_to_all(parts, axis, 0, 0, tiled=True)]
  transfers between devices with their start and end apart: 4 -> 4, of which waited for: 3 -> 1; matrix products, arithmetic and copies ran while one was open for 0% -> 0% of each run, Pallas kernels for 1% -> 1%
where the time goes in v5:
time: 92.4 us; the launch traced here: 92.1 us
  blocking collectives  66.4 us (72%)
  Pallas kernels  11.8 us (13%)
  starting transfers between devices  9.06 us (10%)
  waiting for transfers between devices  3.95 us (4%)
    all_to_all x4, blocking collectives, turned(): return lax.all_to_all(parts, axis, 0, 0, tiled=True)  56.4 us
    pallas_call x8, Pallas kernels, call(): pl.pallas_call(kernel, out_shape=[jax.ShapeDtypeStruct(shape, f32) if isi...  11.8 us
    all_to_all x1, blocking collectives, shards(): lax.all_to_all(parts, ('gx', 'gy', 'gz'), 0, 0, tiled=True, axis_index_gr...  10 us
    ppermute x4, starting transfers between devices, swapped(): return lax.ppermute(block, axis, pairs + [(b, a) for a, b in pairs])  9.06 us
    ppermute x4, waiting for transfers between devices, swapped(): return lax.ppermute(block, axis, pairs + [(b, a) for a, b in pairs])  3.95 us
  transfers between devices with their start and end apart: 4, of which 1 were waited for; matrix products, arithmetic and copies ran while one was open for 0% of the time, Pallas kernels for 1%

profile of v5, /device:TPU:1, one launch (start us, length us, event | category | flops | bytes accessed | tf_op | source)
XLA Modules:
  0.0 92.1 jit_solution(6925171738265662162)
XLA Ops:
  0.6 2.6 %shard_map.102 = (f32[4,34,8,128]{3,2,1,0:T(8,128)S(1)}, f32[4,2,8,128]{3,2,1,0:T(8,128)S(1)}, f32[4,2,8,128]{3,2,1,0:T(8,128)S(1)}, bf16[2,3,8,128,128]{4,3,2,1,0:T(8,128)(2,1)S(1)}) custom-call(s32[1]{0:T(128)} %bitcast.place, s32[1]{0:T(128)} %bitcast.1.odd, s32[1]{0:T(128)} %bitcast.2.turn_z, bf16[8,128]{1,0:T(8,128)(2,1)} %bitcast.6, ...), custom_call_target="tpu_custom_call" | custom-call | tf_op jit(solution)/shard_map/pallas_call | solution.py:470
  3.2 2.6 %collective-permute-start = (f32[4,2,8,128]{3,2,1,0:T(8,128)S(1)}, f32[4,2,8,128]{3,2,1,0:T(8,128)S(1)}, u32[]{:S(2)}, u32[]{:S(2)}) collective-permute-start(f32[4,2,8,128]{3,2,1,0:T(8,128)S(1)} %get-tuple-element.20), channel_id=1, source_target_pairs={{0,1},{2,3},{4,5},{6,7},{1,0},{3,2},{5,4},{7,6},{8,9},{10,11},{12,... | collective-permute-start | bytes 98312 | tf_op jit(solution)/shard_map/ppermute | solution.py:482
  5.8 0.7 collective-permute-start.1
  6.4 0.0 copy-start
  6.4 0.0 copy-start.1
  6.4 0.7 shard_map.103
  7.1 0.0 collective-permute-done
  7.1 0.0 collective-permute-done.1
  7.2 12.0 %all_to_all.25.block = f32[4,34,8,128]{3,2,1,0:T(8,128)S(1)} all-to-all(f32[4,34,8,128]{3,2,1,0:T(8,128)S(1)} %maximum_dynamic-update-slice_fusion), channel_id=1, replica_groups=mesh['gx'=4,'gy'=8,'gz'=8] {'gx'}, dimensions={0} | all-to-all | bytes 1114112 | tf_op jit(solution)/shard_map/all_to_all | solution.py:486
  19.2 5.8 %collective-permute-start.2 = (f32[4,16,8,128]{3,2,1,0:T(8,128)S(1)}, f32[4,16,8,128]{3,2,1,0:T(8,128)S(1)}, u32[]{:S(2)}, u32[]{:S(2)}) collective-permute-start(f32[4,16,8,128]{3,2,1,0:T(8,128)S(1)} %get-tuple-element.23), channel_id=1, source_target_pairs={{8,16},{24,32},{40,48},{16,8},{32,24},{48,40},{9,17},{25,33},{41,4... | collective-permute-start | bytes 786440 | tf_op jit(solution)/shard_map/ppermute | solution.py:482
  25.0 0.1 collective-permute-start.3
  25.1 3.9 %collective-permute-done.2.far = f32[4,16,8,128]{3,2,1,0:T(8,128)S(1)} collective-permute-done((f32[4,16,8,128]{3,2,1,0:T(8,128)S(1)}, f32[4,16,8,128]{3,2,1,0:T(8,128)S(1)}, u32[]{:S(2)}, u32[]{:S(2)}) %collective-permute-start.2) | collective-permute-done | bytes 262176 | tf_op jit(solution)/shard_map/ppermute | solution.py:482
  29.1 0.0 collective-permute-done.3.near
  29.1 0.0 copy-done
  29.1 0.0 copy-done.1
  29.1 3.2 %shard_map.105 = (f32[4,4,6,2,8,128]{5,4,3,2,1,0:T(8,128)S(1)}, f32[2,8,128]{2,1,0:T(8,128)S(1)}) custom-call(s32[1]{0:T(128)} %bitcast.place, s32[1]{0:T(128)} %bitcast.1.odd, f32[3,8]{1,0:T(4,128)S(1)} %copy-done, f32[3,4]{1,0:T(4,128)S(1)} %copy-done.1, f32[4,34,8,128]{3,2,1,0:T(8,128)S(1)} %all_to_all.25.block, ...), custom_call_target="tpu_custom_call" | custom-call | tf_op jit(solution)/shard_map/pallas_call | solution.py:470
  32.2 13.1 %all_to_all.26.states.refs_2_ = f32[4,4,6,2,8,128]{5,4,3,2,1,0:T(8,128)S(1)} all-to-all(f32[4,4,6,2,8,128]{5,4,3,2,1,0:T(8,128)S(1)} %get-tuple-element.25), channel_id=1, replica_groups=mesh['gx'=4,'gy'=8,'gz'=8] {'gx'}, dimensions={0} | all-to-all | bytes 1572864 | tf_op jit(solution)/shard_map/all_to_all | solution.py:486
  45.4 0.5 shard_map.106
  45.9 11.9 %all_to_all.27.parts = f32[8,32,128]{2,1,0:T(8,128)S(1)} all-to-all(f32[8,32,128]{2,1,0:T(8,128)S(1)} %shard_map.106), channel_id=1, replica_groups=mesh['gx'=4,'gy'=8,'gz'=8] {'gy'}, dimensions={0} | all-to-all | bytes 262144 | tf_op jit(solution)/shard_map/all_to_all | solution.py:486
  57.8 19.4 %all_to_all.28.parts = f32[8,32,128]{2,1,0:T(8,128)S(1)} all-to-all(f32[8,32,128]{2,1,0:T(8,128)S(1)} %shard_map.107), channel_id=1, replica_groups=mesh['gx'=4,'gy'=8,'gz'=8] {'gz'}, dimensions={0} | all-to-all | bytes 262144 | tf_op jit(solution)/shard_map/all_to_all | solution.py:486
  77.2 10.0 %all_to_all.29.refs_0_ = f32[8,32,128]{2,1,0:T(8,128)S(1)} all-to-all(f32[8,32,128]{2,1,0:T(8,128)S(1)} %shard_map.108), channel_id=1, replica_groups={{0,8,64,72,128,136,192,200},{1,9,65,73,129,137,193,201},{2,10,66,74,130..., dimensions={0} | all-to-all | bytes 262144 | tf_op jit(solution)/shard_map/all_to_all | solution.py:541
  87.2 4.9 %shard_map.109 = (f32[3,8,2,8,128]{4,3,2,1,0:T(8,128)}, f32[3,8,2,8,128]{4,3,2,1,0:T(8,128)}, f32[4,2,8,128]{3,2,1,0:T(8,128)}, f32[4,8,8]{2,1,0:T(8,128)}) custom-call(f32[8,32,128]{2,1,0:T(8,128)S(1)} %all_to_all.29.refs_0_, bf16[2,3,8,128,128]{4,3,2,1,0:T(8,128)(2,1)S(1)} %get-tuple-element.18.basis.refs_1_, ...), custom_call_target="tpu_custom_call" | custom-call | tf_op jit(solution)/shard_map/pallas_call | solution.py:470
  (5 shorter events, 0.1 us)
Async XLA Ops:
  3.2 3.9 %collective-permute-start = (f32[4,2,8,128]{3,2,1,0:T(8,128)S(1)}, f32[4,2,8,128]{3,2,1,0:T(8,128)S(1)}, u32[]{:S(2)}, u32[]{:S(2)}) collective-permute-start(f32[4,2,8,128]{3,2,1,0:T(8,128)S(1)} %get-tuple-element.20), channel_id=1, source_target_pairs={{0,1},{2,3},{4,5},{6,7},{1,0},{3,2},{5,4},{7,6},{8,9},{10,11},{12,... | collective-permute-start | bytes 98312 | tf_op jit(solution)/shard_map/ppermute | solution.py:482
  5.8 1.4 %collective-permute-start.1 = (f32[4,2,8,128]{3,2,1,0:T(8,128)S(1)}, f32[4,2,8,128]{3,2,1,0:T(8,128)S(1)}, u32[]{:S(2)}, u32[]{:S(2)}) collective-permute-start(f32[4,2,8,128]{3,2,1,0:T(8,128)S(1)} %get-tuple-element.21), channel_id=1, source_target_pairs={{1,2},{3,4},{5,6},{2,1},{4,3},{6,5},{9,10},{11,12},{13,14},{10,9},... | collective-permute-start | bytes 98312 | tf_op jit(solution)/shard_map/ppermute | solution.py:482
  6.4 22.6 %copy-start = (f32[3,8]{1,0:T(4,128)S(1)}, f32[3,8]{1,0:T(4,128)}, u32[]{:S(2)}) copy-start(f32[3,8]{1,0:T(4,128)} %drive.1) | copy-start | bytes 292
  6.4 22.6 %copy-start.1 = (f32[3,4]{1,0:T(4,128)S(1)}, f32[3,4]{1,0:T(4,128)}, u32[]{:S(2)}) copy-start(f32[3,4]{1,0:T(4,128)} %moduli.1) | copy-start | bytes 148
  19.2 9.8 %collective-permute-start.2 = (f32[4,16,8,128]{3,2,1,0:T(8,128)S(1)}, f32[4,16,8,128]{3,2,1,0:T(8,128)S(1)}, u32[]{:S(2)}, u32[]{:S(2)}) collective-permute-start(f32[4,16,8,128]{3,2,1,0:T(8,128)S(1)} %get-tuple-element.23), channel_id=1, source_target_pairs={{8,16},{24,32},{40,48},{16,8},{32,24},{48,40},{9,17},{25,33},{41,4... | collective-permute-start | bytes 786440 | tf_op jit(solution)/shard_map/ppermute | solution.py:482
  25.0 4.0 %collective-permute-start.3 = (f32[4,16,8,128]{3,2,1,0:T(8,128)S(1)}, f32[4,16,8,128]{3,2,1,0:T(8,128)S(1)}, u32[]{:S(2)}, u32[]{:S(2)}) collective-permute-start(f32[4,16,8,128]{3,2,1,0:T(8,128)S(1)} %get-tuple-element.24), channel_id=1, source_target_pairs={{0,8},{16,24},{32,40},{48,56},{8,0},{24,16},{40,32},{56,48},{1,9},... | collective-permute-start | bytes 786440 | tf_op jit(solution)/shard_map/ppermute | solution.py:482

commit v6 on v5

--- a/solution.py
+++ b/solution.py
@@ -6,6 +6,7 @@
 from jax.sharding import PartitionSpec as P
 
 STEPS = 4
+SHARES = 4
 CASES = 8
 step_squared = 0.1
 ramp_steps = 4.0
@@ -310,12 +311,13 @@
         tile = jnp.where(lane // CASES == s, square[s * CASES : (s + 1) * CASES], tile)
     tile = jnp.concatenate([tile, jnp.zeros((CASES, modes - count), f32)], axis=1)
     tile = jnp.where(lanes_of(tile.shape) < modes // 2, tile, local[...])
-    half = count // 2
+    both = jnp.concatenate([share[t] for t in range(share.shape[0])])
     for g in range(out.shape[0]):
-        h = g % 2
-        out[g, :half] = coef[h * half : (h + 1) * half]
-        out[g, half : half + CASES] = tile
-        out[g, half + CASES :] = share[h]
+        k = g * SHARES // out.shape[0]
+        pieces = [v[k * len(v) // SHARES : (k + 1) * len(v) // SHARES] for v in (coef, tile, both)]
+        used = sum(len(v) for v in pieces)
+        pieces.append(jnp.zeros((out.shape[1] - used, modes), f32))
+        out[g] = jnp.concatenate(pieces)
 
 
 def sum_kernel(parts, out):
@@ -377,16 +379,18 @@
     count = STEPS * CASES
     half = modes // 2
     high = lax.Precision.HIGHEST
-    members, upto = parts.shape[0], count // 2 + CASES
+    members = parts.shape[0] // SHARES
+    ends = (count // SHARES, (count + CASES) // SHARES, (count + CASES + 2 * CASES) // SHARES)
     owns = []
-    for h in range(2):
-        own = parts[h, :upto]
-        for g in range(h + 2, members, 2):
-            own = own + parts[g, :upto]
+    for k in range(SHARES):
+        own = parts[k]
+        for g in range(1, members):
+            own = own + parts[g * SHARES + k]
         owns.append(own * weight)
-    coef = jnp.concatenate([own[: count // 2] for own in owns])
-    square = owns[0][count // 2 :]
-    packed = jnp.concatenate([parts[g, upto:] for g in range(members)]) * weight
+    coef = jnp.concatenate([own[: ends[0]] for own in owns])
+    square = jnp.concatenate([own[ends[0] : ends[1]] for own in owns])
+    packed = [parts[g * SHARES + k, ends[1] : ends[2]] for g in range(members) for k in range(SHARES)]
+    packed = jnp.concatenate(packed) * weight
     lane, row = lanes_of(packed.shape), rows_of(packed.shape)
     flipped = padded(packed).T
     diagonal = jnp.where(lane[:1] < half, pltpu.roll(square[:1], half, 1), square[1:2])
@@ -527,15 +531,15 @@
     )
     states = turned(states, "gx")
     count = STEPS * CASES
-    width = count // 2 + CASES + 8
+    width = -(-(count + CASES + 8 * share) // SHARES // 8) * 8
     parts, = call(
         project_kernel, [(rows, width, modes)], [basis, states, gram, local], [(blocks, count * ny, nz)]
     )
     parts, = call(sum_kernel, [(depth, width, modes)], [turned(parts, "gy")])
-    parts, = call(sum_kernel, [(2 * slabs, width, modes)], [turned(parts, "gz")])
+    parts, = call(sum_kernel, [(SHARES * slabs, width, modes)], [turned(parts, "gz")])
     groups = [
-        [(a * rows + 2 * h + core) * depth + z for a in range(slabs) for core in range(2)]
-        for h in range(rows // 2)
+        [(a * rows + 2 * h + core) * depth + z for a in range(slabs) for h in range(rows // 2)]
+        for core in range(2)
         for z in range(depth)
     ]
     parts = lax.all_to_all(parts, ("gx", "gy", "gz"), 0, 0, tiled=True, axis_index_groups=groups)

time: 92.4 us -> 92 us (level); the launches traced: 92.1 us -> 90.5 us
  blocking collectives: 66.4 us -> 64.9 us
    all_to_all x4, blocking collectives: 56.4 us -> 55.4 us  [turned(): return lax.all_to_all(parts, axis, 0, 0, tiled=True)]
where the time goes in v6:
time: 92 us; the launch traced here: 90.5 us
  blocking collectives  64.9 us (71%)
  Pallas kernels  11.8 us (13%)
  starting transfers between devices  9.06 us (10%)
  waiting for transfers between devices  3.95 us (4%)
    all_to_all x4, blocking collectives, turned(): return lax.all_to_all(parts, axis, 0, 0, tiled=True)  55.4 us
    pallas_call x8, Pallas kernels, call(): pl.pallas_call(kernel, out_shape=[jax.ShapeDtypeStruct(shape, f32) if isi...  11.8 us
    all_to_all x1, blocking collectives, shards(): lax.all_to_all(parts, ('gx', 'gy', 'gz'), 0, 0, tiled=True, axis_index_gr...  9.52 us
    ppermute x4, starting transfers between devices, swapped(): return lax.ppermute(block, axis, pairs + [(b, a) for a, b in pairs])  9.06 us
    ppermute x4, waiting for transfers between devices, swapped(): return lax.ppermute(block, axis, pairs + [(b, a) for a, b in pairs])  3.95 us
  transfers between devices with their start and end apart: 4, of which 1 were waited for; matrix products, arithmetic and copies ran while one was open for 0% of the time, Pallas kernels for 1%

profile of v6, /device:TPU:1, one launch (start us, length us, event | category | flops | bytes accessed | tf_op | source)
XLA Modules:
  0.0 90.5 jit_solution(14099097324216962199)
XLA Ops:
  0.6 2.6 %shard_map.102 = (f32[4,34,8,128]{3,2,1,0:T(8,128)S(1)}, f32[4,2,8,128]{3,2,1,0:T(8,128)S(1)}, f32[4,2,8,128]{3,2,1,0:T(8,128)S(1)}, bf16[2,3,8,128,128]{4,3,2,1,0:T(8,128)(2,1)S(1)}) custom-call(s32[1]{0:T(128)} %bitcast.place, s32[1]{0:T(128)} %bitcast.1.odd, s32[1]{0:T(128)} %bitcast.2.turn_z, bf16[8,128]{1,0:T(8,128)(2,1)} %bitcast.6, ...), custom_call_target="tpu_custom_call" | custom-call | tf_op jit(solution)/shard_map/pallas_call | solution.py:474
  3.2 2.6 %collective-permute-start = (f32[4,2,8,128]{3,2,1,0:T(8,128)S(1)}, f32[4,2,8,128]{3,2,1,0:T(8,128)S(1)}, u32[]{:S(2)}, u32[]{:S(2)}) collective-permute-start(f32[4,2,8,128]{3,2,1,0:T(8,128)S(1)} %get-tuple-element.20), channel_id=1, source_target_pairs={{0,1},{2,3},{4,5},{6,7},{1,0},{3,2},{5,4},{7,6},{8,9},{10,11},{12,... | collective-permute-start | bytes 98312 | tf_op jit(solution)/shard_map/ppermute | solution.py:486
  5.8 0.7 collective-permute-start.1
  6.4 0.0 copy-start
  6.4 0.0 copy-start.1
  6.4 0.7 shard_map.103
  7.1 0.0 collective-permute-done
  7.1 0.0 collective-permute-done.1
  7.2 12.0 %all_to_all.25.block = f32[4,34,8,128]{3,2,1,0:T(8,128)S(1)} all-to-all(f32[4,34,8,128]{3,2,1,0:T(8,128)S(1)} %maximum_dynamic-update-slice_fusion), channel_id=1, replica_groups=mesh['gx'=4,'gy'=8,'gz'=8] {'gx'}, dimensions={0} | all-to-all | bytes 1114112 | tf_op jit(solution)/shard_map/all_to_all | solution.py:490
  19.2 5.8 %collective-permute-start.2 = (f32[4,16,8,128]{3,2,1,0:T(8,128)S(1)}, f32[4,16,8,128]{3,2,1,0:T(8,128)S(1)}, u32[]{:S(2)}, u32[]{:S(2)}) collective-permute-start(f32[4,16,8,128]{3,2,1,0:T(8,128)S(1)} %get-tuple-element.23), channel_id=1, source_target_pairs={{8,16},{24,32},{40,48},{16,8},{32,24},{48,40},{9,17},{25,33},{41,4... | collective-permute-start | bytes 786440 | tf_op jit(solution)/shard_map/ppermute | solution.py:486
  25.0 0.1 collective-permute-start.3
  25.1 3.9 %collective-permute-done.2.far = f32[4,16,8,128]{3,2,1,0:T(8,128)S(1)} collective-permute-done((f32[4,16,8,128]{3,2,1,0:T(8,128)S(1)}, f32[4,16,8,128]{3,2,1,0:T(8,128)S(1)}, u32[]{:S(2)}, u32[]{:S(2)}) %collective-permute-start.2) | collective-permute-done | bytes 262176 | tf_op jit(solution)/shard_map/ppermute | solution.py:486
  29.1 0.0 collective-permute-done.3.near
  29.1 0.0 copy-done
  29.1 0.0 copy-done.1
  29.1 3.2 %shard_map.105 = (f32[4,4,6,2,8,128]{5,4,3,2,1,0:T(8,128)S(1)}, f32[2,8,128]{2,1,0:T(8,128)S(1)}) custom-call(s32[1]{0:T(128)} %bitcast.place, s32[1]{0:T(128)} %bitcast.1.odd, f32[3,8]{1,0:T(4,128)S(1)} %copy-done, f32[3,4]{1,0:T(4,128)S(1)} %copy-done.1, f32[4,34,8,128]{3,2,1,0:T(8,128)S(1)} %all_to_all.25.block, ...), custom_call_target="tpu_custom_call" | custom-call | tf_op jit(solution)/shard_map/pallas_call | solution.py:474
  32.2 13.1 %all_to_all.26.states.refs_2_ = f32[4,4,6,2,8,128]{5,4,3,2,1,0:T(8,128)S(1)} all-to-all(f32[4,4,6,2,8,128]{5,4,3,2,1,0:T(8,128)S(1)} %get-tuple-element.25), channel_id=1, replica_groups=mesh['gx'=4,'gy'=8,'gz'=8] {'gx'}, dimensions={0} | all-to-all | bytes 1572864 | tf_op jit(solution)/shard_map/all_to_all | solution.py:490
  45.4 0.5 shard_map.106
  45.8 11.5 %all_to_all.27.parts = f32[8,16,128]{2,1,0:T(8,128)S(1)} all-to-all(f32[8,16,128]{2,1,0:T(8,128)S(1)} %shard_map.106), channel_id=1, replica_groups=mesh['gx'=4,'gy'=8,'gz'=8] {'gy'}, dimensions={0} | all-to-all | bytes 131072 | tf_op jit(solution)/shard_map/all_to_all | solution.py:490
  57.3 18.8 %all_to_all.28.parts = f32[8,16,128]{2,1,0:T(8,128)S(1)} all-to-all(f32[8,16,128]{2,1,0:T(8,128)S(1)} %shard_map.107), channel_id=1, replica_groups=mesh['gx'=4,'gy'=8,'gz'=8] {'gz'}, dimensions={0} | all-to-all | bytes 131072 | tf_op jit(solution)/shard_map/all_to_all | solution.py:490
  76.1 9.5 %all_to_all.29.refs_0_ = f32[16,16,128]{2,1,0:T(8,128)S(1)} all-to-all(f32[16,16,128]{2,1,0:T(8,128)S(1)} %shard_map.108), channel_id=1, replica_groups={{0,16,32,48,64,80,96,112,128,144,160,176,192,208,224,240},{1,17,33,49,6..., dimensions={0} | all-to-all | bytes 262144 | tf_op jit(solution)/shard_map/all_to_all | solution.py:545
  85.6 4.9 %shard_map.109 = (f32[3,8,2,8,128]{4,3,2,1,0:T(8,128)}, f32[3,8,2,8,128]{4,3,2,1,0:T(8,128)}, f32[4,2,8,128]{3,2,1,0:T(8,128)}, f32[4,8,8]{2,1,0:T(8,128)}) custom-call(f32[16,16,128]{2,1,0:T(8,128)S(1)} %all_to_all.29.refs_0_, bf16[2,3,8,128,128]{4,3,2,1,0:T(8,128)(2,1)S(1)} %get-tuple-element.18.basis.refs_1_, ...), custom_call_target="tpu_custom_call" | custom-call | tf_op jit(solution)/shard_map/pallas_call | solution.py:474
  (5 shorter events, 0.1 us)
Async XLA Ops:
  3.2 3.9 %collective-permute-start = (f32[4,2,8,128]{3,2,1,0:T(8,128)S(1)}, f32[4,2,8,128]{3,2,1,0:T(8,128)S(1)}, u32[]{:S(2)}, u32[]{:S(2)}) collective-permute-start(f32[4,2,8,128]{3,2,1,0:T(8,128)S(1)} %get-tuple-element.20), channel_id=1, source_target_pairs={{0,1},{2,3},{4,5},{6,7},{1,0},{3,2},{5,4},{7,6},{8,9},{10,11},{12,... | collective-permute-start | bytes 98312 | tf_op jit(solution)/shard_map/ppermute | solution.py:486
  5.8 1.4 %collective-permute-start.1 = (f32[4,2,8,128]{3,2,1,0:T(8,128)S(1)}, f32[4,2,8,128]{3,2,1,0:T(8,128)S(1)}, u32[]{:S(2)}, u32[]{:S(2)}) collective-permute-start(f32[4,2,8,128]{3,2,1,0:T(8,128)S(1)} %get-tuple-element.21), channel_id=1, source_target_pairs={{1,2},{3,4},{5,6},{2,1},{4,3},{6,5},{9,10},{11,12},{13,14},{10,9},... | collective-permute-start | bytes 98312 | tf_op jit(solution)/shard_map/ppermute | solution.py:486
  6.4 22.6 %copy-start = (f32[3,8]{1,0:T(4,128)S(1)}, f32[3,8]{1,0:T(4,128)}, u32[]{:S(2)}) copy-start(f32[3,8]{1,0:T(4,128)} %drive.1) | copy-start | bytes 292
  6.4 22.6 %copy-start.1 = (f32[3,4]{1,0:T(4,128)S(1)}, f32[3,4]{1,0:T(4,128)}, u32[]{:S(2)}) copy-start(f32[3,4]{1,0:T(4,128)} %moduli.1) | copy-start | bytes 148
  19.2 9.8 %collective-permute-start.2 = (f32[4,16,8,128]{3,2,1,0:T(8,128)S(1)}, f32[4,16,8,128]{3,2,1,0:T(8,128)S(1)}, u32[]{:S(2)}, u32[]{:S(2)}) collective-permute-start(f32[4,16,8,128]{3,2,1,0:T(8,128)S(1)} %get-tuple-element.23), channel_id=1, source_target_pairs={{8,16},{24,32},{40,48},{16,8},{32,24},{48,40},{9,17},{25,33},{41,4... | collective-permute-start | bytes 786440 | tf_op jit(solution)/shard_map/ppermute | solution.py:486
  25.0 4.0 %collective-permute-start.3 = (f32[4,16,8,128]{3,2,1,0:T(8,128)S(1)}, f32[4,16,8,128]{3,2,1,0:T(8,128)S(1)}, u32[]{:S(2)}, u32[]{:S(2)}) collective-permute-start(f32[4,16,8,128]{3,2,1,0:T(8,128)S(1)} %get-tuple-element.24), channel_id=1, source_target_pairs={{0,8},{16,24},{32,40},{48,56},{8,0},{24,16},{40,32},{56,48},{1,9},... | collective-permute-start | bytes 786440 | tf_op jit(solution)/shard_map/ppermute | solution.py:486
